TPU v7x, 32 devices: a whole 2x2x4 slice. The times are simulated.
32 devices in a mesh: seq: 8 (over z, core), dp: 4 (over y, x).
Axes of the slice: x: 2, y: 2, z: 4, core: 2. Of those that a mesh axis runs over, the one named last changes fastest.
Arguments:
- tokens: float32 [4, 4096, 768], P('dp', 'seq'), as said below
- segment_lens: int32 [4, 64], P('dp', 'seq'), may hold values from 16 to 64, as said below
- query_weight: float32 [768, 768], replicated, may hold values from -0.375 to 0.375
- query_bias: float32 [768], replicated, may hold values from -3 to 3
- key_weight: float32 [768, 768], replicated, may hold values from -0.375 to 0.375
- value_weight: float32 [768, 768], replicated, may hold values from -0.21875 to 0.21875
- value_bias: float32 [768], replicated, may hold values from -3 to 3
- conv_taps: float32 [33, 12], replicated, may hold values from -0.3 to 0.3
- output_weight: float32 [768, 768], replicated, may hold values from -0.5 to 0.5
- output_bias: float32 [768], replicated, may hold values from -2 to 2
- first_gain: float32 [768], replicated, may hold values from 0.25 to 1.75
- first_bias: float32 [768], replicated, may hold values from -2 to 2
- inner_weight: float32 [768, 3072], replicated, may hold values from -0.21875 to 0.21875
- inner_bias: float32 [3072], replicated, may hold values from -3 to 3
- outer_weight: float32 [3072, 768], replicated, may hold values from -0.15625 to 0.15625
- outer_bias: float32 [768], replicated, may hold values from -2 to 2
- second_gain: float32 [768], replicated, may hold values from 0.25 to 1.75
- second_bias: float32 [768], replicated, may hold values from -2 to 2
- cotangent: float32 [4, 4096, 768], P('dp', 'seq'), may hold values from -6 to 6
Outputs:
- layer_out: float32 [4, 4096, 768], P('dp', 'seq')
- input_grad: float32 [4, 4096, 768], P('dp', 'seq')
- grad_query_weight: float32 [768, 768], replicated
- grad_query_bias: float32 [768], replicated
- grad_key_weight: float32 [768, 768], replicated
- grad_value_weight: float32 [768, 768], replicated
- grad_value_bias: float32 [768], replicated
- grad_conv_taps: float32 [33, 12], replicated
- grad_output_weight: float32 [768, 768], replicated
- grad_output_bias: float32 [768], replicated
- grad_first_gain: float32 [768], replicated
- grad_first_bias: float32 [768], replicated
- grad_inner_weight: float32 [768, 3072], replicated
- grad_inner_bias: float32 [3072], replicated
- grad_outer_weight: float32 [3072, 768], replicated
- grad_outer_bias: float32 [768], replicated
- grad_second_gain: float32 [768], replicated
- grad_second_bias: float32 [768], replicated
Inputs may be any that keep to these rules, and one draw needn't show every extreme that they name: `segment_lens`: each landmark segment holds 16 to 64 tokens, and every sequence has a segment of exactly 64. `tokens`: entries at padding slots take no part in any output.
All inputs are finite; a program needn't handle non-finite values.
Results may differ from a plain program's by a relative error of at most 0.0003.
Values sent between devices are 32-bit elements; how exact they have to be, the bound alone decides.
A program may use at most 320 MiB of HBM per device.

v0:
```python
from functools import partial
import math

import jax
import jax.numpy as jnp
from jax import lax
from jax.sharding import PartitionSpec as P

HEADS = 12
DH = 64
CONV = 33
NEWTON = 6


highest = lax.Precision.HIGHEST
norm_eps = 1e-05
root_half = 0.7071067811865476
masked_score = -1e30


def with_halo(block, sides, width):
    for axis, dim in sides:
        count = lax.axis_size(axis)
        forward = [(i, i + 1) for i in range(count - 1)]
        backward = [(target, source) for source, target in forward]
        low = lax.ppermute(
            lax.slice_in_dim(block, block.shape[dim] - width, None, axis=dim), axis, forward
        )
        high = lax.ppermute(lax.slice_in_dim(block, 0, width, axis=dim), axis, backward)
        block = jnp.concatenate([low, block, high], axis=dim)
    return block


def matmul(left, right):
    return jnp.dot(left, right, precision=highest, preferred_element_type=jnp.float32)


def contract(form, left, right):
    return jnp.einsum(form, left, right, precision=highest, preferred_element_type=jnp.float32)


def layer_norm(summed, scale_gain, offset):
    centered = summed - jnp.mean(summed, axis=-1, keepdims=True)
    spread = jnp.mean(centered * centered, axis=-1, keepdims=True)
    return centered * lax.rsqrt(spread + norm_eps) * scale_gain + offset


def normalize_rows(scores):
    top_score = jnp.max(scores, axis=-1, keepdims=True)
    raised = jnp.exp(scores - top_score)
    return raised / jnp.sum(raised, axis=-1, keepdims=True)


def newton_inverse(kernel):
    colsum = jnp.sum(kernel, axis=-2)
    scaling = jnp.sqrt(jnp.sum(colsum * colsum, axis=-1))
    iterate = jnp.swapaxes(kernel, -1, -2) / scaling[..., None, None]
    identity = jnp.eye(kernel.shape[-1], dtype=jnp.float32)
    for newton_step in range(NEWTON):
        product = contract("...ij,...jk->...ik", kernel, iterate)
        factor = 7.0 * identity - product
        factor = 15.0 * identity - contract("...ij,...jk->...ik", product, factor)
        factor = 13.0 * identity - contract("...ij,...jk->...ik", product, factor)
        iterate = 0.25 * contract("...ij,...jk->...ik", iterate, factor)
    return iterate


def take_rows(matrix, begin_at, length):
    return lax.dynamic_slice_in_dim(matrix, begin_at, length, 0)


def place_rows(matrix, rows_in, begin_at):
    return lax.dynamic_update_slice_in_dim(matrix, rows_in, begin_at, 0)


def add_rows(matrix, rows_in, begin_at):
    current = lax.dynamic_slice_in_dim(matrix, begin_at, rows_in.shape[0], 0)
    return lax.dynamic_update_slice_in_dim(matrix, current + rows_in, begin_at, 0)


def pack_flat(entries, devices):
    flattened = jnp.concatenate([entry.reshape(-1) for entry in entries])
    target = -(-flattened.shape[0] // devices) * devices
    return jnp.pad(flattened, (0, target - flattened.shape[0]))


def unpack_flat(flattened, layouts):
    pieces = []
    offset = 0
    for layout in layouts:
        length = math.prod(layout)
        pieces.append(flattened[offset : offset + length].reshape(layout))
        offset = offset + length
    return pieces


def per_device(
    tokens,
    segment_lens,
    query_weight,
    query_bias,
    key_weight,
    value_weight,
    value_bias,
    conv_taps,
    output_weight,
    output_bias,
    first_gain,
    first_bias,
    inner_weight,
    inner_bias,
    outer_weight,
    outer_bias,
    second_gain,
    second_bias,
    cotangent,
):
    seqs_here, block_len, features = tokens.shape
    lm_here = segment_lens.shape[1]
    rim_width = (CONV - 1) // 2
    score_scale = DH ** (-0.5)
    devices = lax.axis_size(("seq", "dp"))
    counts = jnp.sum(segment_lens, axis=1)
    segment_ends = jnp.cumsum(segment_lens, axis=1)
    slot_ids = jnp.arange(block_len, dtype=jnp.int32)
    valid = slot_ids[None, :] < counts[:, None]
    slot_mask = valid.astype(jnp.float32)[:, :, None]
    local_seg = jnp.sum(
        (slot_ids[None, :, None] >= segment_ends[:, None, :]).astype(jnp.int32), axis=2
    )
    member = (
        (local_seg[:, :, None] == jnp.arange(lm_here, dtype=jnp.int32)[None, None, :])
        & valid[:, :, None]
    ).astype(jnp.float32)
    inverse_len = (1.0 / segment_lens.astype(jnp.float32))[:, :, None]

    def project(source, query_matrix, query_shift, key_matrix, value_matrix, value_shift):
        return (
            matmul(source, query_matrix) + query_shift,
            matmul(source, key_matrix),
            matmul(source, value_matrix) + value_shift,
        )

    (queries, key_rows, values), project_pull = jax.vjp(
        project, tokens, query_weight, query_bias, key_weight, value_weight, value_bias
    )
    query_mean = contract("stj,std->sjd", member, queries) * inverse_len
    key_mean = contract("stj,std->sjd", member, key_rows) * inverse_len
    query_land, key_land = (
        lax.all_gather(query_mean, "seq", axis=1, tiled=True),
        lax.all_gather(key_mean, "seq", axis=1, tiled=True),
    )

    def split_heads(rows_in):
        return rows_in.reshape(seqs_here, -1, HEADS, DH)

    def core_inverse(query_rows, key_rows_in):
        core = normalize_rows(
            contract("sihd,sjhd->shij", split_heads(query_rows), split_heads(key_rows_in))
            * score_scale
        )
        return newton_inverse(core)

    inverse, inverse_pull = jax.vjp(core_inverse, query_land, key_land)
    land_query = split_heads(query_land)
    key_heads = split_heads(key_rows)
    value_heads = split_heads(values)
    live_keys = valid[:, None, None, :]
    far_scores = jnp.where(
        live_keys, contract("sihd,sthd->shit", land_query, key_heads) * score_scale, masked_score
    )
    far_peak = lax.pmax(jnp.max(far_scores, axis=-1), "seq")
    raised = jnp.where(live_keys, jnp.exp(far_scores - far_peak[..., None]), 0.0)
    far_total, weighted = lax.psum(
        (jnp.sum(raised, axis=-1), contract("shit,sthd->shid", raised, value_heads)), "seq"
    )
    far_prob = raised / far_total[..., None]
    mixed = weighted / far_total[..., None]

    def blend_of(inverse_in, mixed_in):
        return contract("shij,shjd->shid", inverse_in, mixed_in)

    blend, blend_pull = jax.vjp(blend_of, inverse, mixed)

    def near_part(query_rows, key_land_in, blend_in):
        near = normalize_rows(
            contract("sthd,sjhd->shtj", split_heads(query_rows), split_heads(key_land_in))
            * score_scale
        )
        return contract("shtj,shjd->sthd", near, blend_in).reshape(seqs_here, block_len, features)

    attention, near_pull = jax.vjp(near_part, queries, key_land, blend)
    masked_values = values * slot_mask
    last_rows = jax.vmap(partial(take_rows, length=rim_width))(masked_values, counts - rim_width)
    padded_rims = with_halo(
        jnp.concatenate([masked_values[:, :rim_width], last_rows], axis=1), (("seq", 1),), rim_width
    )
    left_rim = padded_rims[:, :rim_width]
    right_rim = padded_rims[:, 3 * rim_width :]

    def conv_part(left_in, values_in, right_in, taps_in):
        extended = jnp.concatenate([left_in, values_in, jnp.zeros_like(left_in)], axis=1)
        extended = jax.vmap(place_rows)(extended, right_in, counts + rim_width)
        feature_taps = jnp.repeat(taps_in, DH, axis=1)
        running = feature_taps[0] * extended[:, 0:block_len]
        for offset in range(1, CONV):
            running = running + feature_taps[offset] * extended[:, offset : offset + block_len]
        return running

    conv_out, conv_pull = jax.vjp(conv_part, left_rim, masked_values, right_rim, conv_taps)
    context = attention + conv_out

    def post_block(
        context_in,
        source,
        out_matrix,
        out_shift,
        gain_one,
        shift_one,
        inner_matrix,
        inner_shift,
        outer_matrix,
        outer_shift,
        gain_two,
        shift_two,
    ):
        hidden_one = layer_norm(
            source + (matmul(context_in, out_matrix) + out_shift), gain_one, shift_one
        )
        pre_act = matmul(hidden_one, inner_matrix) + inner_shift
        activated = 0.5 * pre_act * (1.0 + lax.erf(pre_act * root_half))
        branch = matmul(activated, outer_matrix) + outer_shift
        return layer_norm(hidden_one + branch, gain_two, shift_two) * slot_mask

    layer_out, post_pull = jax.vjp(
        post_block,
        context,
        tokens,
        output_weight,
        output_bias,
        first_gain,
        first_bias,
        inner_weight,
        inner_bias,
        outer_weight,
        outer_bias,
        second_gain,
        second_bias,
    )
    (
        grad_context,
        grad_tokens,
        grad_output_weight,
        grad_output_bias,
        grad_first_gain,
        grad_first_bias,
        grad_inner_weight,
        grad_inner_bias,
        grad_outer_weight,
        grad_outer_bias,
        grad_second_gain,
        grad_second_bias,
    ) = post_pull(cotangent)
    post_small = [
        grad_output_bias,
        grad_first_gain,
        grad_first_bias,
        grad_inner_bias,
        grad_outer_bias,
        grad_second_gain,
        grad_second_bias,
    ]
    post_layouts = [entry.shape for entry in post_small]
    grad_queries_near, grad_key_near, grad_blend_part = near_pull(grad_context)
    grad_blend = lax.psum(grad_blend_part, "seq")
    grad_left, grad_masked, grad_right, grad_conv_taps = conv_pull(grad_context)
    returned = with_halo(jnp.concatenate([grad_left, grad_right], axis=1), (("seq", 1),), rim_width)
    grad_masked = grad_masked.at[:, :rim_width].add(returned[:, :rim_width])
    grad_masked = jax.vmap(add_rows)(grad_masked, returned[:, 3 * rim_width :], counts - rim_width)
    grad_inverse, grad_mixed = blend_pull(grad_blend)
    grad_query_core, grad_key_core = inverse_pull(grad_inverse)
    grad_far = contract("shid,sthd->shit", grad_mixed, value_heads)
    row_dot = jnp.sum(grad_mixed * mixed, axis=-1)
    grad_far_scores = far_prob * (grad_far - row_dot[..., None]) * score_scale
    grad_query_far = contract("shit,sthd->sihd", grad_far_scores, key_heads).reshape(
        seqs_here, -1, features
    )
    grad_key_far = contract("shit,sihd->sthd", grad_far_scores, land_query).reshape(
        seqs_here, block_len, features
    )
    grad_values_far = contract("shit,shid->sthd", far_prob, grad_mixed).reshape(
        seqs_here, block_len, features
    )
    own_query, own_key = (
        lax.psum_scatter(grad_query_far, "seq", scatter_dimension=1, tiled=True),
        lax.psum_scatter(grad_key_near, "seq", scatter_dimension=1, tiled=True),
    )
    own_start = lax.axis_index("seq") * lm_here
    own_query = (
        own_query + lax.dynamic_slice_in_dim(grad_query_core, own_start, lm_here, 1)
    ) * inverse_len
    own_key = (
        own_key + lax.dynamic_slice_in_dim(grad_key_core, own_start, lm_here, 1)
    ) * inverse_len
    grad_queries = grad_queries_near + contract("stj,sjd->std", member, own_query)
    grad_keys = grad_key_far + contract("stj,sjd->std", member, own_key)
    grad_values = (grad_masked + grad_values_far) * slot_mask
    (
        grad_source,
        grad_query_weight,
        grad_query_bias,
        grad_key_weight,
        grad_value_weight,
        grad_value_bias,
    ) = project_pull((grad_queries, grad_keys, grad_values))
    input_grad = grad_tokens + grad_source
    front_small = [grad_query_bias, grad_value_bias, grad_conv_taps]
    front_layouts = [entry.shape for entry in front_small]
    packed = pack_flat(front_small + post_small, devices)
    weight_parts = (
        lax.psum_scatter(
            grad_query_weight.reshape(-1), ("seq", "dp"), scatter_dimension=0, tiled=True
        ),
        lax.psum_scatter(
            grad_key_weight.reshape(-1), ("seq", "dp"), scatter_dimension=0, tiled=True
        ),
        lax.psum_scatter(
            grad_value_weight.reshape(-1), ("seq", "dp"), scatter_dimension=0, tiled=True
        ),
        lax.psum_scatter(
            grad_output_weight.reshape(-1), ("seq", "dp"), scatter_dimension=0, tiled=True
        ),
        lax.psum_scatter(
            grad_inner_weight.reshape(-1), ("seq", "dp"), scatter_dimension=0, tiled=True
        ),
        lax.psum_scatter(
            grad_outer_weight.reshape(-1), ("seq", "dp"), scatter_dimension=0, tiled=True
        ),
        lax.psum_scatter(packed, ("seq", "dp"), scatter_dimension=0, tiled=True),
    )
    weight_sums = (
        lax.all_gather(weight_parts[0], ("seq", "dp"), axis=0, tiled=True),
        lax.all_gather(weight_parts[1], ("seq", "dp"), axis=0, tiled=True),
        lax.all_gather(weight_parts[2], ("seq", "dp"), axis=0, tiled=True),
        lax.all_gather(weight_parts[3], ("seq", "dp"), axis=0, tiled=True),
        lax.all_gather(weight_parts[4], ("seq", "dp"), axis=0, tiled=True),
        lax.all_gather(weight_parts[5], ("seq", "dp"), axis=0, tiled=True),
        lax.all_gather(weight_parts[6], ("seq", "dp"), axis=0, tiled=True),
    )
    grad_query_weight = weight_sums[0].reshape(query_weight.shape)
    grad_key_weight = weight_sums[1].reshape(key_weight.shape)
    grad_value_weight = weight_sums[2].reshape(value_weight.shape)
    grad_output_weight = weight_sums[3].reshape(output_weight.shape)
    grad_inner_weight = weight_sums[4].reshape(inner_weight.shape)
    grad_outer_weight = weight_sums[5].reshape(outer_weight.shape)
    unpacked = unpack_flat(weight_sums[6], front_layouts + post_layouts)
    grad_query_bias, grad_value_bias, grad_conv_taps = (unpacked[0], unpacked[1], unpacked[2])
    post_small = unpacked[3:]
    (
        grad_output_bias,
        grad_first_gain,
        grad_first_bias,
        grad_inner_bias,
        grad_outer_bias,
        grad_second_gain,
        grad_second_bias,
    ) = post_small
    return (
        layer_out,
        input_grad,
        grad_query_weight,
        grad_query_bias,
        grad_key_weight,
        grad_value_weight,
        grad_value_bias,
        grad_conv_taps,
        grad_output_weight,
        grad_output_bias,
        grad_first_gain,
        grad_first_bias,
        grad_inner_weight,
        grad_inner_bias,
        grad_outer_weight,
        grad_outer_bias,
        grad_second_gain,
        grad_second_bias,
    )


def solution(mesh):
    return jax.shard_map(
        per_device,
        mesh=mesh,
        in_specs=(
            P("dp", "seq", None),
            P("dp", "seq"),
            P(),
            P(),
            P(),
            P(),
            P(),
            P(),
            P(),
            P(),
            P(),
            P(),
            P(),
            P(),
            P(),
            P(),
            P(),
            P(),
            P("dp", "seq", None),
        ),
        out_specs=(
            P("dp", "seq", None),
            P("dp", "seq", None),
            P(),
            P(),
            P(),
            P(),
            P(),
            P(),
            P(),
            P(),
            P(),
            P(),
            P(),
            P(),
            P(),
            P(),
            P(),
            P(),
        ),
        check_vma=False,
    )
```

profile of v0, /device:TPU:0, one launch (start us, length us, event | category | flops | bytes accessed | tf_op | source)
XLA Modules:
  0.0 1470.9 jit_solution(9400869609695777111)
XLA Ops:
  25.0 16.3 %all-gather = f32[64,768]{1,0:T(8,128)S(1)} all-gather(f32[8,768]{1,0:T(8,128)S(1)} %convolution_multiply_fusion.10), channel_id=2, replica_groups=mesh['seq'=8,'dp'=4] {'seq'}, dimensions={0}, use_global_device_ids=true | all-gather | bytes 221184 | tf_op jit(solution)/shard_map/all_gather | solution.py:150
  58.9 17.1 %pmax.7 = f32[12,64]{1,0:T(8,128)S(1)} all-reduce(f32[12,64]{1,0:T(8,128)S(1)} %get-tuple-element.301), channel_id=1, replica_groups=mesh['seq'=8,'dp'=4] {'seq'}, use_global_device_ids=true, to_apply=%region_8.9 | all-reduce | flops 768 | bytes 6144 | tf_op jit(solution)/shard_map/pmax | solution.py:172
  96.4 15.4 %all-gather.1 = f32[64,768]{1,0:T(8,128)} all-gather(f32[8,768]{1,0:T(8,128)S(1)} %convolution_multiply_fusion.9), channel_id=3, replica_groups=mesh['seq'=8,'dp'=4] {'seq'}, dimensions={0}, use_global_device_ids=true | all-gather | bytes 221184 | tf_op jit(solution)/shard_map/all_gather | solution.py:151
  165.7 14.9 %psum.22 = f32[12,64]{1,0:T(8,128)S(1)} all-reduce(f32[12,64]{1,0:T(8,128)S(1)} %copy-done.172), channel_id=1, replica_groups=mesh['seq'=8,'dp'=4] {'seq'}, use_global_device_ids=true, to_apply=%region_11.12 | all-reduce | flops 768 | bytes 6144 | tf_op jit(solution)/shard_map/psum | solution.py:174
  196.8 29.1 %add_add_fusion.2 = f32[1,512,768]{2,1,0:T(8,128)S(1)} fusion(f32[1,512,768]{2,1,0:T(8,128)} %copy.268, f32[1,544,768]{2,1,0:T(8,128)} %scatter.10, f32[768]{0:T(1024)S(1)} %broadcast_in_dim.420, f32[768]{0:T(1024)} %broadcast_in_dim.418, f32[768]{0:T(1024)} %broadcast_in_dim.416, f32[768]{0:T(1024)} %broadcast_in_dim.414, f32[768]{0:T(1024)} %broadcast_in_dim.412, ...), kind=kLoop, calls=%fused_computation.155 | loop fusion | flops 25952256 | bytes 55151616 | tf_op jit(solution)/shard_map/add | solution.py:211
  230.9 16.0 %fusion.48 = f32[512,3072]{1,0:T(8,128)S(1)} fusion(f32[768,3072]{1,0:T(8,128)S(1)} %bitcast.767, f32[1,512,768]{2,1,0:T(8,128)S(1)} %get-tuple-element.308, f32[768]{0:T(1024)S(1)} %copy-done.119, f32[768]{0:T(1024)S(1)} %copy-done.118, f32[512]{0:T(512)S(1)} %fusion.247, f32[512]{0:T(512)S(1)} %broadcast_multiply_fusion.2), kind=kOutput, calls=%fused_computation.93 | convolution fusion | flops 14497087488 | bytes 17311744 | tf_op jit(solution)/shard_map/jvp()/dot_general | solution.py:35
  246.9 30.6 %fusion.305 = (f32[512]{0:T(512)S(1)}, f32[1,512,768]{2,1,0:T(8,128)S(1)}) fusion(f32[768]{0:T(1024)S(1)} %copy-done.247, f32[3072,768]{1,0:T(8,128)} %param.41, f32[512,3072]{1,0:T(8,128)S(1)} %fusion.48, f32[3072]{0:T(1024)S(1)} %copy-done.245, f32[768]{0:T(1024)S(1)} %copy-done.119, f32[768]{0:T(1024)S(1)} %copy-done.118, f32[512]{0:T(512)S(1)} %fusion.247, ...), kind=kOutput, calls=%fused_computation.522 | convolution fusion | flops 14506131456 | bytes 18902016 | tf_op jit(solution)/shard_map/jvp()/dot_general | solution.py:35
  282.2 21.3 %fusion.307 = (f32[3072]{0:T(1024)}, f32[512,3072]{1,0:T(8,128)S(1)}) fusion(f32[3072,768]{1,0:T(8,128)} %param.41, f32[1,512,768]{2,1,0:T(8,128)S(1)} %get-tuple-element.244, f32[512]{0:T(512)S(1)} %negate_multiply_fusion.1, f32[512,3072]{1,0:T(8,128)S(1)} %fusion.48, f32[3072]{0:T(1024)S(1)} %copy-done.245), kind=kOutput, calls=%fused_computation.524 | convolution fusion | flops 14517924864 | bytes 23619584 | tf_op jit(solution)/shard_map/transpose(jvp())/dot_general | solution.py:35
  303.5 16.9 %multiply_reduce_fusion.1 = (f32[768]{0:T(1024)}, f32[512]{0:T(512)S(1)}, f32[768]{0:T(1024)}, f32[1,512,768]{2,1,0:T(8,128)S(1)}) fusion(f32[1,512,768]{2,1,0:T(8,128)S(1)} %get-tuple-element.308, f32[512]{0:T(512)S(1)} %fusion.247, f32[512]{0:T(512)S(1)} %broadcast_multiply_fusion.2, f32[768]{0:T(1024)S(1)} %copy-done.118, ...), kind=kOutput, calls=%fused_computation.109 | convolution fusion | flops 14499444736 | bytes 20464640 | tf_op jit(solution)/shard_map/transpose(jvp())/dot_general | solution.py:35
  335.7 11.4 multiply_bitcast_fusion.32
  362.9 19.6 %convolution_bitcast_fusion = f32[96,24,8,128]{3,2,1,0:T(8,128)} fusion(f32[512,3072]{1,0:T(8,128)} %copy-done.10, f32[1,512,768]{2,1,0:T(8,128)S(1)} %copy-done.8, f32[768]{0:T(1024)S(1)} %copy-done.119, f32[768]{0:T(1024)S(1)} %copy-done.118, f32[512]{0:T(512)S(1)} %fusion.247, f32[512]{0:T(512)S(1)} %broadcast_multiply_fusion.2), kind=kOutput, calls=%fused_computation.3 | convolution fusion | flops 14497087488 | bytes 17311744 | tf_op jit(solution)/shard_map/transpose(jvp())/dot_general | solution.py:35
  382.5 19.6 %fusion = f32[3072,768]{1,0:T(8,128)} fusion(f32[512,3072]{1,0:T(8,128)S(1)} %bitcast.775, f32[3072]{0:T(1024)S(1)} %copy-done.246, f32[1,512,768]{2,1,0:T(8,128)S(1)} %copy-done.17, f32[512]{0:T(512)S(1)} %negate_multiply_fusion.1), kind=kOutput, calls=%fused_computation.6 | convolution fusion | flops 14503772160 | bytes 17315840 | tf_op jit(solution)/shard_map/transpose(jvp())/dot_general | solution.py:35
  409.8 18.7 %pad_add_fusion = f32[1,544,768]{2,1,0:T(8,128)S(1)} fusion(f32[1,512,768]{2,1,0:T(8,128)} %get-tuple-element.252, f32[1,512,768]{2,1,0:T(8,128)} %get-tuple-element.253, f32[1,512,768]{2,1,0:T(8,128)} %get-tuple-element.254, f32[1,512,768]{2,1,0:T(8,128)} %get-tuple-element.255, f32[1,512,768]{2,1,0:T(8,128)} %get-tuple-element.256, ...), kind=kLoop, calls=%fused_computation.12 | loop fusion | flops 13369344 | bytes 53575680 | tf_op jit(solution)/shard_map/transpose(jvp())/add_any | solution.py:205
  583.5 13.6 reduce-scatter.5.cloned.1.call-done
  612.9 433.2 %all-reduce.84.cloned.1.call-done = (f32[589824]{0:T(1024)}, f32[589824]{0:T(1024)}, f32[589824]{0:T(1024)}, f32[589824]{0:T(1024)}, f32[2359296]{0:T(1024)}, /*index=5*/f32[2359296]{0:T(1024)}) async-done(((f32[589824]{0:T(1024)}, f32[589824]{0:T(1024)}, f32[589824]{0:T(1024)}, f32[589824]{0:T(1024)}, f32[2359296]{0:T(1024)}, /*index=5*/f32[2359296]{0:T(1024)}), (f32[589824]{0:T(1024)}, f32[589824]{0:T(1024)}, ...) | async-done | bytes 28311568
  1056.7 14.6 fusion.2
  1081.4 40.5 %all-reduce.69 = f32[9632]{0:T(1024)S(1)} all-reduce(f32[9632]{0:T(1024)S(1)} %pad.282), channel_id=7, replica_groups=mesh['seq'=8,'dp'=4] {'seq','dp'}, use_global_device_ids=true, to_apply=%region_79.80.clone | all-reduce | flops 9632 | bytes 77056
  1122.1 40.2 %all-reduce.67 = f32[9632]{0:T(1024)S(1)} all-reduce(f32[9632]{0:T(1024)S(1)} %dynamic-slice_dynamic-update-slice_fusion), channel_id=1, replica_groups=mesh['seq'=8,'dp'=4] {'seq','dp'}, use_global_device_ids=true, to_apply=%add.67 | all-reduce | flops 9632 | bytes 77056
  1183.1 42.9 %all-gather.13.cloned.1.call-done = f32[589824]{0:T(1024)} async-done(((f32[18432]{0:T(1024)}), f32[589824]{0:T(1024)}) %all-gather.13.cloned.1.call-update) | async-done | bytes 2359312 | tf_op jit(solution)/shard_map/all_gather | solution.py:344
  1229.4 55.7 %all-gather.15.cloned.1.call-done = f32[589824]{0:T(1024)} async-done(((f32[18432]{0:T(1024)}), f32[589824]{0:T(1024)}) %all-gather.15.cloned.1.call-update) | async-done | bytes 2359312 | tf_op jit(solution)/shard_map/all_gather | solution.py:345
  1288.5 80.9 %all-gather.17.cloned.1.call-done = f32[2359296]{0:T(1024)} async-done(((f32[73728]{0:T(1024)}), f32[2359296]{0:T(1024)}) %all-gather.17.cloned.1.call-update) | async-done | bytes 9437200 | tf_op jit(solution)/shard_map/all_gather | solution.py:346
  1369.4 10.9 reshape.2056
  1380.3 72.6 %all-gather.19.cloned.1.call-done = f32[2359296]{0:T(1024)} async-done(((f32[73728]{0:T(1024)}), f32[2359296]{0:T(1024)}) %all-gather.19.cloned.1.call-update) | async-done | bytes 9437200 | tf_op jit(solution)/shard_map/all_gather | solution.py:347
  1452.9 11.3 reshape.2058
  (866 shorter events, 386.8 us)
Async XLA Ops:
  7.2 180.4 %all-reduce.80.cloned.1.call-start = ((), (), s32[]{:S(2)}) async-start(), calls=%async_computation.2 | async-start | bytes 786432 | tf_op jit(solution)/shard_map/psum | solution.py:174
  80.4 393.7 %all-reduce.82.cloned.1.call-start = ((), (), s32[]{:S(2)}) async-start(), calls=%async_computation.3 | async-start | bytes 786432 | tf_op jit(solution)/shard_map/psum | solution.py:275
  83.4 97.2 %collective-permute-start = (f32[1,16,768]{2,1,0:T(8,128)}, f32[1,16,768]{2,1,0:T(8,128)}, u32[]{:S(2)}, u32[]{:S(2)}) collective-permute-start(f32[1,16,768]{2,1,0:T(8,128)} %dynamic-slice_bitcast_fusion), channel_id=1, source_target_pairs={{0,4},{4,8},{8,12},{12,16},{16,20},{20,24},{24,28},{1,5},{5,9},{9,... | collective-permute-start | bytes 147464 | tf_op jit(solution)/shard_map/ppermute | solution.py:26
  86.7 95.5 %collective-permute-start.1 = (f32[1,16,768]{2,1,0:T(8,128)}, f32[1,16,768]{2,1,0:T(8,128)}, u32[]{:S(2)}, u32[]{:S(2)}) collective-permute-start(f32[1,16,768]{2,1,0:T(8,128)} %slice.631), channel_id=1, source_target_pairs={{4,0},{8,4},{12,8},{16,12},{20,16},{24,20},{28,24},{5,1},{9,5},{13... | collective-permute-start | bytes 147464 | tf_op jit(solution)/shard_map/ppermute | solution.py:29
  409.7 158.2 %reduce-scatter.3.cloned.1.call-start = ((), (), s32[]{:S(2)}) async-start(), calls=%async_computation.4 | async-start | bytes 221184 | tf_op jit(solution)/shard_map/reduce_scatter | solution.py:296
  430.5 40.2 %collective-permute-start.2 = (f32[1,16,768]{2,1,0:T(8,128)}, f32[1,16,768]{2,1,0:T(8,128)}, u32[]{:S(2)}, u32[]{:S(2)}) collective-permute-start(f32[1,16,768]{2,1,0:T(8,128)} %get-tuple-element.247), channel_id=1, source_target_pairs={{0,4},{4,8},{8,12},{12,16},{16,20},{20,24},{24,28},{1,5},{5,9},{9,... | collective-permute-start | bytes 147464 | tf_op jit(solution)/shard_map/ppermute | solution.py:26
  470.7 126.4 %reduce-scatter.5.cloned.1.call-start = ((), (), s32[]{:S(2)}) async-start(), calls=%async_computation.5 | async-start | bytes 221184 | tf_op jit(solution)/shard_map/reduce_scatter | solution.py:295
  472.2 62.7 %collective-permute-start.3 = (f32[1,16,768]{2,1,0:T(8,128)}, f32[1,16,768]{2,1,0:T(8,128)}, u32[]{:S(2)}, u32[]{:S(2)}) collective-permute-start(f32[1,16,768]{2,1,0:T(8,128)} %get-tuple-element.245), channel_id=1, source_target_pairs={{4,0},{8,4},{12,8},{16,12},{20,16},{24,20},{28,24},{5,1},{9,5},{13... | collective-permute-start | bytes 147464 | tf_op jit(solution)/shard_map/ppermute | solution.py:29
  567.6 478.4 %all-reduce.84.cloned.1.call-start = ((), (), s32[]{:S(2)}) async-start(), calls=%async_computation.12 | async-start | bytes 56623104
  612.7 443.8 %copy-start.198 = (f32[768]{0:T(1024)S(1)}, f32[768]{0:T(1024)}, u32[]{:S(2)}) copy-start(f32[768]{0:T(1024)} %get-tuple-element.179) | copy-start | bytes 9220
  612.7 443.8 %copy-start.197 = (f32[768]{0:T(1024)S(1)}, f32[768]{0:T(1024)}, u32[]{:S(2)}) copy-start(f32[768]{0:T(1024)} %get-tuple-element.178) | copy-start | bytes 9220
  612.7 443.8 %copy-start.196 = (f32[768]{0:T(1024)S(1)}, f32[768]{0:T(1024)}, u32[]{:S(2)}) copy-start(f32[768]{0:T(1024)} %get-tuple-element.177) | copy-start | bytes 9220
  612.8 443.8 %copy-start.195 = (f32[768]{0:T(1024)S(1)}, f32[768]{0:T(1024)}, u32[]{:S(2)}) copy-start(f32[768]{0:T(1024)} %get-tuple-element.176) | copy-start | bytes 9220
  612.8 443.8 %copy-start.194 = (f32[768]{0:T(1024)S(1)}, f32[768]{0:T(1024)}, u32[]{:S(2)}) copy-start(f32[768]{0:T(1024)} %get-tuple-element.175) | copy-start | bytes 9220
  612.8 443.8 %copy-start.193 = (f32[768]{0:T(1024)S(1)}, f32[768]{0:T(1024)}, u32[]{:S(2)}) copy-start(f32[768]{0:T(1024)} %get-tuple-element.174) | copy-start | bytes 9220
  612.8 443.8 %copy-start.192 = (f32[768]{0:T(1024)S(1)}, f32[768]{0:T(1024)}, u32[]{:S(2)}) copy-start(f32[768]{0:T(1024)} %get-tuple-element.173) | copy-start | bytes 9220
  612.8 443.8 %copy-start.191 = (f32[768]{0:T(1024)S(1)}, f32[768]{0:T(1024)}, u32[]{:S(2)}) copy-start(f32[768]{0:T(1024)} %get-tuple-element.172) | copy-start | bytes 9220
  612.8 443.9 %copy-start.190 = (f32[768]{0:T(1024)S(1)}, f32[768]{0:T(1024)}, u32[]{:S(2)}) copy-start(f32[768]{0:T(1024)} %get-tuple-element.171) | copy-start | bytes 9220
  612.8 563.6 %all-gather.9.cloned.1.call-start = ((), (), s32[]{:S(2)}) async-start(), calls=%async_computation.6 | async-start | bytes 2433024 | tf_op jit(solution)/shard_map/all_gather | solution.py:342
  1047.6 132.1 %all-gather.11.cloned.1.call-start = ((), (), s32[]{:S(2)}) async-start(), calls=%async_computation.7 | async-start | bytes 2433024 | tf_op jit(solution)/shard_map/all_gather | solution.py:343
  1049.2 176.8 %all-gather.13.cloned.1.call-start = ((), (), s32[]{:S(2)}) async-start(), calls=%async_computation.8 | async-start | bytes 2433024 | tf_op jit(solution)/shard_map/all_gather | solution.py:344
  1050.8 234.3 %all-gather.15.cloned.1.call-start = ((), (), s32[]{:S(2)}) async-start(), calls=%async_computation.9 | async-start | bytes 2433024 | tf_op jit(solution)/shard_map/all_gather | solution.py:345
  1052.4 317.0 %all-gather.17.cloned.1.call-start = ((), (), s32[]{:S(2)}) async-start(), calls=%async_computation.10 | async-start | bytes 9732096 | tf_op jit(solution)/shard_map/all_gather | solution.py:346
  1054.2 398.8 %all-gather.19.cloned.1.call-start = ((), (), s32[]{:S(2)}) async-start(), calls=%async_computation.11 | async-start | bytes 9732096 | tf_op jit(solution)/shard_map/all_gather | solution.py:347
  (247 other events, 5930.4 us)
Sparse Core Ops, SparseCore 0:
  80.6 53.9 all-reduce.79
  409.9 53.7 all-reduce.81
  470.8 28.5 reduce-scatter.2
  567.7 29.2 reduce-scatter.4
  612.8 433.2 all-reduce.83
  1049.4 57.2 all-gather.8
  1110.2 56.1 all-gather.10
  1169.8 56.1 all-gather.12
  1228.9 56.1 all-gather.14
  1288.4 80.9 all-gather.16
  1372.3 80.6 all-gather.18
where the time goes:
time: 1480 us; the launch traced here: 1470 us
  waiting for transfers between devices  699 us (47%)
  matrix products  310 us (21%)
  local copies, waits for them, and re-layouts  170 us (11%)
  blocking collectives  144 us (10%)
  other arithmetic  118 us (8%)
  between operations  20.7 us (1%)
    unnamed x12, waiting for transfers between devices  433 us
    dot_general x18, matrix products, matmul(): jnp.dot(left, right, precision=highest, preferred_element_type=jnp.float32)  201 us
    dot_general x94, matrix products, contract(): jnp.einsum(form, left, right, precision=highest, preferred_element_type=j...  109 us
    all_gather x1, waiting for transfers between devices, per_device(): lax.all_gather(weight_parts[4], ('seq', 'dp'), axis=0, tiled=True)  80.9 us
    unnamed x2, blocking collectives  80.7 us
    all_gather x1, waiting for transfers between devices, per_device(): lax.all_gather(weight_parts[5], ('seq', 'dp'), axis=0, tiled=True)  72.6 us
    all_gather x1, waiting for transfers between devices, per_device(): lax.all_gather(weight_parts[3], ('seq', 'dp'), axis=0, tiled=True)  55.7 us
    all_gather x1, waiting for transfers between devices, per_device(): lax.all_gather(weight_parts[2], ('seq', 'dp'), axis=0, tiled=True)  42.9 us
  transfers between devices with their start and end apart: 15, of which 6 were waited for; matrix products, arithmetic and copies ran while one was open for 21% of the time, Pallas kernels for 0%

commit v1 on v0

v1 whole, which is shorter than its diff:
```python
from functools import partial
import math

import jax
import jax.numpy as jnp
from jax import lax
from jax.experimental import pallas as pl
from jax.experimental.pallas import tpu as pltpu
from jax.sharding import PartitionSpec as P

HEADS = 12
DH = 64
CONV = 33
NEWTON = 6
RIM = (CONV - 1) // 2
LANES = 128
PAIRS = HEADS * DH // LANES
QUAD = 256
SCALE = DH ** (-0.5)
EPS = 1e-05
ROOT_HALF = 0.7071067811865476
INV_ROOT_TAU = 0.3989422804014327
MASKED = -1e30
f32 = jnp.float32
HI = lax.Precision.HIGH
TOP = lax.Precision.HIGHEST
MESH = pl.DeviceIdType.MESH
VMEM_CAP = 60 << 20


def _dg(a, b, ca, cb, prec):
    return lax.dot_general(
        a, b, (((ca,), (cb,)), ((), ())), precision=prec, preferred_element_type=f32
    )


def mm(a, b, prec=HI):
    return _dg(a, b, 1, 0, prec)


def mm_t(a, b, prec=HI):
    return _dg(a, b, 1, 1, prec)


def t_mm(a, b, prec=HI):
    return _dg(a, b, 0, 0, prec)


def head_mask(size):
    row = lax.broadcasted_iota(jnp.int32, (size, size), 0) >> 6
    col = lax.broadcasted_iota(jnp.int32, (size, size), 1) >> 6
    return row == col


def spread(rows, mask):
    return jnp.where(mask, jnp.concatenate([rows] * (mask.shape[0] // DH), axis=0), 0.0)


def fold(square, mask):
    kept = jnp.where(mask, square, 0.0)
    total = kept[:DH]
    for at in range(DH, mask.shape[0], DH):
        total = total + kept[at : at + DH]
    return total


def seg_ends(lens_ref, count):
    ends = []
    total = 0
    for j in range(count):
        total = total + lens_ref[0, j]
        ends.append(total)
    return ends


def member_rows(ends, slots):
    shape = (len(ends), slots)
    row = lax.broadcasted_iota(jnp.int32, shape, 0)
    col = lax.broadcasted_iota(jnp.int32, shape, 1)
    low = jnp.zeros(shape, jnp.int32)
    high = jnp.zeros(shape, jnp.int32)
    before = 0
    for j, end in enumerate(ends):
        low = jnp.where(row == j, before, low)
        high = jnp.where(row == j, end, high)
        before = end
    return jnp.where((col >= low) & (col < high), 1.0, 0.0)


def inverse_lens(lens_ref, count):
    row = lax.broadcasted_iota(jnp.int32, (count, 1), 0)
    out = jnp.zeros((count, 1), f32)
    for j in range(count):
        out = jnp.where(row == j, lens_ref[0, j].astype(f32), out)
    return 1.0 / out


def valid_rows(count, slots):
    return lax.broadcasted_iota(jnp.int32, (slots, 1), 0) < count


def rims_of(matrix, count):
    slots = matrix.shape[0]
    row = lax.broadcasted_iota(jnp.int32, (2 * RIM, slots), 0)
    col = lax.broadcasted_iota(jnp.int32, (2 * RIM, slots), 1)
    want = jnp.where(row < RIM, row, row - 2 * RIM + count)
    return mm(jnp.where(col == want, 1.0, 0.0), matrix)


def fill_extended(ext_ref, middle, left, right, count):
    slots = middle.shape[0]
    ext_ref[0:RIM, :] = left
    ext_ref[RIM : RIM + slots, :] = middle
    tail = ext_ref.shape[0] - RIM - slots
    ext_ref[RIM + slots :, :] = jnp.zeros((tail, middle.shape[1]), f32)
    rows = slots + RIM
    row = lax.broadcasted_iota(jnp.int32, (rows, RIM), 0)
    col = lax.broadcasted_iota(jnp.int32, (rows, RIM), 1)
    put = jnp.where(row == col + count, 1.0, 0.0)
    ext_ref[RIM : RIM + rows, :] += mm(put, right)


CONV_ROWS = 64


def shifted(ext_ref, r0, l0):
    slab = ext_ref[pl.ds(r0, CONV_ROWS + 40), pl.ds(l0, LANES)]
    for b in range(8):
        moved = slab[b : b + CONV_ROWS + 32]
        for a in range(5):
            if 8 * a + b < CONV:
                yield 8 * a + b, moved[8 * a : 8 * a + CONV_ROWS]


def conv_into(out_ref, ext_ref, taps_ref, slots, flip, add):
    def block(i, carry):
        r0 = pl.multiple_of((i // PAIRS) * CONV_ROWS, CONV_ROWS)
        l0 = pl.multiple_of((i % PAIRS) * LANES, LANES)
        acc = jnp.zeros((CONV_ROWS, LANES), f32)
        for c, part in shifted(ext_ref, r0, l0):
            at = CONV - 1 - c if flip else c
            acc = acc + taps_ref[at : at + 1, pl.ds(l0, LANES)] * part
        here = (pl.ds(r0, CONV_ROWS), pl.ds(l0, LANES))
        if add:
            out_ref[here] += acc
        else:
            out_ref[here] = acc
        return carry

    lax.fori_loop(0, (slots // CONV_ROWS) * PAIRS, block, 0)


def taps_grad_into(scr_ref, grad_ref, ext_ref, slots):
    scr_ref[...] = jnp.zeros_like(scr_ref)

    def block(i, carry):
        r0 = pl.multiple_of((i // PAIRS) * CONV_ROWS, CONV_ROWS)
        l0 = pl.multiple_of((i % PAIRS) * LANES, LANES)
        grad = grad_ref[pl.ds(r0, CONV_ROWS), pl.ds(l0, LANES)]
        for c, part in shifted(ext_ref, r0, l0):
            prod = grad * part
            total = prod[0:8]
            for at in range(8, CONV_ROWS, 8):
                total = total + prod[at : at + 8]
            scr_ref[c, :, pl.ds(l0, LANES)] += total
        return carry

    lax.fori_loop(0, (slots // CONV_ROWS) * PAIRS, block, 0)


def whole(shape=None):
    return pl.BlockSpec(memory_space=pltpu.VMEM)


def smem():
    return pl.BlockSpec(memory_space=pltpu.SMEM)


def params(**more):
    return pltpu.CompilerParams(vmem_limit_bytes=VMEM_CAP, **more)


def shape(*dims):
    return jax.ShapeDtypeStruct(dims, f32)


def project_kernel(
    lens_ref, x_ref, wq_ref, wk_ref, wv_ref, bq_ref, bv_ref,
    q_ref, k_ref, v_ref, land_ref, rim_ref,
):
    slots = x_ref.shape[0]
    segs = land_ref.shape[1]
    ends = seg_ends(lens_ref, segs)
    member = member_rows(ends, slots)
    inv = inverse_lens(lens_ref, segs)
    x = x_ref[...]
    q = mm(x, wq_ref[...]) + bq_ref[...][None, :]
    k = mm(x, wk_ref[...])
    v = mm(x, wv_ref[...]) + bv_ref[...][None, :]
    v = jnp.where(valid_rows(ends[-1], slots), v, 0.0)
    q_ref[...] = q
    k_ref[...] = k
    v_ref[...] = v
    land_ref[0] = mm(member, q) * inv
    land_ref[1] = mm(member, k) * inv
    rim_ref[...] = rims_of(v, ends[-1])


def project(lens, x, wq, wk, wv, bq, bv):
    slots, width = x.shape
    segs = lens.shape[1]
    col = 256
    wspec = pl.BlockSpec((width, col), lambda i: (0, i))
    bspec = pl.BlockSpec((col,), lambda i: (i,))
    ospec = pl.BlockSpec((slots, col), lambda i: (0, i))
    return pl.pallas_call(
        project_kernel,
        grid=(width // col,),
        in_specs=[smem(), pl.BlockSpec((slots, width), lambda i: (0, 0)), wspec, wspec, wspec, bspec, bspec],
        out_specs=[
            ospec, ospec, ospec,
            pl.BlockSpec((2, segs, col), lambda i: (0, 0, i)),
            pl.BlockSpec((2 * RIM, col), lambda i: (0, i)),
        ],
        out_shape=[
            shape(slots, width), shape(slots, width), shape(slots, width),
            shape(2, segs, width), shape(2 * RIM, width),
        ],
        compiler_params=params(),
        name="project",
    )(lens, x, wq, wk, wv, bq, bv)


def greet_all(n):
    me = lax.axis_index("seq")
    barrier = pltpu.get_barrier_semaphore()
    for d in range(1, n):
        pl.semaphore_signal(
            barrier, inc=1, device_id={"seq": lax.rem(me + d, n)}, device_id_type=MESH
        )
    pl.semaphore_wait(barrier, n - 1)
    return me


def to_seq(src, dst, send, recv, target):
    return pltpu.make_async_remote_copy(
        src, dst, send, recv, device_id={"seq": target}, device_id_type=MESH
    )


def rim_copies(n, me, rim_ref, left_ref, right_ref, rsend, rrecv):
    up = to_seq(rim_ref.at[pl.ds(RIM, RIM)], left_ref, rsend.at[0], rrecv.at[0], lax.rem(me + 1, n))
    down = to_seq(rim_ref.at[pl.ds(0, RIM)], right_ref, rsend.at[1], rrecv.at[1], lax.rem(me + n - 1, n))
    return up, down


def rim_start(n, me, up, down, left_ref, right_ref):
    @pl.when(me < n - 1)
    def _():
        up.start()

    @pl.when(me > 0)
    def _():
        down.start()

    @pl.when(me == 0)
    def _():
        left_ref[...] = jnp.zeros_like(left_ref)

    @pl.when(me == n - 1)
    def _():
        right_ref[...] = jnp.zeros_like(right_ref)


def rim_wait(n, me, up, down):
    @pl.when(me > 0)
    def _():
        up.wait_recv()
        down.wait_send()

    @pl.when(me < n - 1)
    def _():
        down.wait_recv()
        up.wait_send()


def land_exchange_kernel(
    n, mine_ref, rim_ref, all_ref, left_ref, right_ref, send, recv, rsend, rrecv
):
    me = greet_all(n)
    up, down = rim_copies(n, me, rim_ref, left_ref, right_ref, rsend, rrecv)
    copies = []
    for d in range(1, n):
        copy = to_seq(
            mine_ref, all_ref.at[me], send.at[d], recv.at[me], lax.rem(me + d, n)
        )
        copy.start()
        copies.append(copy)
    rim_start(n, me, up, down, left_ref, right_ref)
    all_ref[me] = mine_ref[...]
    for d in range(1, n):
        source = lax.rem(me + d, n)
        to_seq(mine_ref, all_ref.at[source], send.at[d], recv.at[source], source).wait_recv()
    rim_wait(n, me, up, down)
    for copy in copies:
        copy.wait_send()


def land_exchange(n, mine, rim):
    _, segs, width = mine.shape
    dma = pltpu.SemaphoreType.DMA
    return pl.pallas_call(
        partial(land_exchange_kernel, n),
        in_specs=[whole()] * 2,
        out_specs=[whole()] * 3,
        out_shape=[shape(n, 2, segs, width), shape(RIM, width), shape(RIM, width)],
        scratch_shapes=[dma((n,)), dma((n,)), dma((2,)), dma((2,))],
        compiler_params=params(collective_id=1, has_side_effects=True),
        name="land_exchange",
    )(mine, rim)


MSG = DH + 8


def eye(size):
    row = lax.broadcasted_iota(jnp.int32, (size, size), 0)
    col = lax.broadcasted_iota(jnp.int32, (size, size), 1)
    return jnp.where(row == col, 1.0, 0.0)


def pair_sums(row):
    lane = lax.broadcasted_iota(jnp.int32, row.shape, 1)
    first = jnp.sum(jnp.where(lane < DH, row, 0.0), axis=1, keepdims=True)
    second = jnp.sum(jnp.where(lane < DH, 0.0, row), axis=1, keepdims=True)
    return jnp.where(lane < DH, first, second)


def core_of(query, key, mask):
    scores = jnp.where(mask, mm_t(query, key, TOP) * SCALE, MASKED)
    raised = jnp.exp(scores - jnp.max(scores, axis=1, keepdims=True))
    return raised / jnp.sum(raised, axis=1, keepdims=True)


def far_exchange_kernel(
    n, f_ref, ql_ref, kl_ref, b_ref, core_ref, zs_ref, ps_ref, rs_ref, qs_ref, mx_ref,
    land, s1, r1, s2, r2,
):
    me = greet_all(n)
    for p in range(PAIRS):

        @pl.when(me != p)
        def _(p=p):
            to_seq(f_ref.at[p], land.at[me], s1.at[p], r1.at[me], p).start()

    @pl.when(me < PAIRS)
    def _():
        mask = head_mask(LANES)
        lanes = pl.ds(pl.multiple_of(me * LANES, LANES), LANES)
        query = spread(ql_ref[:, lanes], mask)
        key = spread(kl_ref[:, lanes], mask)
        core = core_of(query, key, mask)
        core_ref[...] = core
        colsum = jnp.sum(core, axis=0, keepdims=True)
        sigma = jnp.sqrt(pair_sums(colsum * colsum))
        z = core.T / sigma
        unit = eye(LANES)
        for step in range(NEWTON):
            zs_ref[step] = z
            prod = mm(core, z, TOP)
            ps_ref[step] = prod
            r = 15.0 * unit - mm(prod, 7.0 * unit - prod, TOP)
            rs_ref[step] = r
            q = 13.0 * unit - mm(prod, r, TOP)
            qs_ref[step] = q
            z = 0.25 * mm(z, q, TOP)
        zs_ref[NEWTON] = z
        land[me] = f_ref[me]
        for s in range(n):

            @pl.when(me != s)
            def _(s=s):
                to_seq(f_ref.at[0], land.at[s], s1.at[0], r1.at[s], s).wait_recv()

        top = land[0][DH : DH + 1]
        for s in range(1, n):
            top = jnp.maximum(top, land[s][DH : DH + 1])
        total = jnp.zeros_like(top)
        mixed = jnp.zeros((DH, LANES), f32)
        for s in range(n):
            part = land[s]
            factor = jnp.exp(part[DH : DH + 1] - top)
            total = total + part[DH + 1 : DH + 2] * factor
            mixed = mixed + part[:DH] * factor
        mixed = mixed / total
        mx_ref[...] = mixed
        b_ref[me, 0:DH, :] = mm_t(mixed, z, TOP)
        pad = jnp.zeros((MSG - DH - 2, LANES), f32)
        b_ref[me, DH:MSG, :] = jnp.concatenate([top, total, pad], axis=0)
        for t in range(n):

            @pl.when(me != t)
            def _(t=t):
                to_seq(b_ref.at[me], b_ref.at[me], s2.at[t], r2.at[me], t).start()

    for p in range(PAIRS):

        @pl.when(me != p)
        def _(p=p):
            to_seq(b_ref.at[p], b_ref.at[p], s2.at[p], r2.at[p], p).wait_recv()
            to_seq(f_ref.at[p], land.at[me], s1.at[p], r1.at[me], p).wait_send()

    @pl.when(me < PAIRS)
    def _():
        for t in range(n):

            @pl.when(me != t)
            def _(t=t):
                to_seq(b_ref.at[me], b_ref.at[me], s2.at[t], r2.at[me], t).wait_send()


def far_exchange(n, parts, ql, kl):
    dma = pltpu.SemaphoreType.DMA
    square = (LANES, LANES)
    return pl.pallas_call(
        partial(far_exchange_kernel, n),
        in_specs=[whole()] * 3,
        out_specs=[whole()] * 7,
        out_shape=[
            shape(PAIRS, MSG, LANES), shape(*square), shape(NEWTON + 1, *square),
            shape(NEWTON, *square), shape(NEWTON, *square), shape(NEWTON, *square),
            shape(DH, LANES),
        ],
        scratch_shapes=[pltpu.VMEM((n, MSG, LANES), f32), dma((PAIRS,)), dma((n,)), dma((n,)), dma((n,))],
        compiler_params=params(collective_id=2, has_side_effects=True),
        name="far_exchange",
    )(parts, ql, kl)


def blend_exchange_kernel(
    n, g_ref, rim_ref, ql_ref, kl_ref, core_ref, zs_ref, ps_ref, rs_ref, qs_ref, mx_ref,
    c_ref, left_ref, right_ref, gl_ref,
    land, s1, r1, s2, r2, rsend, rrecv,
):
    me = greet_all(n)
    for p in range(PAIRS):

        @pl.when(me != p)
        def _(p=p):
            to_seq(g_ref.at[p], land.at[me], s1.at[p], r1.at[me], p).start()

    up, down = rim_copies(n, me, rim_ref, left_ref, right_ref, rsend, rrecv)
    rim_start(n, me, up, down, left_ref, right_ref)

    @pl.when(me >= PAIRS)
    def _():
        gl_ref[...] = jnp.zeros_like(gl_ref)

    @pl.when(me < PAIRS)
    def _():
        mask = head_mask(LANES)
        land[me] = g_ref[me]
        for s in range(n):

            @pl.when(me != s)
            def _(s=s):
                to_seq(g_ref.at[0], land.at[s], s1.at[0], r1.at[s], s).wait_recv()

        gblend = land[0]
        for s in range(1, n):
            gblend = gblend + land[s]
        mixed = mx_ref[...]
        gmixed = mm(gblend, zs_ref[NEWTON], TOP)
        c_ref[me, 0:DH, :] = gmixed
        dots = jnp.sum(gmixed * mixed, axis=0, keepdims=True)
        pad = jnp.zeros((MSG - DH - 1, LANES), f32)
        c_ref[me, DH:MSG, :] = jnp.concatenate([dots, pad], axis=0)
        for t in range(n):

            @pl.when(me != t)
            def _(t=t):
                to_seq(c_ref.at[me], c_ref.at[me], s2.at[t], r2.at[me], t).start()

        core = core_ref[...]
        core_t = core.T
        unit = eye(LANES)
        g = jnp.where(mask, t_mm(gblend, mixed, TOP), 0.0)
        gcore = jnp.zeros((LANES, LANES), f32)
        for step in reversed(range(NEWTON)):
            z = zs_ref[step]
            prod_t = ps_ref[step].T
            gq = 0.25 * mm(z.T, g, TOP)
            gr = -mm(prod_t, gq, TOP)
            gs = -mm(prod_t, gr, TOP)
            gp = -mm_t(gq, rs_ref[step], TOP) - mm_t(gr, 7.0 * unit - ps_ref[step], TOP) - gs
            gcore = gcore + mm_t(gp, z, TOP)
            g = 0.25 * mm_t(g, qs_ref[step], TOP) + mm(core_t, gp, TOP)
        colsum = jnp.sum(core, axis=0, keepdims=True)
        square = pair_sums(colsum * colsum)
        sigma = jnp.sqrt(square)
        dot = pair_sums(jnp.sum(g * zs_ref[0], axis=0, keepdims=True))
        gcore = gcore + g.T / sigma - jnp.where(mask, dot / square * colsum, 0.0)
        gscore = core * (gcore - jnp.sum(core * gcore, axis=1, keepdims=True)) * SCALE
        lanes = pl.ds(pl.multiple_of(me * LANES, LANES), LANES)
        query = spread(ql_ref[:, lanes], mask)
        key = spread(kl_ref[:, lanes], mask)
        gl_ref[...] = jnp.zeros_like(gl_ref)
        gl_ref[0, :, lanes] = fold(mm(gscore, key, TOP), mask)
        gl_ref[1, :, lanes] = fold(t_mm(gscore, query, TOP), mask)

    for p in range(PAIRS):

        @pl.when(me != p)
        def _(p=p):
            to_seq(c_ref.at[p], c_ref.at[p], s2.at[p], r2.at[p], p).wait_recv()
            to_seq(g_ref.at[p], land.at[me], s1.at[p], r1.at[me], p).wait_send()

    rim_wait(n, me, up, down)

    @pl.when(me < PAIRS)
    def _():
        for t in range(n):

            @pl.when(me != t)
            def _(t=t):
                to_seq(c_ref.at[me], c_ref.at[me], s2.at[t], r2.at[me], t).wait_send()


def blend_exchange(n, gblend, rim, ql, kl, saved):
    dma = pltpu.SemaphoreType.DMA
    width = rim.shape[1]
    return pl.pallas_call(
        partial(blend_exchange_kernel, n),
        in_specs=[whole()] * 10,
        out_specs=[whole()] * 4,
        out_shape=[shape(PAIRS, MSG, LANES), shape(RIM, width), shape(RIM, width), shape(2, DH, width)],
        scratch_shapes=[
            pltpu.VMEM((n, DH, LANES), f32),
            dma((PAIRS,)), dma((n,)), dma((n,)), dma((n,)), dma((2,)), dma((2,)),
        ],
        compiler_params=params(collective_id=3, has_side_effects=True),
        name="blend_exchange",
    )(gblend, rim, ql, kl, *saved)


def land_return_kernel(n, x_ref, own_ref, land, send, recv):
    me = greet_all(n)
    copies = []
    for d in range(1, n):
        target = lax.rem(me + d, n)
        copy = to_seq(x_ref.at[target], land.at[me], send.at[d], recv.at[me], target)
        copy.start()
        copies.append(copy)
    land[me] = x_ref[me]
    for d in range(1, n):
        source = lax.rem(me + d, n)
        to_seq(x_ref.at[0], land.at[source], send.at[d], recv.at[source], source).wait_recv()
    total = land[0]
    for s in range(1, n):
        total = total + land[s]
    own_ref[...] = total
    for copy in copies:
        copy.wait_send()


def land_return(n, parts):
    dma = pltpu.SemaphoreType.DMA
    return pl.pallas_call(
        partial(land_return_kernel, n),
        in_specs=[whole()],
        out_specs=whole(),
        out_shape=shape(*parts.shape[1:]),
        scratch_shapes=[pltpu.VMEM(parts.shape, f32), dma((n,)), dma((n,))],
        compiler_params=params(collective_id=4, has_side_effects=True),
        name="land_return",
    )(parts)


def far_kernel(lens_ref, k_ref, v_ref, ql_ref, f_ref, p_ref, m_ref):
    slots = k_ref.shape[0]
    count = seg_ends(lens_ref, lens_ref.shape[1])[-1]
    valid = valid_rows(count, slots)
    mask = head_mask(QUAD)
    for g in range(HEADS * DH // QUAD):
        cols = slice(g * QUAD, (g + 1) * QUAD)
        scores = mm_t(k_ref[:, cols], spread(ql_ref[:, cols], mask)) * SCALE
        scores = jnp.where(valid, scores, MASKED)
        top = jnp.max(scores, axis=0, keepdims=True)
        raised = jnp.where(valid, jnp.exp(scores - top), 0.0)
        p_ref[:, cols] = raised
        m_ref[:, cols] = top
        total = jnp.sum(raised, axis=0, keepdims=True)
        weighted = fold(t_mm(v_ref[:, cols], raised), mask)
        tail = jnp.concatenate([top, total, jnp.zeros((MSG - DH - 2, QUAD), f32)], axis=0)
        for j in range(QUAD // LANES):
            part = slice(j * LANES, (j + 1) * LANES)
            f_ref[g * 2 + j, 0:DH, :] = weighted[:, part]
            f_ref[g * 2 + j, DH:MSG, :] = tail[:, part]


def far_local(lens, k, v, ql):
    slots, width = k.shape
    return pl.pallas_call(
        far_kernel,
        in_specs=[smem()] + [whole()] * 3,
        out_specs=[whole()] * 3,
        out_shape=[shape(PAIRS, MSG, LANES), shape(slots, width), shape(1, width)],
        compiler_params=params(),
        name="far_local",
    )(lens, k, v, ql)


def norm_stats(r):
    centered = r - jnp.mean(r, axis=1, keepdims=True)
    spread_ = jnp.mean(centered * centered, axis=1, keepdims=True)
    inv = lax.rsqrt(spread_ + EPS)
    return centered * inv, inv


def norm_back(unit, inv, gain, grad):
    ge = grad * gain
    return (
        ge
        - jnp.mean(ge, axis=1, keepdims=True)
        - unit * jnp.mean(ge * unit, axis=1, keepdims=True)
    ) * inv


def pair_rows(ref, g, rows):
    return jnp.concatenate([ref[2 * g, rows, :], ref[2 * g + 1, rows, :]], axis=1)


def attend_kernel(
    lens_ref, q_ref, v_ref, kl_ref, b_ref, left_ref, right_ref, taps_ref, x_ref, wo_ref, bo_ref, g1_ref, b1_ref,
    near_ref, ctx_ref, h1_ref, u1_ref, inv1_ref,
    ext_ref,
):
    slots = q_ref.shape[0]
    count = seg_ends(lens_ref, lens_ref.shape[1])[-1]
    fill_extended(ext_ref, v_ref[...], left_ref[...], right_ref[...], count)
    conv_into(ctx_ref, ext_ref, taps_ref, slots, False, False)
    mask = head_mask(QUAD)
    ones = jnp.where(mask, 1.0, 0.0)
    head = lax.broadcasted_iota(jnp.int32, (slots, QUAD), 1) >> 6
    for g in range(HEADS * DH // QUAD):
        cols = slice(g * QUAD, (g + 1) * QUAD)
        scores = mm_t(q_ref[:, cols], spread(kl_ref[:, cols], mask)) * SCALE
        tops = [jnp.max(scores[:, h * DH : (h + 1) * DH], axis=1, keepdims=True) for h in range(4)]
        top = jnp.where(head < 2, jnp.where(head < 1, tops[0], tops[1]), jnp.where(head < 3, tops[2], tops[3]))
        raised = jnp.exp(scores - top)
        near = raised / mm(raised, ones)
        near_ref[:, cols] = near
        blend = spread(pair_rows(b_ref, g, slice(0, DH)), mask)
        ctx_ref[:, cols] += mm_t(near, blend)
    summed = x_ref[...] + (mm(ctx_ref[...], wo_ref[...]) + bo_ref[...][None, :])
    unit, inv = norm_stats(summed)
    u1_ref[...] = unit
    inv1_ref[...] = inv
    h1_ref[...] = unit * g1_ref[...][None, :] + b1_ref[...][None, :]


def attend(lens, q, v, kl, b, left, right, taps, x, wo, bo, g1, b1):
    slots, width = q.shape
    return pl.pallas_call(
        attend_kernel,
        in_specs=[smem()] + [whole()] * 12,
        out_specs=[whole()] * 5,
        out_shape=[shape(slots, width)] * 4 + [shape(slots, 1)],
        scratch_shapes=[pltpu.VMEM((slots + 40, width), f32)],
        compiler_params=params(),
        name="attend",
    )(lens, q, v, kl, b, left, right, taps, x, wo, bo, g1, b1)


def forward_kernel(
    lens_ref, h1_ref, wi_ref, bi_ref, wo_ref, bo_ref, cot_ref, g2_ref, b2_ref,
    pre_ref, out_ref, gs2_ref, small_ref,
    acc_ref,
):
    step = pl.program_id(0)
    pre = mm(h1_ref[...], wi_ref[...]) + bi_ref[...]
    pre_ref[...] = pre
    act = 0.5 * pre * (1.0 + lax.erf(pre * ROOT_HALF))
    part = mm(act, wo_ref[...])

    @pl.when(step == 0)
    def _():
        acc_ref[...] = part

    @pl.when(step > 0)
    def _():
        acc_ref[...] += part

    @pl.when(step == pl.num_programs(0) - 1)
    def _():
        slots = h1_ref.shape[0]
        valid = valid_rows(seg_ends(lens_ref, lens_ref.shape[1])[-1], slots)
        summed = h1_ref[...] + (acc_ref[...] + bo_ref[...][None, :])
        unit, inv = norm_stats(summed)
        out_ref[...] = jnp.where(valid, unit * g2_ref[...][None, :] + b2_ref[...][None, :], 0.0)
        e = jnp.where(valid, cot_ref[...], 0.0)
        grad = norm_back(unit, inv, g2_ref[...][None, :], e)
        gs2_ref[...] = grad
        small_ref[...] = jnp.concatenate(
            [
                jnp.sum(e * unit, axis=0, keepdims=True),
                jnp.sum(e, axis=0, keepdims=True),
                jnp.sum(grad, axis=0, keepdims=True),
                jnp.zeros((5, e.shape[1]), f32),
            ],
            axis=0,
        )


def ffn_forward(lens, h1, wi, bi, wo, bo, cot, g2, b2):
    slots, width = h1.shape
    inner = wi.shape[1]
    const = lambda *dims: pl.BlockSpec(dims, lambda j: (0,) * len(dims))
    return pl.pallas_call(
        forward_kernel,
        grid=(inner // width,),
        in_specs=[
            smem(), const(slots, width),
            pl.BlockSpec((width, width), lambda j: (0, j)), pl.BlockSpec((1, width), lambda j: (0, j)),
            pl.BlockSpec((width, width), lambda j: (j, 0)), const(width),
            const(slots, width), const(width), const(width),
        ],
        out_specs=[
            pl.BlockSpec((slots, width), lambda j: (0, j)),
            const(slots, width), const(slots, width), const(8, width),
        ],
        out_shape=[shape(slots, inner), shape(slots, width), shape(slots, width), shape(8, width)],
        scratch_shapes=[pltpu.VMEM((slots, width), f32)],
        compiler_params=params(),
        name="ffn_forward",
    )(lens, h1, wi, bi, wo, bo, cot, g2, b2)


def put_strips(ref, block):
    for s in range(block.shape[1] // LANES):
        ref[s] = block[:, s * LANES : (s + 1) * LANES]


def backward_kernel(
    h1_ref, gs2_ref, pre_ref, wi_ref, wo_ref, u1_ref, inv1_ref, g1_ref,
    dwo_ref, dwi_ref, gs1_ref, dbi_ref, small_ref,
    acc_ref,
):
    step = pl.program_id(0)
    gs2 = gs2_ref[...]
    pre = pre_ref[...]
    phi_big = 0.5 * (1.0 + lax.erf(pre * ROOT_HALF))
    act = pre * phi_big
    slope = phi_big + pre * (INV_ROOT_TAU * jnp.exp(-0.5 * pre * pre))
    gpre = mm_t(gs2, wo_ref[...]) * slope
    put_strips(dwo_ref, t_mm(act, gs2))
    put_strips(dwi_ref, t_mm(h1_ref[...], gpre))
    dbi_ref[...] = jnp.sum(gpre, axis=0, keepdims=True)
    part = mm_t(gpre, wi_ref[...])

    @pl.when(step == 0)
    def _():
        acc_ref[...] = gs2 + part

    @pl.when(step > 0)
    def _():
        acc_ref[...] += part

    @pl.when(step == pl.num_programs(0) - 1)
    def _():
        e = acc_ref[...]
        unit = u1_ref[...]
        grad = norm_back(unit, inv1_ref[...], g1_ref[...][None, :], e)
        gs1_ref[...] = grad
        small_ref[...] = jnp.concatenate(
            [
                jnp.sum(e * unit, axis=0, keepdims=True),
                jnp.sum(e, axis=0, keepdims=True),
                jnp.sum(grad, axis=0, keepdims=True),
                jnp.zeros((5, e.shape[1]), f32),
            ],
            axis=0,
        )


def ffn_backward(h1, gs2, pre, wi, wo, u1, inv1, g1):
    slots, width = h1.shape
    inner = wi.shape[1]
    strips = width // LANES
    const = lambda *dims: pl.BlockSpec(dims, lambda j: (0,) * len(dims))
    return pl.pallas_call(
        backward_kernel,
        grid=(inner // width,),
        in_specs=[
            const(slots, width), const(slots, width),
            pl.BlockSpec((slots, width), lambda j: (0, j)),
            pl.BlockSpec((width, width), lambda j: (0, j)),
            pl.BlockSpec((width, width), lambda j: (j, 0)),
            const(slots, width), const(slots, 1), const(width),
        ],
        out_specs=[
            pl.BlockSpec((strips, width, LANES), lambda j: (j, 0, 0)),
            pl.BlockSpec((strips, width, LANES), lambda j: (j, 0, 0)),
            const(slots, width),
            pl.BlockSpec((1, width), lambda j: (0, j)),
            const(8, width),
        ],
        out_shape=[
            shape(inner // LANES, width, LANES), shape(inner // LANES, width, LANES),
            shape(slots, width), shape(1, inner), shape(8, width),
        ],
        scratch_shapes=[pltpu.VMEM((slots, width), f32)],
        compiler_params=params(),
        name="ffn_backward",
    )(h1, gs2, pre, wi, wo, u1, inv1, g1)


def near_back_kernel(
    lens_ref, gs1_ref, wo_ref, near_ref, q_ref, kl_ref, b_ref,
    gctx_ref, gq_ref, gb_ref, gkl_ref, rim_ref,
):
    count = seg_ends(lens_ref, lens_ref.shape[1])[-1]
    gctx_ref[...] = mm_t(gs1_ref[...], wo_ref[...])
    rim_ref[...] = rims_of(gctx_ref[...], count)
    mask = head_mask(QUAD)
    ones = jnp.where(mask, 1.0, 0.0)
    for g in range(HEADS * DH // QUAD):
        cols = slice(g * QUAD, (g + 1) * QUAD)
        gctx = gctx_ref[:, cols]
        near = near_ref[:, cols]
        gblend = fold(t_mm(gctx, near), mask)
        gb_ref[2 * g] = gblend[:, :LANES]
        gb_ref[2 * g + 1] = gblend[:, LANES:]
        gnear = mm(gctx, spread(pair_rows(b_ref, g, slice(0, DH)), mask))
        gscore = near * (gnear - mm(near * gnear, ones)) * SCALE
        gq_ref[:, cols] = mm(gscore, spread(kl_ref[:, cols], mask))
        gkl_ref[:, cols] = fold(t_mm(gscore, q_ref[:, cols]), mask)


def near_back(lens, gs1, wo, near, q, kl, b):
    slots, width = gs1.shape
    return pl.pallas_call(
        near_back_kernel,
        in_specs=[smem()] + [whole()] * 6,
        out_specs=[whole()] * 5,
        out_shape=[
            shape(slots, width), shape(slots, width), shape(PAIRS, DH, LANES),
            shape(DH, width), shape(2 * RIM, width),
        ],
        compiler_params=params(),
        name="near_back",
    )(lens, gs1, wo, near, q, kl, b)


def far_back_kernel(
    lens_ref, k_ref, v_ref, p_ref, m_ref, b_ref, c_ref, ql_ref, gkl_ref, gl_ref,
    gk_ref, gv_ref, ret_ref,
):
    mask = head_mask(QUAD)
    n, _, segs, _ = ret_ref.shape
    for g in range(HEADS * DH // QUAD):
        cols = slice(g * QUAD, (g + 1) * QUAD)
        top = pair_rows(b_ref, g, slice(DH, DH + 1))
        total = pair_rows(b_ref, g, slice(DH + 1, DH + 2))
        prob = p_ref[:, cols] * (jnp.exp(m_ref[:, cols] - top) / total)
        gmixed = spread(pair_rows(c_ref, g, slice(0, DH)), mask)
        dots = pair_rows(c_ref, g, slice(DH, DH + 1))
        gscore = prob * (mm(v_ref[:, cols], gmixed) - dots) * SCALE
        gk_ref[:, cols] = mm(gscore, spread(ql_ref[:, cols], mask))
        gv_ref[:, cols] = mm_t(prob, gmixed)
        gql = fold(t_mm(gscore, k_ref[:, cols]), mask) + gl_ref[0, :, cols]
        gkl = gkl_ref[:, cols] + gl_ref[1, :, cols]
        for s in range(n):
            rows = slice(s * segs, (s + 1) * segs)
            ret_ref[s, 0, :, cols] = gql[rows]
            ret_ref[s, 1, :, cols] = gkl[rows]


def far_back(n, lens, k, v, p, m, b, c, ql, gkl, gl):
    slots, width = k.shape
    segs = lens.shape[1]
    return pl.pallas_call(
        far_back_kernel,
        in_specs=[smem()] + [whole()] * 9,
        out_specs=[whole()] * 3,
        out_shape=[shape(slots, width), shape(slots, width), shape(n, 2, segs, width)],
        compiler_params=params(),
        name="far_back",
    )(lens, k, v, p, m, b, c, ql, gkl, gl)


def conv_back_kernel(
    lens_ref, v_ref, left_ref, right_ref, gctx_ref, gleft_ref, gright_ref, taps_ref, ctx_ref, gs1_ref,
    gv_ref, gtaps_ref, dwo_ref,
    ext_ref, scr_ref,
):
    slots = v_ref.shape[0]
    count = seg_ends(lens_ref, lens_ref.shape[1])[-1]
    put_strips(dwo_ref, t_mm(ctx_ref[...], gs1_ref[...]))
    fill_extended(ext_ref, gctx_ref[...], gleft_ref[...], gright_ref[...], count)
    conv_into(gv_ref, ext_ref, taps_ref, slots, True, False)
    fill_extended(ext_ref, v_ref[...], left_ref[...], right_ref[...], count)
    taps_grad_into(scr_ref, gctx_ref, ext_ref, slots)
    rows = jnp.concatenate(
        [jnp.sum(scr_ref[c], axis=0, keepdims=True) for c in range(CONV)] + [jnp.zeros((7, v_ref.shape[1]), f32)],
        axis=0,
    )
    row = lax.broadcasted_iota(jnp.int32, (v_ref.shape[1], LANES), 0) >> 6
    col = lax.broadcasted_iota(jnp.int32, (v_ref.shape[1], LANES), 1)
    gtaps_ref[...] = mm(rows, jnp.where(row == col, 1.0, 0.0), TOP)


def conv_back(lens, v, left, right, gctx, gleft, gright, taps, ctx, gs1):
    slots, width = v.shape
    return pl.pallas_call(
        conv_back_kernel,
        in_specs=[smem()] + [whole()] * 9,
        out_specs=[whole()] * 3,
        out_shape=[shape(slots, width), shape(40, LANES), shape(width // LANES, width, LANES)],
        scratch_shapes=[pltpu.VMEM((slots + 40, width), f32), pltpu.VMEM((CONV, 8, width), f32)],
        compiler_params=params(),
        name="conv_back",
    )(lens, v, left, right, gctx, gleft, gright, taps, ctx, gs1)


def project_back_kernel(
    lens_ref, x_ref, gs1_ref, gqn_ref, gkf_ref, gvc_ref, gvf_ref, own_ref, wq_ref, wk_ref, wv_ref,
    ig_ref, dq_ref, dk_ref, dv_ref, small_ref,
    gq_ref, gk_ref, gv_ref,
):
    @pl.when(pl.program_id(0) == 0)
    def _():
        slots = gqn_ref.shape[0]
        segs = own_ref.shape[1]
        ends = seg_ends(lens_ref, segs)
        member = member_rows(ends, slots)
        inv = inverse_lens(lens_ref, segs)
        gq = gqn_ref[...] + t_mm(member, own_ref[0] * inv)
        gk = gkf_ref[...] + t_mm(member, own_ref[1] * inv)
        gv = jnp.where(valid_rows(ends[-1], slots), gvc_ref[...] + gvf_ref[...], 0.0)
        gq_ref[...] = gq
        gk_ref[...] = gk
        gv_ref[...] = gv
        small_ref[...] = jnp.concatenate(
            [
                jnp.sum(gq, axis=0, keepdims=True),
                jnp.sum(gv, axis=0, keepdims=True),
                jnp.zeros((6, gq.shape[1]), f32),
            ],
            axis=0,
        )

    x = x_ref[...]
    put_strips(dq_ref, t_mm(x, gq_ref[...]))
    put_strips(dk_ref, t_mm(x, gk_ref[...]))
    put_strips(dv_ref, t_mm(x, gv_ref[...]))
    ig_ref[...] = (
        gs1_ref[...]
        + mm_t(gq_ref[...], wq_ref[...])
        + mm_t(gk_ref[...], wk_ref[...])
        + mm_t(gv_ref[...], wv_ref[...])
    )


def project_back(lens, x, gs1, gqn, gkf, gvc, gvf, own, wq, wk, wv):
    slots, width = x.shape
    col = 256
    strips = width // LANES
    const = lambda *dims: pl.BlockSpec(dims, lambda i: (0,) * len(dims))
    part = pl.BlockSpec((slots, col), lambda i: (0, i))
    wspec = pl.BlockSpec((col, width), lambda i: (i, 0))
    dspec = pl.BlockSpec((strips, col, LANES), lambda i: (0, i, 0))
    return pl.pallas_call(
        project_back_kernel,
        grid=(width // col,),
        in_specs=[smem(), part, part] + [const(slots, width)] * 4 + [const(*own.shape), wspec, wspec, wspec],
        out_specs=[part, dspec, dspec, dspec, const(8, width)],
        out_shape=[shape(slots, width)] + [shape(strips, width, LANES)] * 3 + [shape(8, width)],
        scratch_shapes=[pltpu.VMEM((slots, width), f32)] * 3,
        compiler_params=params(),
        name="project_back",
    )(lens, x, gs1, gqn, gkf, gvc, gvf, own, wq, wk, wv)


def sum_plain(parts):
    sizes = [part.size for part in parts]
    shapes = [part.shape for part in parts]
    devices = lax.axis_size(("seq", "dp"))
    flat = jnp.concatenate([part.reshape(-1) for part in parts])
    flat = jnp.pad(flat, (0, -flat.shape[0] % devices))
    own = lax.psum_scatter(flat, ("seq", "dp"), scatter_dimension=0, tiled=True)
    flat = lax.all_gather(own, ("seq", "dp"), axis=0, tiled=True)
    out = []
    at = 0
    for size, dims in zip(sizes, shapes):
        out.append(flat[at : at + size].reshape(dims))
        at += size
    return out


STRIP = 768
HALF = STRIP // 2
PART = HALF // 2
Z_ROWS = PART // 4
OWN = Z_ROWS // 2
STAGES = 13
SMALL_STEPS = 5


def pack_small(sb_ref, small0, small1, small2, inner_bias, taps):
    at = 0
    for ref, count in ((small0, 2), (small1, 3), (small2, 3), (inner_bias, 1)):
        for r in range(count):
            for j in range(ref.shape[1] // LANES):
                sb_ref[0, at : at + 1, :] = ref[r : r + 1, j * LANES : (j + 1) * LANES]
                at += 1
    sb_ref[0, at : at + 40, :] = taps[...]


SMALL_ROWS = 8 * 6 + 24 + 40


def unpack_small(s_ref, outs):
    at = 0
    for ref in outs[:-1]:
        for j in range(ref.shape[0] // LANES):
            ref[pl.ds(j * LANES, LANES)] = s_ref[at, :]
            at += 1
    outs[-1][...] = s_ref[at : at + CONV, :HEADS]


def reduce_kernel(spans, lag, *refs):
    count = len(spans)
    grads = refs[:count]
    smalls = refs[count : count + 5]
    o_ref, so_ref, acc, lc, l1, lz, l3, sb, sl = refs[count + 5 : count + 14]
    (
        local, out_local, cs, cr, s1, r1, zs, zr, s3, r3, s4, r4, gs, gr, s5, r5, es, er, ss, sr,
    ) = refs[count + 14 :]
    chunks = spans[-1][1]
    seq = lax.axis_index("seq")
    dp = lax.axis_index("dp")
    z = seq // 2
    c = lax.rem(seq, 2)
    y = dp // 2
    x = lax.rem(dp, 2)
    zb = 3 - z
    place = lambda z_, c_, y_, x_: (z_ * 2 + c_, y_ * 2 + x_)
    by_core = place(z, 1 - c, y, x)
    by_x = place(z, c, y, 1 - x)
    by_y = place(z, c, 1 - y, x)
    right = place(lax.rem(z + 1, 4), c, y, x)
    left = place(lax.rem(z + 3, 4), c, y, x)
    opposite = place(lax.rem(z + 2, 4), c, y, x)
    near_z = place(z + 1 - 2 * lax.rem(z, 2), c, y, x)
    barrier = pltpu.get_barrier_semaphore()
    for target in (by_core, by_x, by_y, right, left, opposite):
        pl.semaphore_signal(barrier, inc=1, device_id=target, device_id_type=MESH)
    pl.semaphore_wait(barrier, 6)

    def remote(src, dst, send, recv, target):
        return pltpu.make_async_remote_copy(src, dst, send, recv, device_id=target, device_id_type=MESH)

    aligned = lambda at: pl.multiple_of(at, 8)
    a1 = x * PART
    b1 = HALF + y * PART
    firsts = ((0, a1, (1 - x) * PART, by_x), (1, b1, HALF + (1 - y) * PART, by_y))
    starts = (a1, b1)
    az = a1 + z * Z_ROWS
    bz = b1 + z * Z_ROWS
    thirds = (
        (0, az + y * OWN, az + (1 - y) * OWN, by_y),
        (1, bz + x * OWN, bz + (1 - x) * OWN, by_x),
    )

    def rows(ref, k, at, size):
        return ref.at[k, pl.ds(aligned(at), size)]

    def core_out(k):
        for g, (lo, hi) in zip(grads, spans):
            half = hi - lo

            @pl.when((k >= lo) & (k < hi))
            def _(g=g, lo=lo, half=half):
                pltpu.make_async_copy(g.at[c * half + (k - lo)], acc.at[k], local.at[k]).start()
                remote(g.at[(1 - c) * half + (k - lo)], lc.at[k], cs.at[k], cr.at[k], by_core).start()

    def first(k, j):
        _, _, other, target = firsts[j]
        return remote(rows(acc, k, other, PART), l1.at[k, j], s1.at[k, j], r1.at[k, j], target)

    def first_out(k):
        pltpu.make_async_copy(grads[0].at[0], acc.at[k], local.at[k]).wait()
        remote(grads[0].at[0], lc.at[k], cs.at[k], cr.at[k], by_core).wait_recv()
        acc[k] += lc[k]
        for j in range(2):
            first(k, j).start()

    def z_copy(k, j, way, step, block):
        target = right if way == 0 else left
        return remote(
            rows(acc, k, starts[j] + block * Z_ROWS, Z_ROWS), lz.at[k, way, j, step],
            zs.at[k, way, step, j], zr.at[k, way, step, j], target,
        )

    def z_out(k, step):
        if step == 0:
            for j, mine, _, _ in firsts:
                first(k, j).wait_recv()
                acc[k, pl.ds(aligned(mine), PART)] += l1[k, j]
        for way, at in ((0, z), (1, zb)):
            block = 3 - step + z if way == 0 else step - zb
            if step > 0:

                @pl.when((at > 0) & (at <= step))
                def _(way=way, block=block):
                    for j in range(2):
                        z_copy(k, j, way, step - 1, 0).wait_recv()
                    for j in range(2):
                        acc[k, pl.ds(aligned(starts[j] + block * Z_ROWS), Z_ROWS)] += lz[k, way, j, step - 1]

            if step < 3:

                @pl.when((at <= step) & (at < 3))
                def _(way=way, block=block):
                    for j in range(2):
                        z_copy(k, j, way, step, block).start()

    def third(k, j):
        _, _, other, target = thirds[j]
        return remote(rows(acc, k, other, OWN), l3.at[k, j], s3.at[k, j], r3.at[k, j], target)

    def third_out(k):
        z_out(k, 3)
        for j in range(2):
            third(k, j).start()

    def back_third(k, j):
        _, mine, _, target = thirds[j]
        return remote(rows(acc, k, mine, OWN), rows(o_ref.at[c], k, mine, OWN), s4.at[k, j], r4.at[k, j], target)

    def keep(k, j):
        mine = thirds[j][1]
        return pltpu.make_async_copy(rows(acc, k, mine, OWN), rows(o_ref.at[c], k, mine, OWN), out_local.at[k, j])

    def back_third_out(k):
        for j, mine, _, _ in thirds:
            third(k, j).wait_recv()
            acc[k, pl.ds(aligned(mine), OWN)] += l3[k, j]
        for j in range(2):
            back_third(k, j).start()
            keep(k, j).start()

    def back_z(k, j, way, step, block):
        target = right if way == 0 else left
        part = rows(o_ref.at[c], k, starts[j] + block * Z_ROWS, Z_ROWS)
        return remote(part, part, gs.at[k, way, step, j], gr.at[k, way, step, j], target)

    def back_z_out(k, step):
        if step == 0:
            for j in range(2):
                keep(k, j).wait()
                back_third(k, j).wait_recv()
        for way, at in ((0, z), (1, zb)):
            block = z - step if way == 0 else z + step
            if step > 0:

                @pl.when(at >= step)
                def _(way=way):
                    for j in range(2):
                        back_z(k, j, way, step - 1, 0).wait_recv()

            if step < 3:

                @pl.when((at >= step) & (at < 3))
                def _(way=way, block=block):
                    for j in range(2):
                        back_z(k, j, way, step, block).start()

    def back_first(k, j):
        _, mine, _, target = firsts[j]
        part = rows(o_ref.at[c], k, mine, PART)
        return remote(part, part, s5.at[k, j], r5.at[k, j], target)

    def back_first_out(k):
        back_z_out(k, 3)
        for j in range(2):
            back_first(k, j).start()

    def back_core(k):
        part = o_ref.at[c, k]
        return remote(part, part, es.at[k], er.at[k], by_core)

    def back_core_out(k):
        for j in range(2):
            back_first(k, j).wait_recv()
        back_core(k).start()

    def finish(k):
        back_core(k).wait()
        remote(grads[0].at[0], lc.at[k], cs.at[k], cr.at[k], by_core).wait_send()
        for j in range(2):
            first(k, j).wait_send()
            third(k, j).wait_send()
            back_third(k, j).wait_send()
            back_first(k, j).wait_send()
        for step in range(3):
            for way, at in ((0, z), (1, zb)):

                @pl.when((at <= step) & (at < 3))
                def _(way=way, step=step):
                    for j in range(2):
                        z_copy(k, j, way, step, 0).wait_send()

                @pl.when((at >= step) & (at < 3))
                def _(way=way, step=step):
                    for j in range(2):
                        back_z(k, j, way, step, 0).wait_send()

    stages = [
        core_out, first_out, partial(z_out, step=0), partial(z_out, step=1), partial(z_out, step=2), third_out,
        back_third_out, partial(back_z_out, step=0), partial(back_z_out, step=1), partial(back_z_out, step=2),
        back_first_out, back_core_out, finish,
    ]

    partners = (by_core, by_x, by_y, near_z, opposite)

    def small(i):
        return remote(sb.at[i], sl.at[i], ss.at[i], sr.at[i], partners[i])

    pack_small(sb, *smalls)
    small(0).start()

    def tick(t, carry):
        for i in range(1, SMALL_STEPS + 1):

            @pl.when(t == 2 * i)
            def _(i=i):
                small(i - 1).wait_recv()
                sb[i] = sb[i - 1] + sl[i - 1]
                if i < SMALL_STEPS:
                    small(i).start()

        for stage, run in reversed(list(enumerate(stages))):
            k = t - lag[stage]

            @pl.when((k >= 0) & (k < chunks))
            def _(run=run, k=k):
                run(k)

        return carry

    lax.fori_loop(0, chunks + lag[-1], tick, 0)
    for i in range(SMALL_STEPS):
        small(i).wait_send()
    so_ref[...] = sb[SMALL_STEPS]


LAG = tuple(range(0, 2 * STAGES, 2))


def reduce_grads(grads, smalls):
    spans = []
    at = 0
    for g in grads:
        spans.append((at, at + g.shape[0] // 2))
        at += g.shape[0] // 2
    dma = pltpu.SemaphoreType.DMA
    vm = lambda *dims: pltpu.VMEM(dims, f32)
    return pl.pallas_call(
        partial(reduce_kernel, tuple(spans), LAG),
        in_specs=[pl.BlockSpec(memory_space=pl.ANY)] * len(grads) + [whole()] * 5,
        out_specs=[pl.BlockSpec(memory_space=pl.ANY), whole()],
        out_shape=[shape(2, at, STRIP, LANES), shape(SMALL_ROWS, LANES)],
        scratch_shapes=[
            vm(at, STRIP, LANES), vm(at, STRIP, LANES), vm(at, 2, PART, LANES), vm(at, 2, 2, 3, Z_ROWS, LANES),
            vm(at, 2, OWN, LANES), vm(SMALL_STEPS + 1, SMALL_ROWS, LANES), vm(SMALL_STEPS, SMALL_ROWS, LANES),
            dma((at,)), dma((at, 2)), dma((at,)), dma((at,)), dma((at, 2)), dma((at, 2)),
            dma((at, 2, 3, 2)), dma((at, 2, 3, 2)), dma((at, 2)), dma((at, 2)), dma((at, 2)), dma((at, 2)),
            dma((at, 2, 3, 2)), dma((at, 2, 3, 2)), dma((at, 2)), dma((at, 2)), dma((at,)), dma((at,)),
            dma((SMALL_STEPS,)), dma((SMALL_STEPS,)),
        ],
        compiler_params=params(collective_id=5, has_side_effects=True),
        name="reduce_grads",
    )(*grads, *smalls)


def sum_on_block(grads, smalls, shapes):
    summed, packed = reduce_grads(grads, smalls)
    spans = []
    at = 0
    for g in grads:
        spans.append((at, at + g.shape[0] // 2))
        at += g.shape[0] // 2
    return place_strips(summed, packed, spans, shapes)


def unstrip(strips):
    count, rows, _ = strips.shape
    return strips.transpose(1, 0, 2).reshape(rows, count * LANES)


def unstrip_tall(strips, across):
    count, rows, _ = strips.shape
    down = count // across
    return strips.reshape(down, across, rows, LANES).transpose(0, 2, 1, 3).reshape(down * rows, across * LANES)


PLACE_SLOTS = 24


def place_strips_kernel(spans, s_ref, small_ref, *refs):
    outs = refs[: len(spans)]
    smalls = refs[len(spans) : -3]
    buf, in_sem, out_sem = refs[-3:]
    moves = []
    for out, (lo, hi) in zip(outs, spans):
        across = out.shape[1] // LANES
        for c in range(2):
            for k in range(lo, hi):
                at = c * (hi - lo) + k - lo
                rows = pl.ds(at // across * STRIP, STRIP)
                cols = pl.ds(at % across * LANES, LANES)
                slot = len(moves) % PLACE_SLOTS
                moves.append((
                    pltpu.make_async_copy(s_ref.at[c, k], buf.at[slot], in_sem.at[slot]),
                    pltpu.make_async_copy(buf.at[slot], out.at[rows, cols], out_sem.at[slot]),
                ))
    ahead = PLACE_SLOTS // 2
    for i in range(len(moves) + ahead):
        if i < len(moves):
            if i >= PLACE_SLOTS:
                moves[i - PLACE_SLOTS][1].wait()
            moves[i][0].start()
        if i >= ahead:
            moves[i - ahead][0].wait()
            moves[i - ahead][1].start()
    unpack_small(small_ref, smalls)
    for _, out in moves[-PLACE_SLOTS:]:
        out.wait()


def place_strips(summed, packed, spans, shapes):
    anywhere = pl.BlockSpec(memory_space=pl.ANY)
    dma = pltpu.SemaphoreType.DMA
    width = shapes[0][1]
    return pl.pallas_call(
        partial(place_strips_kernel, spans),
        in_specs=[anywhere, whole()],
        out_specs=[anywhere] * len(shapes) + [whole()] * 10,
        out_shape=[shape(*dims) for dims in shapes] + [shape(width)] * 8 + [shape(shapes[0][0]), shape(CONV, HEADS)],
        scratch_shapes=[pltpu.VMEM((PLACE_SLOTS, STRIP, LANES), f32), dma((PLACE_SLOTS,)), dma((PLACE_SLOTS,))],
        compiler_params=params(),
        name="place_strips",
    )(summed, packed)


def per_device(
    tokens, segment_lens, query_weight, query_bias, key_weight, value_weight, value_bias, conv_taps,
    output_weight, output_bias, first_gain, first_bias, inner_weight, inner_bias, outer_weight, outer_bias,
    second_gain, second_bias, cotangent,
):
    n = lax.axis_size("seq")
    _, slots, width = tokens.shape
    x = tokens.reshape(slots, width)
    cot = cotangent.reshape(slots, width)
    lens = segment_lens
    taps = jnp.repeat(conv_taps, DH, axis=1)

    q, k, v, land, rim = project(lens, x, query_weight, key_weight, value_weight, query_bias, value_bias)
    lands, left, right = land_exchange(n, land, rim)
    ql = lands[:, 0].reshape(DH, width)
    kl = lands[:, 1].reshape(DH, width)
    parts, raised, tops = far_local(lens, k, v, ql)
    b, *saved = far_exchange(n, parts, ql, kl)
    near, ctx, h1, u1, inv1 = attend(
        lens, q, v, kl, b, left, right, taps, x, output_weight, output_bias, first_gain, first_bias
    )
    pre, layer_out, gs2, small2 = ffn_forward(
        lens, h1, inner_weight, inner_bias.reshape(1, -1), outer_weight, outer_bias, cot, second_gain, second_bias
    )
    d_outer, d_inner, gs1, d_inner_bias, small1 = ffn_backward(
        h1, gs2, pre, inner_weight, outer_weight, u1, inv1, first_gain
    )
    gctx, gqn, gblend, gkl, grim = near_back(lens, gs1, output_weight, near, q, kl, b)
    c, gleft, gright, gl = blend_exchange(n, gblend, grim, ql, kl, saved)
    gkf, gvf, back = far_back(n, lens, k, v, raised, tops, b, c, ql, gkl, gl)
    own = land_return(n, back)
    gvc, gtaps, d_output = conv_back(lens, v, left, right, gctx, gleft, gright, taps, ctx, gs1)
    input_grad, d_query, d_key, d_value, small0 = project_back(
        lens, x, gs1, gqn, gkf, gvc, gvf, own, query_weight, key_weight, value_weight
    )
    grads = [d_outer, d_inner, d_output, d_query, d_key, d_value]
    smalls = [small0, small1, small2, d_inner_bias, gtaps]
    weights = [outer_weight, inner_weight, output_weight, query_weight, key_weight, value_weight]
    if n == 8 and lax.axis_size("dp") == 4:
        sums = sum_on_block(grads, smalls, [w.shape for w in weights])
    else:
        sums = sum_plain(grads + smalls)
        small = sums[6:]
        sums = (
            [unstrip_tall(sums[0], width // LANES)] + [unstrip(s) for s in sums[1:6]]
            + [small[0][0], small[0][1], *small[1][:3], *small[2][:3], small[3][0], small[4][:CONV, :HEADS]]
        )
    d_outer, d_inner, d_output, d_query, d_key, d_value, *vectors = sums
    d_query_bias, d_value_bias, d_first_gain, d_first_bias, d_output_bias = vectors[:5]
    d_second_gain, d_second_bias, d_outer_bias, d_inner_bias, d_taps = vectors[5:]
    return (
        layer_out.reshape(tokens.shape), input_grad.reshape(tokens.shape),
        d_query, d_query_bias, d_key, d_value, d_value_bias, d_taps,
        d_output, d_output_bias, d_first_gain, d_first_bias,
        d_inner, d_inner_bias, d_outer, d_outer_bias, d_second_gain, d_second_bias,
    )


def solution(mesh):
    block = P("dp", "seq", None)
    return jax.shard_map(
        per_device,
        mesh=mesh,
        in_specs=(block, P("dp", "seq")) + (P(),) * 16 + (block,),
        out_specs=(block, block) + (P(),) * 16,
        check_vma=False,
    )
```

time: 1480 us -> 498 us (0.34)
  waiting for transfers between devices: 699 us -> 0 us
  Pallas kernels: 0 us -> 485 us
  matrix products: 310 us -> 0 us
  local copies, waits for them, and re-layouts: 170 us -> 4.89 us
  blocking collectives: 144 us -> 0 us
  other arithmetic: 118 us -> 0 us
  between operations: 20.7 us -> 1.23 us
    pallas_call x0 -> x15, Pallas kernels: none -> 485 us  [the longest x1 229 us: reduce_grads(): pl.pallas_call(partial(reduce_kernel, tuple(spans), LAG), in_specs=[pl.Bl...]
    unnamed x12 -> x0, waiting for transfers between devices: 433 us -> none
    dot_general x112 -> x0, matrix products: 310 us -> none  [the longest x18 201 us: matmul(): jnp.dot(left, right, precision=highest, preferred_element_type=jnp.float32)]
    all_gather x6 -> x0, waiting for transfers between devices: 252 us -> none  [the longest x1 80.9 us: per_device(): lax.all_gather(weight_parts[4], ('seq', 'dp'), axis=0, tiled=True)]
    unnamed x2 -> x0, blocking collectives: 80.7 us -> none
    reshape x22 -> x1, local copies, waits for them, and re-layouts: 73.6 us -> 0.77 us  [per_device(): taps = jnp.repeat(conv_taps, DH, axis=1)]
    reduce_sum x20 -> x0, other arithmetic: 32.3 us -> none  [the longest x1 14.6 us: conv_part(): feature_taps[offset] * extended[:, offset:offset + block_len]]
    all_gather x2 -> x0, blocking collectives: 31.8 us -> none  [the longest x1 16.3 us: per_device(): lax.all_gather(query_mean, 'seq', axis=1, tiled=True)]
  transfers between devices with their start and end apart: 15 -> 0, of which waited for: 6 -> 0; matrix products, arithmetic and copies ran while one was open for 21% -> 0% of each run, Pallas kernels for 0% -> 0%
where the time goes in v1:
time: 498 us; the launch traced here: 491 us
  Pallas kernels  485 us (97%)
    pallas_call x1, Pallas kernels, reduce_grads(): pl.pallas_call(partial(reduce_kernel, tuple(spans), LAG), in_specs=[pl.Bl...  229 us
    pallas_call x1, Pallas kernels, ffn_backward(): pl.pallas_call(backward_kernel, grid=(inner // width,), in_specs=[const(s...  41 us
    pallas_call x1, Pallas kernels, ffn_forward(): pl.pallas_call(forward_kernel, grid=(inner // width,), in_specs=[smem(),...  25.1 us
    pallas_call x1, Pallas kernels, conv_back(): pl.pallas_call(conv_back_kernel, in_specs=[smem()] + [whole()] * 9, out_s...  23.3 us
    pallas_call x1, Pallas kernels, blend_exchange(): pl.pallas_call(partial(blend_exchange_kernel, n), in_specs=[whole()] * 10...  22 us
    pallas_call x1, Pallas kernels, attend(): pl.pallas_call(attend_kernel, in_specs=[smem()] + [whole()] * 12, out_spe...  21.8 us
    pallas_call x1, Pallas kernels, place_strips(): pl.pallas_call(partial(place_strips_kernel, spans), in_specs=[anywhere, w...  20.9 us
    pallas_call x1, Pallas kernels, far_exchange(): pl.pallas_call(partial(far_exchange_kernel, n), in_specs=[whole()] * 3, o...  19.7 us

profile of v1, /device:TPU:0, one launch (start us, length us, event | category | flops | bytes accessed | tf_op | source)
XLA Modules:
  0.0 490.7 jit_solution(5674363020053021699)
XLA Ops:
  0.7 0.8 copy.39
  1.4 0.1 broadcast_in_dim.3
  1.6 0.8 reshape.55.taps_ref
  2.3 11.0 %project.1 = (f32[512,768]{1,0:T(8,128)}, f32[512,768]{1,0:T(8,128)}, f32[512,768]{1,0:T(8,128)}, f32[2,8,768]{2,1,0:T(8,128)}, f32[32,768]{1,0:T(8,128)}) custom-call(s32[1,8]{1,0:T(1,128)} %lens_ref.15, f32[512,768]{1,0:T(8,128)} %bitcast.9, f32[768,768]{1,0:T(8,128)} %wq_ref.3, f32[768,768]{1,0:T(8,128)} %wk_ref.3, f32[768,768]{1,0:T(8,128)} %wv_ref.3, ...), custom_call_target="tpu_custom_call" | custom-call | tf_op jit(solution)/shard_map/project/pallas_call | solution.py:216
  13.4 14.3 %land_exchange.1 = (f32[8,2,8,768]{3,2,1,0:T(8,128)}, f32[16,768]{1,0:T(8,128)}, f32[16,768]{1,0:T(8,128)}) custom-call(f32[2,8,768]{2,1,0:T(8,128)} %get-tuple-element.90.mine_ref, f32[32,768]{1,0:T(8,128)} %get-tuple-element.91.rim_ref), custom_call_target="tpu_custom_call" | custom-call | tf_op jit(solution)/shard_map/land_exchange/pallas_call | solution.py:312
  27.7 1.8 slice_bitcast_fusion
  29.5 5.5 %far_local.1 = (f32[6,72,128]{2,1,0:T(8,128)}, f32[512,768]{1,0:T(8,128)}, f32[1,768]{1,0:T(1,128)}) custom-call(s32[1,8]{1,0:T(1,128)} %lens_ref.15, f32[512,768]{1,0:T(8,128)} %get-tuple-element.93.k_ref, f32[512,768]{1,0:T(8,128)} %get-tuple-element.89.v_ref, f32[64,768]{1,0:T(8,128)} %get-tuple-element.194.ql_ref), custom_call_target="tpu_custom_call" | custom-call | tf_op jit(solution)/shard_map/far_local/pallas_call | solution.py:603
  35.1 19.7 %far_exchange.1 = (f32[6,72,128]{2,1,0:T(8,128)}, f32[128,128]{1,0:T(8,128)}, f32[7,128,128]{2,1,0:T(8,128)}, f32[6,128,128]{2,1,0:T(8,128)}, f32[6,128,128]{2,1...) custom-call(f32[6,72,128]{2,1,0:T(8,128)} %get-tuple-element.94.f_ref, f32[64,768]{1,0:T(8,128)} %get-tuple-element.194.ql_ref, ...), custom_call_target="tpu_custom_call" | custom-call | tf_op jit(solution)/shard_map/far_exchange/pallas_call | solution.py:425
  54.7 21.8 %attend.1 = (f32[512,768]{1,0:T(8,128)}, f32[512,768]{1,0:T(8,128)}, f32[512,768]{1,0:T(8,128)}, f32[512,768]{1,0:T(8,128)}, f32[512,1]{1,0:T(8,128)}) custom-call(s32[1,8]{1,0:T(1,128)} %lens_ref.15, f32[512,768]{1,0:T(8,128)} %get-tuple-element.88.q_ref, f32[512,768]{1,0:T(8,128)} %get-tuple-element.89.v_ref, f32[64,768]{1,0:T(8,128)} %get-tuple-element.195.kl_ref, ...), custom_call_target="tpu_custom_call" | custom-call | tf_op jit(solution)/shard_map/attend/pallas_call | solution.py:664
  76.5 25.1 %ffn_forward.1 = (f32[512,3072]{1,0:T(8,128)}, f32[512,768]{1,0:T(8,128)}, f32[512,768]{1,0:T(8,128)}, f32[8,768]{1,0:T(8,128)}) custom-call(s32[1,8]{1,0:T(1,128)} %lens_ref.15, f32[512,768]{1,0:T(8,128)} %get-tuple-element.98.h1_ref, f32[768,3072]{1,0:T(8,128)} %wi_ref.3, f32[1,3072]{1,0:T(1,128)} %bitcast.13, f32[3072,768]{1,0:T(8,128)} %wo_ref.6, ...), custom_call_target="tpu_custom_call" | custom-call | tf_op jit(solution)/shard_map/ffn_forward/pallas_call | solution.py:719
  101.6 41.0 %ffn_backward.1 = (f32[24,768,128]{2,1,0:T(8,128)}, f32[24,768,128]{2,1,0:T(8,128)}, f32[512,768]{1,0:T(8,128)}, f32[1,3072]{1,0:T(1,128)}, f32[8,768]{1,0:T(8,128)}) custom-call(f32[512,768]{1,0:T(8,128)} %get-tuple-element.98.h1_ref, f32[512,768]{1,0:T(8,128)} %get-tuple-element.100.gs2_ref, f32[512,3072]{1,0:T(8,128)} %get-tuple-element.101.pre_ref, ...), custom_call_target="tpu_custom_call" | custom-call | tf_op jit(solution)/shard_map/ffn_backward/pallas_call | solution.py:791
  142.6 11.7 %near_back.1 = (f32[512,768]{1,0:T(8,128)}, f32[512,768]{1,0:T(8,128)}, f32[6,64,128]{2,1,0:T(8,128)}, f32[64,768]{1,0:T(8,128)}, f32[32,768]{1,0:T(8,128)}) custom-call(s32[1,8]{1,0:T(1,128)} %lens_ref.15, f32[512,768]{1,0:T(8,128)} %get-tuple-element.104.gs1_ref, f32[768,768]{1,0:T(8,128)} %wo_ref.7, f32[512,768]{1,0:T(8,128)} %get-tuple-element.105.near_ref, ...), custom_call_target="tpu_custom_call" | custom-call | tf_op jit(solution)/shard_map/near_back/pallas_call | solution.py:842
  154.4 22.0 %blend_exchange.1 = (f32[6,72,128]{2,1,0:T(8,128)}, f32[16,768]{1,0:T(8,128)}, f32[16,768]{1,0:T(8,128)}, f32[2,64,768]{2,1,0:T(8,128)}) custom-call(f32[6,64,128]{2,1,0:T(8,128)} %get-tuple-element.109.g_ref, f32[32,768]{1,0:T(8,128)} %get-tuple-element.110.rim_ref, f32[64,768]{1,0:T(8,128)} %get-tuple-element.194.ql_ref, ...), custom_call_target="tpu_custom_call" | custom-call | tf_op jit(solution)/shard_map/blend_exchange/pallas_call | solution.py:532
  176.4 7.2 %far_back.1 = (f32[512,768]{1,0:T(8,128)}, f32[512,768]{1,0:T(8,128)}, f32[8,2,8,768]{3,2,1,0:T(8,128)}) custom-call(s32[1,8]{1,0:T(1,128)} %lens_ref.15, f32[512,768]{1,0:T(8,128)} %get-tuple-element.93.k_ref, f32[512,768]{1,0:T(8,128)} %get-tuple-element.89.v_ref, f32[512,768]{1,0:T(8,128)} %get-tuple-element.107.p_ref, ...), custom_call_target="tpu_custom_call" | custom-call | tf_op jit(solution)/shard_map/far_back/pallas_call | solution.py:882
  183.6 23.3 %conv_back.1 = (f32[512,768]{1,0:T(8,128)}, f32[40,128]{1,0:T(8,128)}, f32[6,768,128]{2,1,0:T(8,128)}) custom-call(s32[1,8]{1,0:T(1,128)} %lens_ref.15, f32[512,768]{1,0:T(8,128)} %get-tuple-element.89.v_ref, f32[16,768]{1,0:T(8,128)} %get-tuple-element.96.left_ref, f32[16,768]{1,0:T(8,128)} %get-tuple-element.97.right_ref, ...), custom_call_target="tpu_custom_call" | custom-call | tf_op jit(solution)/shard_map/conv_back/pallas_call | solution.py:915
  206.9 12.2 %land_return.1.own_ref = f32[2,8,768]{2,1,0:T(8,128)} custom-call(f32[8,2,8,768]{3,2,1,0:T(8,128)} %get-tuple-element.127.x_ref), custom_call_target="tpu_custom_call" | custom-call | tf_op jit(solution)/shard_map/land_return/pallas_call | solution.py:568
  219.2 19.6 %project_back.1 = (f32[512,768]{1,0:T(8,128)}, f32[6,768,128]{2,1,0:T(8,128)}, f32[6,768,128]{2,1,0:T(8,128)}, f32[6,768,128]{2,1,0:T(8,128)}, f32[8,768]{1,0:T(8,128)}) custom-call(s32[1,8]{1,0:T(1,128)} %lens_ref.15, f32[512,768]{1,0:T(8,128)} %bitcast.11, f32[512,768]{1,0:T(8,128)} %get-tuple-element.104.gs1_ref, f32[512,768]{1,0:T(8,128)} %get-tuple-element.106.gqn_ref, ...), custom_call_target="tpu_custom_call" | custom-call | tf_op jit(solution)/shard_map/project_back/pallas_call | solution.py:973
  238.8 229.1 %reduce_grads.1 = (f32[2,36,768,128]{3,2,1,0:T(8,128)}, f32[112,128]{1,0:T(8,128)}) custom-call(f32[24,768,128]{2,1,0:T(8,128)} %get-tuple-element.129.refs_0_, f32[24,768,128]{2,1,0:T(8,128)} %get-tuple-element.130.refs_1_, f32[6,768,128]{2,1,0:T(8,128)} %get-tuple-element.131.refs_2_, f32[6,768,128]{2,1,0:T(8,128)} %get-tuple-element.132.refs_3_, ...), custom_call_target="tpu_custom_call" | custom-call | tf_op jit(solution)/shard_map/reduce_grads/pallas_call | solution.py:1270
  467.9 20.9 %place_strips.1 = (f32[3072,768]{1,0:T(8,128)}, f32[768,3072]{1,0:T(8,128)}, f32[768,768]{1,0:T(8,128)}, f32[768,768]{1,0:T(8,128)}, f32[768,768]{1,0:T(8,128)},...) custom-call(f32[2,36,768,128]{3,2,1,0:T(8,128)} %get-tuple-element.1, ...), custom_call_target="tpu_custom_call" | custom-call | tf_op jit(solution)/shard_map/place_strips/pallas_call | solution.py:1347
  488.8 1.4 copy.40

commit v2 on v1

--- a/solution.py
+++ b/solution.py
@@ -16,6 +16,7 @@
 LANES = 128
 PAIRS = HEADS * DH // LANES
 QUAD = 256
+QUADS = HEADS * DH // QUAD
 SCALE = DH ** (-0.5)
 EPS = 1e-05
 ROOT_HALF = 0.7071067811865476
@@ -132,7 +133,7 @@
                 yield 8 * a + b, moved[8 * a : 8 * a + CONV_ROWS]
 
 
-def conv_into(out_ref, ext_ref, taps_ref, slots, flip, add):
+def conv_into(out_ref, ext_ref, taps_ref, slots, flip, add, low=0):
     def block(i, carry):
         r0 = pl.multiple_of((i // PAIRS) * CONV_ROWS, CONV_ROWS)
         l0 = pl.multiple_of((i % PAIRS) * LANES, LANES)
@@ -147,11 +148,12 @@
             out_ref[here] = acc
         return carry
 
-    lax.fori_loop(0, (slots // CONV_ROWS) * PAIRS, block, 0)
-
-
-def taps_grad_into(scr_ref, grad_ref, ext_ref, slots):
-    scr_ref[...] = jnp.zeros_like(scr_ref)
+    lax.fori_loop((low // CONV_ROWS) * PAIRS, (slots // CONV_ROWS) * PAIRS, block, 0)
+
+
+def taps_grad_into(scr_ref, grad_ref, ext_ref, slots, low=0, clear=True):
+    if clear:
+        scr_ref[...] = jnp.zeros_like(scr_ref)
 
     def block(i, carry):
         r0 = pl.multiple_of((i // PAIRS) * CONV_ROWS, CONV_ROWS)
@@ -165,7 +167,7 @@
             scr_ref[c, :, pl.ds(l0, LANES)] += total
         return carry
 
-    lax.fori_loop(0, (slots // CONV_ROWS) * PAIRS, block, 0)
+    lax.fori_loop((low // CONV_ROWS) * PAIRS, (slots // CONV_ROWS) * PAIRS, block, 0)
 
 
 def whole(shape=None):
@@ -185,46 +187,60 @@
 
 
 def project_kernel(
-    lens_ref, x_ref, wq_ref, wk_ref, wv_ref, bq_ref, bv_ref,
+    lens_ref, x_ref, wq_hbm, wk_hbm, wv_hbm, bq_ref, bv_ref,
     q_ref, k_ref, v_ref, land_ref, rim_ref,
+    w_ref, bias_ref, out_ref, load,
 ):
-    slots = x_ref.shape[0]
+    slots, width = x_ref.shape
     segs = land_ref.shape[1]
+    loads = [
+        pltpu.make_async_copy(hbm.at[:, pl.ds(g * QUAD, QUAD)], w_ref.at[i * QUADS + g], load.at[i * QUADS + g])
+        for i, hbm in enumerate((wq_hbm, wk_hbm, wv_hbm))
+        for g in range(QUADS)
+    ]
+    for copy in loads:
+        copy.start()
     ends = seg_ends(lens_ref, segs)
     member = member_rows(ends, slots)
     inv = inverse_lens(lens_ref, segs)
-    x = x_ref[...]
-    q = mm(x, wq_ref[...]) + bq_ref[...][None, :]
-    k = mm(x, wk_ref[...])
-    v = mm(x, wv_ref[...]) + bv_ref[...][None, :]
-    v = jnp.where(valid_rows(ends[-1], slots), v, 0.0)
-    q_ref[...] = q
-    k_ref[...] = k
-    v_ref[...] = v
-    land_ref[0] = mm(member, q) * inv
-    land_ref[1] = mm(member, k) * inv
-    rim_ref[...] = rims_of(v, ends[-1])
+    for g in range(QUADS):
+        bias_ref[g] = jnp.broadcast_to(bq_ref[pl.ds(g * QUAD, QUAD)][None, :], (8, QUAD))
+        bias_ref[QUADS + g] = jnp.zeros((8, QUAD), f32)
+        bias_ref[2 * QUADS + g] = jnp.broadcast_to(bv_ref[pl.ds(g * QUAD, QUAD)][None, :], (8, QUAD))
+
+    def one(i, carry):
+        pltpu.make_async_copy(wq_hbm.at[:, pl.ds(0, QUAD)], w_ref.at[i], load.at[i]).wait()
+        out_ref[i] = mm(x_ref[...], w_ref[i]) + bias_ref[i, 0:1, :]
+        return carry
+
+    lax.fori_loop(0, 3 * QUADS, one, 0)
+    valid = valid_rows(ends[-1], slots)
+    for g in range(QUADS):
+        cols = slice(g * QUAD, (g + 1) * QUAD)
+        q_ref[:, cols] = out_ref[g]
+        k_ref[:, cols] = out_ref[QUADS + g]
+        v_ref[:, cols] = jnp.where(valid, out_ref[2 * QUADS + g], 0.0)
+    land_ref[0] = mm(member, q_ref[...]) * inv
+    land_ref[1] = mm(member, k_ref[...]) * inv
+    rim_ref[...] = rims_of(v_ref[...], ends[-1])
 
 
 def project(lens, x, wq, wk, wv, bq, bv):
     slots, width = x.shape
     segs = lens.shape[1]
-    col = 256
-    wspec = pl.BlockSpec((width, col), lambda i: (0, i))
-    bspec = pl.BlockSpec((col,), lambda i: (i,))
-    ospec = pl.BlockSpec((slots, col), lambda i: (0, i))
+    anywhere = pl.BlockSpec(memory_space=pl.ANY)
+    count = 3 * QUADS
     return pl.pallas_call(
         project_kernel,
-        grid=(width // col,),
-        in_specs=[smem(), pl.BlockSpec((slots, width), lambda i: (0, 0)), wspec, wspec, wspec, bspec, bspec],
-        out_specs=[
-            ospec, ospec, ospec,
-            pl.BlockSpec((2, segs, col), lambda i: (0, 0, i)),
-            pl.BlockSpec((2 * RIM, col), lambda i: (0, i)),
-        ],
+        in_specs=[smem(), whole()] + [anywhere] * 3 + [whole()] * 2,
+        out_specs=[whole()] * 5,
         out_shape=[
             shape(slots, width), shape(slots, width), shape(slots, width),
             shape(2, segs, width), shape(2 * RIM, width),
+        ],
+        scratch_shapes=[
+            pltpu.VMEM((count, width, QUAD), f32), pltpu.VMEM((count, 8, QUAD), f32),
+            pltpu.VMEM((count, slots, QUAD), f32), pltpu.SemaphoreType.DMA((count,)),
         ],
         compiler_params=params(),
         name="project",
@@ -365,16 +381,21 @@
         sigma = jnp.sqrt(pair_sums(colsum * colsum))
         z = core.T / sigma
         unit = eye(LANES)
-        for step in range(NEWTON):
-            zs_ref[step] = z
-            prod = mm(core, z, TOP)
+        zs_ref[0] = z
+
+        def newton(step, carry):
+            z = zs_ref[step]
+            prod = mm(core_ref[...], z, TOP)
             ps_ref[step] = prod
             r = 15.0 * unit - mm(prod, 7.0 * unit - prod, TOP)
             rs_ref[step] = r
             q = 13.0 * unit - mm(prod, r, TOP)
             qs_ref[step] = q
-            z = 0.25 * mm(z, q, TOP)
-        zs_ref[NEWTON] = z
+            zs_ref[step + 1] = 0.25 * mm(z, q, TOP)
+            return carry
+
+        lax.fori_loop(0, NEWTON, newton, 0)
+        z = zs_ref[NEWTON]
         land[me] = f_ref[me]
         for s in range(n):
 
@@ -437,6 +458,35 @@
     )(parts, ql, kl)
 
 
+def inverse_grad(gblend, mixed):
+    return jnp.where(head_mask(LANES), t_mm(gblend, mixed, TOP), 0.0)
+
+
+def newton_back(g, gcore, core, z, prod, r, q):
+    prod_t = prod.T
+    gq = 0.25 * mm(z.T, g, TOP)
+    gr = -mm(prod_t, gq, TOP)
+    gs = -mm(prod_t, gr, TOP)
+    gp = -mm_t(gq, r, TOP) - mm_t(gr, 7.0 * eye(LANES) - prod, TOP) - gs
+    return 0.25 * mm_t(g, q, TOP) + mm(core.T, gp, TOP), gcore + mm_t(gp, z, TOP)
+
+
+def core_back(g, gcore, core, first, ql_ref, kl_ref, gl_ref, me):
+    mask = head_mask(LANES)
+    colsum = jnp.sum(core, axis=0, keepdims=True)
+    square = pair_sums(colsum * colsum)
+    sigma = jnp.sqrt(square)
+    dot = pair_sums(jnp.sum(g * first, axis=0, keepdims=True))
+    gcore = gcore + g.T / sigma - jnp.where(mask, dot / square * colsum, 0.0)
+    gscore = core * (gcore - jnp.sum(core * gcore, axis=1, keepdims=True)) * SCALE
+    lanes = pl.ds(pl.multiple_of(me * LANES, LANES), LANES)
+    query = spread(ql_ref[:, lanes], mask)
+    key = spread(kl_ref[:, lanes], mask)
+    gl_ref[...] = jnp.zeros_like(gl_ref)
+    gl_ref[0, :, lanes] = fold(mm(gscore, key, TOP), mask)
+    gl_ref[1, :, lanes] = fold(t_mm(gscore, query, TOP), mask)
+
+
 def blend_exchange_kernel(
     n, g_ref, rim_ref, ql_ref, kl_ref, core_ref, zs_ref, ps_ref, rs_ref, qs_ref, mx_ref,
     c_ref, left_ref, right_ref, gl_ref,
@@ -481,32 +531,11 @@
             def _(t=t):
                 to_seq(c_ref.at[me], c_ref.at[me], s2.at[t], r2.at[me], t).start()
 
-        core = core_ref[...]
-        core_t = core.T
-        unit = eye(LANES)
-        g = jnp.where(mask, t_mm(gblend, mixed, TOP), 0.0)
         gcore = jnp.zeros((LANES, LANES), f32)
+        g = inverse_grad(gblend, mixed)
         for step in reversed(range(NEWTON)):
-            z = zs_ref[step]
-            prod_t = ps_ref[step].T
-            gq = 0.25 * mm(z.T, g, TOP)
-            gr = -mm(prod_t, gq, TOP)
-            gs = -mm(prod_t, gr, TOP)
-            gp = -mm_t(gq, rs_ref[step], TOP) - mm_t(gr, 7.0 * unit - ps_ref[step], TOP) - gs
-            gcore = gcore + mm_t(gp, z, TOP)
-            g = 0.25 * mm_t(g, qs_ref[step], TOP) + mm(core_t, gp, TOP)
-        colsum = jnp.sum(core, axis=0, keepdims=True)
-        square = pair_sums(colsum * colsum)
-        sigma = jnp.sqrt(square)
-        dot = pair_sums(jnp.sum(g * zs_ref[0], axis=0, keepdims=True))
-        gcore = gcore + g.T / sigma - jnp.where(mask, dot / square * colsum, 0.0)
-        gscore = core * (gcore - jnp.sum(core * gcore, axis=1, keepdims=True)) * SCALE
-        lanes = pl.ds(pl.multiple_of(me * LANES, LANES), LANES)
-        query = spread(ql_ref[:, lanes], mask)
-        key = spread(kl_ref[:, lanes], mask)
-        gl_ref[...] = jnp.zeros_like(gl_ref)
-        gl_ref[0, :, lanes] = fold(mm(gscore, key, TOP), mask)
-        gl_ref[1, :, lanes] = fold(t_mm(gscore, query, TOP), mask)
+            g, gcore = newton_back(g, gcore, core_ref[...], zs_ref[step], ps_ref[step], rs_ref[step], qs_ref[step])
+        core_back(g, gcore, core_ref[...], zs_ref[0], ql_ref, kl_ref, gl_ref, me)
 
     for p in range(PAIRS):
 
@@ -581,8 +610,9 @@
     count = seg_ends(lens_ref, lens_ref.shape[1])[-1]
     valid = valid_rows(count, slots)
     mask = head_mask(QUAD)
-    for g in range(HEADS * DH // QUAD):
-        cols = slice(g * QUAD, (g + 1) * QUAD)
+
+    def one(g, carry):
+        cols = quad(g)
         scores = mm_t(k_ref[:, cols], spread(ql_ref[:, cols], mask)) * SCALE
         scores = jnp.where(valid, scores, MASKED)
         top = jnp.max(scores, axis=0, keepdims=True)
@@ -596,6 +626,9 @@
             part = slice(j * LANES, (j + 1) * LANES)
             f_ref[g * 2 + j, 0:DH, :] = weighted[:, part]
             f_ref[g * 2 + j, DH:MSG, :] = tail[:, part]
+        return carry
+
+    lax.fori_loop(0, QUADS, one, 0)
 
 
 def far_local(lens, k, v, ql):
@@ -626,14 +659,17 @@
     ) * inv
 
 
+def quad(g):
+    return pl.ds(pl.multiple_of(g * QUAD, QUAD), QUAD)
+
+
 def pair_rows(ref, g, rows):
     return jnp.concatenate([ref[2 * g, rows, :], ref[2 * g + 1, rows, :]], axis=1)
 
 
 def attend_kernel(
     lens_ref, q_ref, v_ref, kl_ref, b_ref, left_ref, right_ref, taps_ref, x_ref, wo_ref, bo_ref, g1_ref, b1_ref,
-    near_ref, ctx_ref, h1_ref, u1_ref, inv1_ref,
-    ext_ref,
+    near_ref, ctx_ref, h1_ref, u1_ref, inv1_ref, ext_ref,
 ):
     slots = q_ref.shape[0]
     count = seg_ends(lens_ref, lens_ref.shape[1])[-1]
@@ -642,8 +678,9 @@
     mask = head_mask(QUAD)
     ones = jnp.where(mask, 1.0, 0.0)
     head = lax.broadcasted_iota(jnp.int32, (slots, QUAD), 1) >> 6
-    for g in range(HEADS * DH // QUAD):
-        cols = slice(g * QUAD, (g + 1) * QUAD)
+
+    def one(g, carry):
+        cols = quad(g)
         scores = mm_t(q_ref[:, cols], spread(kl_ref[:, cols], mask)) * SCALE
         tops = [jnp.max(scores[:, h * DH : (h + 1) * DH], axis=1, keepdims=True) for h in range(4)]
         top = jnp.where(head < 2, jnp.where(head < 1, tops[0], tops[1]), jnp.where(head < 3, tops[2], tops[3]))
@@ -652,7 +689,17 @@
         near_ref[:, cols] = near
         blend = spread(pair_rows(b_ref, g, slice(0, DH)), mask)
         ctx_ref[:, cols] += mm_t(near, blend)
-    summed = x_ref[...] + (mm(ctx_ref[...], wo_ref[...]) + bo_ref[...][None, :])
+        return carry
+
+    lax.fori_loop(0, QUADS, one, 0)
+
+    def two(g, carry):
+        cols = quad(g)
+        u1_ref[:, cols] = mm(ctx_ref[...], wo_ref[:, cols])
+        return carry
+
+    lax.fori_loop(0, QUADS, two, 0)
+    summed = x_ref[...] + (u1_ref[...] + bo_ref[...][None, :])
     unit, inv = norm_stats(summed)
     u1_ref[...] = unit
     inv1_ref[...] = inv
@@ -664,9 +711,8 @@
     return pl.pallas_call(
         attend_kernel,
         in_specs=[smem()] + [whole()] * 12,
-        out_specs=[whole()] * 5,
-        out_shape=[shape(slots, width)] * 4 + [shape(slots, 1)],
-        scratch_shapes=[pltpu.VMEM((slots + 40, width), f32)],
+        out_specs=[whole()] * 6,
+        out_shape=[shape(slots, width)] * 4 + [shape(slots, 1), shape(slots + 40, width)],
         compiler_params=params(),
         name="attend",
     )(lens, q, v, kl, b, left, right, taps, x, wo, bo, g1, b1)
@@ -675,21 +721,29 @@
 def forward_kernel(
     lens_ref, h1_ref, wi_ref, bi_ref, wo_ref, bo_ref, cot_ref, g2_ref, b2_ref,
     pre_ref, out_ref, gs2_ref, small_ref,
-    acc_ref,
+    acc_ref, act_ref,
 ):
     step = pl.program_id(0)
-    pre = mm(h1_ref[...], wi_ref[...]) + bi_ref[...]
-    pre_ref[...] = pre
-    act = 0.5 * pre * (1.0 + lax.erf(pre * ROOT_HALF))
-    part = mm(act, wo_ref[...])
 
     @pl.when(step == 0)
     def _():
-        acc_ref[...] = part
-
-    @pl.when(step > 0)
-    def _():
-        acc_ref[...] += part
+        acc_ref[...] = jnp.zeros_like(acc_ref)
+
+    def one(g, carry):
+        cols = quad(g)
+        pre = mm(h1_ref[...], wi_ref[:, cols]) + bi_ref[:, cols]
+        pre_ref[:, cols] = pre
+        act_ref[:, cols] = 0.5 * pre * (1.0 + lax.erf(pre * ROOT_HALF))
+        return carry
+
+    lax.fori_loop(0, QUADS, one, 0)
+
+    def two(g, carry):
+        cols = quad(g)
+        acc_ref[:, cols] += mm(act_ref[...], wo_ref[:, cols])
+        return carry
+
+    lax.fori_loop(0, QUADS, two, 0)
 
     @pl.when(step == pl.num_programs(0) - 1)
     def _():
@@ -730,41 +784,48 @@
             const(slots, width), const(slots, width), const(8, width),
         ],
         out_shape=[shape(slots, inner), shape(slots, width), shape(slots, width), shape(8, width)],
-        scratch_shapes=[pltpu.VMEM((slots, width), f32)],
+        scratch_shapes=[pltpu.VMEM((slots, width), f32)] * 2,
         compiler_params=params(),
         name="ffn_forward",
     )(lens, h1, wi, bi, wo, bo, cot, g2, b2)
 
 
-def put_strips(ref, block):
+def put_strips(ref, block, rows=slice(None), first=0):
     for s in range(block.shape[1] // LANES):
-        ref[s] = block[:, s * LANES : (s + 1) * LANES]
+        ref[first + s, rows, :] = block[:, s * LANES : (s + 1) * LANES]
 
 
 def backward_kernel(
     h1_ref, gs2_ref, pre_ref, wi_ref, wo_ref, u1_ref, inv1_ref, g1_ref,
     dwo_ref, dwi_ref, gs1_ref, dbi_ref, small_ref,
-    acc_ref,
+    acc_ref, gpre_ref,
 ):
     step = pl.program_id(0)
-    gs2 = gs2_ref[...]
-    pre = pre_ref[...]
-    phi_big = 0.5 * (1.0 + lax.erf(pre * ROOT_HALF))
-    act = pre * phi_big
-    slope = phi_big + pre * (INV_ROOT_TAU * jnp.exp(-0.5 * pre * pre))
-    gpre = mm_t(gs2, wo_ref[...]) * slope
-    put_strips(dwo_ref, t_mm(act, gs2))
-    put_strips(dwi_ref, t_mm(h1_ref[...], gpre))
-    dbi_ref[...] = jnp.sum(gpre, axis=0, keepdims=True)
-    part = mm_t(gpre, wi_ref[...])
 
     @pl.when(step == 0)
     def _():
-        acc_ref[...] = gs2 + part
-
-    @pl.when(step > 0)
-    def _():
-        acc_ref[...] += part
+        acc_ref[...] = gs2_ref[...]
+
+    def one(g, carry):
+        cols = quad(g)
+        pre = pre_ref[:, cols]
+        phi_big = 0.5 * (1.0 + lax.erf(pre * ROOT_HALF))
+        slope = phi_big + pre * (INV_ROOT_TAU * jnp.exp(-0.5 * pre * pre))
+        gpre = mm_t(gs2_ref[...], wo_ref[cols, :]) * slope
+        gpre_ref[:, cols] = gpre
+        dbi_ref[:, cols] = jnp.sum(gpre, axis=0, keepdims=True)
+        put_strips(dwo_ref, t_mm(pre * phi_big, gs2_ref[...]), cols)
+        return carry
+
+    lax.fori_loop(0, QUADS, one, 0)
+
+    def two(g, carry):
+        cols = quad(g)
+        put_strips(dwi_ref, t_mm(h1_ref[:, cols], gpre_ref[...]), cols)
+        acc_ref[:, cols] += mm_t(gpre_ref[...], wi_ref[cols, :])
+        return carry
+
+    lax.fori_loop(0, QUADS, two, 0)
 
     @pl.when(step == pl.num_programs(0) - 1)
     def _():
@@ -809,10 +870,25 @@
             shape(inner // LANES, width, LANES), shape(inner // LANES, width, LANES),
             shape(slots, width), shape(1, inner), shape(8, width),
         ],
-        scratch_shapes=[pltpu.VMEM((slots, width), f32)],
+        scratch_shapes=[pltpu.VMEM((slots, width), f32)] * 2,
         compiler_params=params(),
         name="ffn_backward",
     )(h1, gs2, pre, wi, wo, u1, inv1, g1)
+
+
+def near_back_quad(g, gctx_ref, near_ref, q_ref, kl_ref, b_ref, gq_ref, gb_ref, gkl_ref):
+    mask = head_mask(QUAD)
+    ones = jnp.where(mask, 1.0, 0.0)
+    cols = quad(g)
+    gctx = gctx_ref[:, cols]
+    near = near_ref[:, cols]
+    gblend = fold(t_mm(gctx, near), mask)
+    gb_ref[2 * g] = gblend[:, :LANES]
+    gb_ref[2 * g + 1] = gblend[:, LANES:]
+    gnear = mm(gctx, spread(pair_rows(b_ref, g, slice(0, DH)), mask))
+    gscore = near * (gnear - mm(near * gnear, ones)) * SCALE
+    gq_ref[:, cols] = mm(gscore, spread(kl_ref[:, cols], mask))
+    gkl_ref[:, cols] = fold(t_mm(gscore, q_ref[:, cols]), mask)
 
 
 def near_back_kernel(
@@ -822,19 +898,11 @@
     count = seg_ends(lens_ref, lens_ref.shape[1])[-1]
     gctx_ref[...] = mm_t(gs1_ref[...], wo_ref[...])
     rim_ref[...] = rims_of(gctx_ref[...], count)
-    mask = head_mask(QUAD)
-    ones = jnp.where(mask, 1.0, 0.0)
-    for g in range(HEADS * DH // QUAD):
-        cols = slice(g * QUAD, (g + 1) * QUAD)
-        gctx = gctx_ref[:, cols]
-        near = near_ref[:, cols]
-        gblend = fold(t_mm(gctx, near), mask)
-        gb_ref[2 * g] = gblend[:, :LANES]
-        gb_ref[2 * g + 1] = gblend[:, LANES:]
-        gnear = mm(gctx, spread(pair_rows(b_ref, g, slice(0, DH)), mask))
-        gscore = near * (gnear - mm(near * gnear, ones)) * SCALE
-        gq_ref[:, cols] = mm(gscore, spread(kl_ref[:, cols], mask))
-        gkl_ref[:, cols] = fold(t_mm(gscore, q_ref[:, cols]), mask)
+    def one(g, carry):
+        near_back_quad(g, gctx_ref, near_ref, q_ref, kl_ref, b_ref, gq_ref, gb_ref, gkl_ref)
+        return carry
+
+    lax.fori_loop(0, QUADS, one, 0)
 
 
 def near_back(lens, gs1, wo, near, q, kl, b):
@@ -852,28 +920,42 @@
     )(lens, gs1, wo, near, q, kl, b)
 
 
+def far_back_quad(g, k_ref, v_ref, p_ref, m_ref, b_ref, c_ref, ql_ref, gk_ref, gv_ref, gql_ref, add):
+    mask = head_mask(QUAD)
+    cols = quad(g)
+    top = pair_rows(b_ref, g, slice(DH, DH + 1))
+    total = pair_rows(b_ref, g, slice(DH + 1, DH + 2))
+    prob = p_ref[:, cols] * (jnp.exp(m_ref[:, cols] - top) / total)
+    gmixed = spread(pair_rows(c_ref, g, slice(0, DH)), mask)
+    dots = pair_rows(c_ref, g, slice(DH, DH + 1))
+    gscore = prob * (mm(v_ref[:, cols], gmixed) - dots) * SCALE
+    gk_ref[:, cols] = mm(gscore, spread(ql_ref[:, cols], mask))
+    gval = mm_t(prob, gmixed)
+    if add:
+        gv_ref[:, cols] += gval
+    else:
+        gv_ref[:, cols] = gval
+    gql_ref[:, cols] = fold(t_mm(gscore, k_ref[:, cols]), mask)
+
+
+def land_parts(ret_ref, gql, gkl):
+    n, _, segs, _ = ret_ref.shape
+    for s in range(n):
+        rows = slice(s * segs, (s + 1) * segs)
+        ret_ref[s, 0] = gql[rows]
+        ret_ref[s, 1] = gkl[rows]
+
+
 def far_back_kernel(
-    lens_ref, k_ref, v_ref, p_ref, m_ref, b_ref, c_ref, ql_ref, gkl_ref, gl_ref,
-    gk_ref, gv_ref, ret_ref,
+    k_ref, v_ref, p_ref, m_ref, b_ref, c_ref, ql_ref, gkl_ref, gl_ref,
+    gk_ref, gv_ref, ret_ref, gql_ref,
 ):
-    mask = head_mask(QUAD)
-    n, _, segs, _ = ret_ref.shape
-    for g in range(HEADS * DH // QUAD):
-        cols = slice(g * QUAD, (g + 1) * QUAD)
-        top = pair_rows(b_ref, g, slice(DH, DH + 1))
-        total = pair_rows(b_ref, g, slice(DH + 1, DH + 2))
-        prob = p_ref[:, cols] * (jnp.exp(m_ref[:, cols] - top) / total)
-        gmixed = spread(pair_rows(c_ref, g, slice(0, DH)), mask)
-        dots = pair_rows(c_ref, g, slice(DH, DH + 1))
-        gscore = prob * (mm(v_ref[:, cols], gmixed) - dots) * SCALE
-        gk_ref[:, cols] = mm(gscore, spread(ql_ref[:, cols], mask))
-        gv_ref[:, cols] = mm_t(prob, gmixed)
-        gql = fold(t_mm(gscore, k_ref[:, cols]), mask) + gl_ref[0, :, cols]
-        gkl = gkl_ref[:, cols] + gl_ref[1, :, cols]
-        for s in range(n):
-            rows = slice(s * segs, (s + 1) * segs)
-            ret_ref[s, 0, :, cols] = gql[rows]
-            ret_ref[s, 1, :, cols] = gkl[rows]
+    def one(g, carry):
+        far_back_quad(g, k_ref, v_ref, p_ref, m_ref, b_ref, c_ref, ql_ref, gk_ref, gv_ref, gql_ref, False)
+        return carry
+
+    lax.fori_loop(0, QUADS, one, 0)
+    land_parts(ret_ref, gql_ref[...] + gl_ref[0], gkl_ref[...] + gl_ref[1])
 
 
 def far_back(n, lens, k, v, p, m, b, c, ql, gkl, gl):
@@ -881,12 +963,23 @@
     segs = lens.shape[1]
     return pl.pallas_call(
         far_back_kernel,
-        in_specs=[smem()] + [whole()] * 9,
+        in_specs=[whole()] * 9,
         out_specs=[whole()] * 3,
         out_shape=[shape(slots, width), shape(slots, width), shape(n, 2, segs, width)],
+        scratch_shapes=[pltpu.VMEM((DH, width), f32)],
         compiler_params=params(),
         name="far_back",
-    )(lens, k, v, p, m, b, c, ql, gkl, gl)
+    )(k, v, p, m, b, c, ql, gkl, gl)
+
+
+def taps_sums(scr_ref):
+    width = scr_ref.shape[2]
+    rows = jnp.concatenate(
+        [jnp.sum(scr_ref[c], axis=0, keepdims=True) for c in range(CONV)] + [jnp.zeros((7, width), f32)], axis=0
+    )
+    row = lax.broadcasted_iota(jnp.int32, (width, LANES), 0) >> 6
+    col = lax.broadcasted_iota(jnp.int32, (width, LANES), 1)
+    return mm(rows, jnp.where(row == col, 1.0, 0.0), TOP)
 
 
 def conv_back_kernel(
@@ -901,13 +994,7 @@
     conv_into(gv_ref, ext_ref, taps_ref, slots, True, False)
     fill_extended(ext_ref, v_ref[...], left_ref[...], right_ref[...], count)
     taps_grad_into(scr_ref, gctx_ref, ext_ref, slots)
-    rows = jnp.concatenate(
-        [jnp.sum(scr_ref[c], axis=0, keepdims=True) for c in range(CONV)] + [jnp.zeros((7, v_ref.shape[1]), f32)],
-        axis=0,
-    )
-    row = lax.broadcasted_iota(jnp.int32, (v_ref.shape[1], LANES), 0) >> 6
-    col = lax.broadcasted_iota(jnp.int32, (v_ref.shape[1], LANES), 1)
-    gtaps_ref[...] = mm(rows, jnp.where(row == col, 1.0, 0.0), TOP)
+    gtaps_ref[...] = taps_sums(scr_ref)
 
 
 def conv_back(lens, v, left, right, gctx, gleft, gright, taps, ctx, gs1):
@@ -1029,15 +1116,9 @@
     outs[-1][...] = s_ref[at : at + CONV, :HEADS]
 
 
-def reduce_kernel(spans, lag, *refs):
-    count = len(spans)
-    grads = refs[:count]
-    smalls = refs[count : count + 5]
-    o_ref, so_ref, acc, lc, l1, lz, l3, sb, sl = refs[count + 5 : count + 14]
-    (
-        local, out_local, cs, cr, s1, r1, zs, zr, s3, r3, s4, r4, gs, gr, s5, r5, es, er, ss, sr,
-    ) = refs[count + 14 :]
-    chunks = spans[-1][1]
+def reduce_stages(spans, grads, o_ref, bufs, sems):
+    acc, lc, l1, lz, l3 = bufs
+    local, out_local, cs, cr, s1, r1, zs, zr, s3, r3, s4, r4, gs, gr, s5, r5, es, er = sems
     seq = lax.axis_index("seq")
     dp = lax.axis_index("dp")
     z = seq // 2
@@ -1053,15 +1134,12 @@
     left = place(lax.rem(z + 3, 4), c, y, x)
     opposite = place(lax.rem(z + 2, 4), c, y, x)
     near_z = place(z + 1 - 2 * lax.rem(z, 2), c, y, x)
-    barrier = pltpu.get_barrier_semaphore()
-    for target in (by_core, by_x, by_y, right, left, opposite):
-        pl.semaphore_signal(barrier, inc=1, device_id=target, device_id_type=MESH)
-    pl.semaphore_wait(barrier, 6)
 
     def remote(src, dst, send, recv, target):
         return pltpu.make_async_remote_copy(src, dst, send, recv, device_id=target, device_id_type=MESH)
 
     aligned = lambda at: pl.multiple_of(at, 8)
+    slot = lambda ref, k: lax.rem(k, ref.shape[0])
     a1 = x * PART
     b1 = HALF + y * PART
     firsts = ((0, a1, (1 - x) * PART, by_x), (1, b1, HALF + (1 - y) * PART, by_y))
@@ -1076,30 +1154,38 @@
     def rows(ref, k, at, size):
         return ref.at[k, pl.ds(aligned(at), size)]
 
+    def acc_rows(k, at, size):
+        return rows(acc, slot(acc, k), at, size)
+
+    def core_copies(k, g, lo):
+        mine = pltpu.make_async_copy(g.at[2 * (k - lo) + c], acc.at[slot(acc, k)], local.at[k])
+        other = remote(g.at[2 * (k - lo) + 1 - c], lc.at[slot(lc, k)], cs.at[k], cr.at[k], by_core)
+        return mine, other
+
     def core_out(k):
         for g, (lo, hi) in zip(grads, spans):
-            half = hi - lo
 
             @pl.when((k >= lo) & (k < hi))
-            def _(g=g, lo=lo, half=half):
-                pltpu.make_async_copy(g.at[c * half + (k - lo)], acc.at[k], local.at[k]).start()
-                remote(g.at[(1 - c) * half + (k - lo)], lc.at[k], cs.at[k], cr.at[k], by_core).start()
+            def _(g=g, lo=lo):
+                for copy in core_copies(k, g, lo):
+                    copy.start()
 
     def first(k, j):
         _, _, other, target = firsts[j]
-        return remote(rows(acc, k, other, PART), l1.at[k, j], s1.at[k, j], r1.at[k, j], target)
+        return remote(acc_rows(k, other, PART), l1.at[slot(l1, k), j], s1.at[k, j], r1.at[k, j], target)
 
     def first_out(k):
-        pltpu.make_async_copy(grads[0].at[0], acc.at[k], local.at[k]).wait()
-        remote(grads[0].at[0], lc.at[k], cs.at[k], cr.at[k], by_core).wait_recv()
-        acc[k] += lc[k]
+        mine, other = core_copies(k, grads[0], k)
+        mine.wait()
+        other.wait_recv()
+        acc[slot(acc, k)] += lc[slot(lc, k)]
         for j in range(2):
             first(k, j).start()
 
     def z_copy(k, j, way, step, block):
         target = right if way == 0 else left
         return remote(
-            rows(acc, k, starts[j] + block * Z_ROWS, Z_ROWS), lz.at[k, way, j, step],
+            acc_rows(k, starts[j] + block * Z_ROWS, Z_ROWS), lz.at[slot(lz, k), way, j, step],
             zs.at[k, way, step, j], zr.at[k, way, step, j], target,
         )
 
@@ -1107,7 +1193,7 @@
         if step == 0:
             for j, mine, _, _ in firsts:
                 first(k, j).wait_recv()
-                acc[k, pl.ds(aligned(mine), PART)] += l1[k, j]
+                acc[slot(acc, k), pl.ds(aligned(mine), PART)] += l1[slot(l1, k), j]
         for way, at in ((0, z), (1, zb)):
             block = 3 - step + z if way == 0 else step - zb
             if step > 0:
@@ -1116,8 +1202,8 @@
                 def _(way=way, block=block):
                     for j in range(2):
                         z_copy(k, j, way, step - 1, 0).wait_recv()
-                    for j in range(2):
-                        acc[k, pl.ds(aligned(starts[j] + block * Z_ROWS), Z_ROWS)] += lz[k, way, j, step - 1]
+                        here = (slot(acc, k), pl.ds(aligned(starts[j] + block * Z_ROWS), Z_ROWS))
+                        acc[here] += lz[slot(lz, k), way, j, step - 1]
 
             if step < 3:
 
@@ -1128,7 +1214,7 @@
 
     def third(k, j):
         _, _, other, target = thirds[j]
-        return remote(rows(acc, k, other, OWN), l3.at[k, j], s3.at[k, j], r3.at[k, j], target)
+        return remote(acc_rows(k, other, OWN), l3.at[slot(l3, k), j], s3.at[k, j], r3.at[k, j], target)
 
     def third_out(k):
         z_out(k, 3)
@@ -1137,16 +1223,16 @@
 
     def back_third(k, j):
         _, mine, _, target = thirds[j]
-        return remote(rows(acc, k, mine, OWN), rows(o_ref.at[c], k, mine, OWN), s4.at[k, j], r4.at[k, j], target)
+        return remote(acc_rows(k, mine, OWN), rows(o_ref.at[c], k, mine, OWN), s4.at[k, j], r4.at[k, j], target)
 
     def keep(k, j):
         mine = thirds[j][1]
-        return pltpu.make_async_copy(rows(acc, k, mine, OWN), rows(o_ref.at[c], k, mine, OWN), out_local.at[k, j])
+        return pltpu.make_async_copy(acc_rows(k, mine, OWN), rows(o_ref.at[c], k, mine, OWN), out_local.at[k, j])
 
     def back_third_out(k):
         for j, mine, _, _ in thirds:
             third(k, j).wait_recv()
-            acc[k, pl.ds(aligned(mine), OWN)] += l3[k, j]
+            acc[slot(acc, k), pl.ds(aligned(mine), OWN)] += l3[slot(l3, k), j]
         for j in range(2):
             back_third(k, j).start()
             keep(k, j).start()
@@ -1158,9 +1244,20 @@
 
     def back_z_out(k, step):
         if step == 0:
+            core_copies(k, grads[0], k)[1].wait_send()
             for j in range(2):
                 keep(k, j).wait()
-                back_third(k, j).wait_recv()
+                first(k, j).wait_send()
+                third(k, j).wait_send()
+                back_third(k, j).wait()
+            for s in range(3):
+                for way, at in ((0, z), (1, zb)):
+
+                    @pl.when((at <= s) & (at < 3))
+                    def _(way=way, s=s):
+                        for j in range(2):
+                            z_copy(k, j, way, s, 0).wait_send()
+
         for way, at in ((0, z), (1, zb)):
             block = z - step if way == 0 else z + step
             if step > 0:
@@ -1198,19 +1295,10 @@
 
     def finish(k):
         back_core(k).wait()
-        remote(grads[0].at[0], lc.at[k], cs.at[k], cr.at[k], by_core).wait_send()
         for j in range(2):
-            first(k, j).wait_send()
-            third(k, j).wait_send()
-            back_third(k, j).wait_send()
             back_first(k, j).wait_send()
         for step in range(3):
             for way, at in ((0, z), (1, zb)):
-
-                @pl.when((at <= step) & (at < 3))
-                def _(way=way, step=step):
-                    for j in range(2):
-                        z_copy(k, j, way, step, 0).wait_send()
 
                 @pl.when((at >= step) & (at < 3))
                 def _(way=way, step=step):
@@ -1222,77 +1310,343 @@
         back_third_out, partial(back_z_out, step=0), partial(back_z_out, step=1), partial(back_z_out, step=2),
         back_first_out, back_core_out, finish,
     ]
-
-    partners = (by_core, by_x, by_y, near_z, opposite)
+    return stages, (by_core, by_x, by_y, near_z, opposite), remote
+
+
+LAG = tuple(range(0, 2 * STAGES, 2))
+RING_ACC = 16
+RING_LC = 4
+RING_Z = 6
+SEQ_DEVICES = 8
+SMALL_AT = 24
+
+
+def greet_block():
+    seq = lax.axis_index("seq")
+    dp = lax.axis_index("dp")
+    y = dp // 2
+    x = lax.rem(dp, 2)
+    barrier = pltpu.get_barrier_semaphore()
+    for d in range(1, SEQ_DEVICES):
+        pl.semaphore_signal(
+            barrier, inc=1, device_id=(lax.rem(seq + d, SEQ_DEVICES), dp), device_id_type=MESH
+        )
+    for other in (y * 2 + 1 - x, (1 - y) * 2 + x):
+        pl.semaphore_signal(barrier, inc=1, device_id=(seq, other), device_id_type=MESH)
+    pl.semaphore_wait(barrier, SEQ_DEVICES + 1)
+    return seq
+
+
+def tail_kernel(
+    spans,
+    lens_ref, dout_ref, din_ref, gs1_hbm, wo_hbm, near_hbm, q_hbm, ctx_hbm, ext_hbm, k_hbm, v_hbm, p_hbm, x_hbm,
+    wq_hbm, wk_hbm, wv_hbm,
+    m_ref, b_ref, ql_ref, kl_ref, core_ref, zs_ref, ps_ref, rs_ref, qs_ref, mx_ref, taps_ref,
+    small1_ref, small2_ref, dbi_ref,
+    o_ref, so_ref, ig_hbm,
+    acc, lc, l1, lz, l3, sb, sl, gw,
+    stack, w, ext, k, v, gext, tap_scr, gtaps, small0,
+    gb, rim, gkl, gql, gl, land, cmsg, gleft, gright, ng, ncore, ret, rland, own,
+    loads, ig_sem, b1s, b1r, b2s, b2r, ms, mr, rets, retr, ss, sr,
+    *sems,
+):
+    n = SEQ_DEVICES
+    chunks = spans[-1][1]
+    slots = k.shape[0]
+    segs = own.shape[1]
+    gs1, near, p, gv, ctx, q, gctx, ig = [stack.at[i] for i in range(8)]
+
+    def load(i, src, dst):
+        return pltpu.make_async_copy(src, dst, loads.at[i])
+
+    early = [
+        load(0, gs1_hbm, gs1), load(1, wo_hbm, w.at[0]), load(2, near_hbm, near), load(3, q_hbm, q), load(4, ctx_hbm, ctx),
+        load(5, ext_hbm, ext), load(6, v_hbm, v), load(7, p_hbm, p), load(8, k_hbm, k),
+    ]
+    late = [load(9, x_hbm, q), load(10, wq_hbm, w.at[1]), load(11, wk_hbm, w.at[2]), load(12, wv_hbm, w.at[3])]
+    for copy in early:
+        copy.start()
+    me = greet_block()
+    owner = me < PAIRS
+    stages, partners, remote = reduce_stages(spans, (dout_ref, din_ref, gw), o_ref, (acc, lc, l1, lz, l3), sems)
+    ends = seg_ends(lens_ref, segs)
+    count = ends[-1]
+
+    def weight_event(i):
+        left = jnp.where(i == 0, 4, 5)
+
+        def one(g, carry):
+            block = t_mm(stack[left, :, quad(g)], stack[i])
+            put_strips(gw, block, quad(g), i * PAIRS)
+            return carry
+
+        lax.fori_loop(0, QUADS, one, 0)
+
+    def through_event(i):
+        at = jnp.where(i == 0, 6, 7)
+
+        def one(g, carry):
+            stack[at, :, quad(g)] += mm_t(stack[i], w[i, quad(g), :])
+            return carry
+
+        lax.fori_loop(0, QUADS, one, 0)
+
+    def ev_start():
+        gctx[...] = jnp.zeros_like(gctx)
+        early[0].wait()
+        early[1].wait()
+        ig[...] = gs1[...]
+
+    def ev_near(g):
+        near_back_quad(g, gctx, near, q, kl_ref, b_ref, near, gb, gkl)
+
+    def blend_copy(pair):
+        return to_seq(gb.at[pair], land.at[me], b1s.at[pair], b1r.at[me], pair)
+
+    up, down = rim_copies(n, me, rim, gleft, gright, ms, mr)
+
+    def ev_blend():
+        for pair in range(PAIRS):
+
+            @pl.when(me != pair)
+            def _(pair=pair):
+                blend_copy(pair).start()
+
+        rim_start(n, me, up, down, gleft, gright)
+        for copy in late[:2]:
+            copy.start()
+
+    def mixed_copy(target):
+        return to_seq(cmsg.at[me], cmsg.at[me], b2s.at[target], b2r.at[me], target)
+
+    def ev_owner():
+        @pl.when(owner)
+        def _():
+            land[me] = gb[me]
+            for s in range(n):
+
+                @pl.when(me != s)
+                def _(s=s):
+                    to_seq(gb.at[0], land.at[s], b1s.at[0], b1r.at[s], s).wait_recv()
+
+            gblend = land[0]
+            for s in range(1, n):
+                gblend = gblend + land[s]
+            mixed = mx_ref[...]
+            gmixed = mm(gblend, zs_ref[NEWTON], TOP)
+            cmsg[me, 0:DH, :] = gmixed
+            dots = jnp.sum(gmixed * mixed, axis=0, keepdims=True)
+            cmsg[me, DH:MSG, :] = jnp.concatenate([dots, jnp.zeros((MSG - DH - 1, LANES), f32)], axis=0)
+            for t in range(n):
+
+                @pl.when(me != t)
+                def _(t=t):
+                    mixed_copy(t).start()
+
+            ng[...] = inverse_grad(gblend, mixed)
+            ncore[...] = jnp.zeros_like(ncore)
+
+        gl[...] = jnp.zeros_like(gl)
+
+    def ev_newton(step):
+        @pl.when(owner)
+        def _():
+            ng[...], ncore[...] = newton_back(
+                ng[...], ncore[...], core_ref[...], zs_ref[step], ps_ref[step], rs_ref[step], qs_ref[step]
+            )
+
+    def ev_core():
+        @pl.when(owner)
+        def _():
+            core_back(ng[...], ncore[...], core_ref[...], zs_ref[0], ql_ref, kl_ref, gl, me)
+
+    quarter = slots // 4
+
+    def ev_taps(part):
+        @pl.when(part == 0)
+        def _():
+            early[5].wait()
+            tap_scr[...] = jnp.zeros_like(tap_scr)
+
+        taps_grad_into(tap_scr, gctx, ext, quarter * (part + 1), quarter * part, False)
+
+        @pl.when(part == 3)
+        def _():
+            gtaps[...] = taps_sums(tap_scr)
+
+    def ev_conv(part):
+        @pl.when(part == 0)
+        def _():
+            rim_wait(n, me, up, down)
+            fill_extended(gext, gctx[...], gleft[...], gright[...], count)
+
+        conv_into(gv, gext, taps_ref, quarter * (part + 1), True, False, quarter * part)
+
+    def ev_mixed():
+        for pair in range(PAIRS):
+
+            @pl.when(me != pair)
+            def _(pair=pair):
+                to_seq(cmsg.at[pair], cmsg.at[pair], b2s.at[pair], b2r.at[pair], pair).wait_recv()
+
+        for copy in early[6:]:
+            copy.wait()
+
+    def ev_far(g):
+        far_back_quad(g, k, v, p, m_ref, b_ref, cmsg, ql_ref, p, gv, gql, True)
+
+    def ev_return():
+        land_parts(ret, gql[...] + gl[0], gkl[...] + gl[1])
+        for d in range(1, n):
+            target = lax.rem(me + d, n)
+            to_seq(ret.at[target], rland.at[me], rets.at[d], retr.at[me], target).start()
+        for copy in late[2:]:
+            copy.start()
+
+    def ev_own():
+        rland[me] = ret[me]
+        for d in range(1, n):
+            source = lax.rem(me + d, n)
+            to_seq(ret.at[0], rland.at[source], rets.at[d], retr.at[source], source).wait_recv()
+        total = rland[0]
+        for s in range(1, n):
+            total = total + rland[s]
+        own[...] = total
+        inv = inverse_lens(lens_ref, segs)
+        member = member_rows(ends, slots)
+        near[...] += t_mm(member, own[0] * inv)
+        p[...] += t_mm(member, own[1] * inv)
+        gv[...] = jnp.where(valid_rows(count, slots), gv[...], 0.0)
+        small0[0:1, :] = jnp.sum(near[...], axis=0, keepdims=True)
+        small0[1:2, :] = jnp.sum(gv[...], axis=0, keepdims=True)
 
     def small(i):
         return remote(sb.at[i], sl.at[i], ss.at[i], sr.at[i], partners[i])
 
-    pack_small(sb, *smalls)
-    small(0).start()
+    def ev_small(i):
+        if i == 0:
+            pack_small(sb, small0, small1_ref, small2_ref, dbi_ref, gtaps)
+        else:
+            small(i - 1).wait_recv()
+            sb[i] = sb[i - 1] + sl[i - 1]
+        if i < SMALL_STEPS:
+            small(i).start()
+
+    def at_tick(t, when, event):
+        @pl.when(t == when)
+        def _():
+            event()
+
+    def at_ticks(t, start, every, count, event):
+        after = t - start
+
+        @pl.when((after >= 0) & (after < every * count) & (lax.rem(after + every, every) == 0))
+        def _():
+            event(after // every)
 
     def tick(t, carry):
-        for i in range(1, SMALL_STEPS + 1):
-
-            @pl.when(t == 2 * i)
-            def _(i=i):
-                small(i - 1).wait_recv()
-                sb[i] = sb[i - 1] + sl[i - 1]
-                if i < SMALL_STEPS:
-                    small(i).start()
-
         for stage, run in reversed(list(enumerate(stages))):
-            k = t - lag[stage]
-
-            @pl.when((k >= 0) & (k < chunks))
-            def _(run=run, k=k):
-                run(k)
-
+            at = t - LAG[stage]
+
+            @pl.when((at >= 0) & (at < chunks))
+            def _(run=run, at=at):
+                run(at)
+
+        at_tick(t, 0, ev_start)
+        at_tick(t, 21, lambda: early[4].wait())
+        at_tick(t, 24, lambda: [copy.wait() for copy in late])
+        turn = jnp.where(t == 0, 0, (t - 23) // 3)
+
+        @pl.when((t == 0) | (t == 26) | (t == 29) | (t == 32))
+        def _():
+            through_event(turn)
+
+        @pl.when(t == 0)
+        def _():
+            rim[...] = rims_of(gctx[...], count)
+            early[2].wait()
+            early[3].wait()
+
+        at_ticks(t, 1, 1, QUADS, ev_near)
+        at_tick(t, 3, ev_blend)
+        at_ticks(t, 4, 1, 4, ev_taps)
+        at_tick(t, 7, ev_owner)
+        at_ticks(t, 8, 1, NEWTON, lambda i: ev_newton(NEWTON - 1 - i))
+        at_ticks(t, 9, 2, 4, ev_conv)
+        at_tick(t, 16, ev_core)
+        at_tick(t, 16, ev_mixed)
+        at_ticks(t, 16, 1, QUADS, ev_far)
+        at_tick(t, 19, ev_return)
+        at_tick(t, 23, ev_own)
+        filled = jnp.where(t == 21, 0, (t - 22) // 3)
+
+        @pl.when((t == 21) | (t == 25) | (t == 28) | (t == 31))
+        def _():
+            weight_event(filled)
+
+        at_tick(t, 33, lambda: pltpu.make_async_copy(ig, ig_hbm, ig_sem.at[0]).start())
+        for i in range(SMALL_STEPS + 1):
+            at_tick(t, SMALL_AT + 3 * i, partial(ev_small, i))
         return carry
 
-    lax.fori_loop(0, chunks + lag[-1], tick, 0)
+    lax.fori_loop(0, chunks + LAG[-1], tick, 0)
     for i in range(SMALL_STEPS):
         small(i).wait_send()
     so_ref[...] = sb[SMALL_STEPS]
-
-
-LAG = tuple(range(0, 2 * STAGES, 2))
-
-
-def reduce_grads(grads, smalls):
-    spans = []
-    at = 0
-    for g in grads:
-        spans.append((at, at + g.shape[0] // 2))
-        at += g.shape[0] // 2
+    pltpu.make_async_copy(ig, ig_hbm, ig_sem.at[0]).wait()
+    for pair in range(PAIRS):
+
+        @pl.when(me != pair)
+        def _(pair=pair):
+            blend_copy(pair).wait_send()
+
+    @pl.when(owner)
+    def _():
+        for t in range(n):
+
+            @pl.when(me != t)
+            def _(t=t):
+                mixed_copy(t).wait_send()
+
+    for d in range(1, n):
+        target = lax.rem(me + d, n)
+        to_seq(ret.at[target], rland.at[me], rets.at[d], retr.at[me], target).wait_send()
+
+
+def tail(lens, d_outer, d_inner, big, little, small1, small2, d_inner_bias):
+    slots, width = big[0].shape
+    segs = lens.shape[1]
+    spans = ((0, 12), (12, 24), (24, 36))
+    at = spans[-1][1]
+    n = SEQ_DEVICES
     dma = pltpu.SemaphoreType.DMA
     vm = lambda *dims: pltpu.VMEM(dims, f32)
+    rows = vm(slots, width)
+    anywhere = pl.BlockSpec(memory_space=pl.ANY)
+    two = dma((at, 2))
+    zsem = dma((at, 2, 3, 2))
+    one = dma((at,))
     return pl.pallas_call(
-        partial(reduce_kernel, tuple(spans), LAG),
-        in_specs=[pl.BlockSpec(memory_space=pl.ANY)] * len(grads) + [whole()] * 5,
-        out_specs=[pl.BlockSpec(memory_space=pl.ANY), whole()],
-        out_shape=[shape(2, at, STRIP, LANES), shape(SMALL_ROWS, LANES)],
+        partial(tail_kernel, spans),
+        in_specs=[smem()] + [anywhere] * (2 + len(big)) + [whole()] * (len(little) + 3),
+        out_specs=[anywhere, whole(), anywhere],
+        out_shape=[shape(2, at, STRIP, LANES), shape(SMALL_ROWS, LANES), shape(slots, width)],
         scratch_shapes=[
-            vm(at, STRIP, LANES), vm(at, STRIP, LANES), vm(at, 2, PART, LANES), vm(at, 2, 2, 3, Z_ROWS, LANES),
-            vm(at, 2, OWN, LANES), vm(SMALL_STEPS + 1, SMALL_ROWS, LANES), vm(SMALL_STEPS, SMALL_ROWS, LANES),
-            dma((at,)), dma((at, 2)), dma((at,)), dma((at,)), dma((at, 2)), dma((at, 2)),
-            dma((at, 2, 3, 2)), dma((at, 2, 3, 2)), dma((at, 2)), dma((at, 2)), dma((at, 2)), dma((at, 2)),
-            dma((at, 2, 3, 2)), dma((at, 2, 3, 2)), dma((at, 2)), dma((at, 2)), dma((at,)), dma((at,)),
-            dma((SMALL_STEPS,)), dma((SMALL_STEPS,)),
+            vm(RING_ACC, STRIP, LANES), vm(RING_LC, STRIP, LANES), vm(RING_LC, 2, PART, LANES),
+            vm(RING_Z, 2, 2, 3, Z_ROWS, LANES), vm(RING_LC, 2, OWN, LANES),
+            vm(SMALL_STEPS + 1, SMALL_ROWS, LANES), vm(SMALL_STEPS, SMALL_ROWS, LANES), vm(24, STRIP, LANES),
+            vm(8, slots, width), vm(4, width, width), vm(slots + 40, width), rows, rows,
+            vm(slots + 40, width), vm(CONV, 8, width), vm(40, LANES), vm(8, width),
+            vm(PAIRS, DH, LANES), vm(2 * RIM, width), vm(DH, width), vm(DH, width), vm(2, DH, width),
+            vm(n, DH, LANES), vm(PAIRS, MSG, LANES), vm(RIM, width), vm(RIM, width), vm(LANES, LANES), vm(LANES, LANES),
+            vm(n, 2, segs, width), vm(n, 2, segs, width), vm(2, segs, width),
+            dma((13,)), dma((1,)), dma((PAIRS,)), dma((n,)), dma((n,)), dma((n,)), dma((2,)), dma((2,)),
+            dma((n,)), dma((n,)), dma((SMALL_STEPS,)), dma((SMALL_STEPS,)),
+            one, two, one, one, two, two, zsem, zsem, two, two, two, two, zsem, zsem, two, two, one, one,
         ],
         compiler_params=params(collective_id=5, has_side_effects=True),
-        name="reduce_grads",
-    )(*grads, *smalls)
-
-
-def sum_on_block(grads, smalls, shapes):
-    summed, packed = reduce_grads(grads, smalls)
-    spans = []
-    at = 0
-    for g in grads:
-        spans.append((at, at + g.shape[0] // 2))
-        at += g.shape[0] // 2
-    return place_strips(summed, packed, spans, shapes)
+        name="tail",
+    )(lens, d_outer, d_inner, *big, *little, small1, small2, d_inner_bias)
 
 
 def unstrip(strips):
@@ -1318,7 +1672,7 @@
         across = out.shape[1] // LANES
         for c in range(2):
             for k in range(lo, hi):
-                at = c * (hi - lo) + k - lo
+                at = 2 * (k - lo) + c
                 rows = pl.ds(at // across * STRIP, STRIP)
                 cols = pl.ds(at % across * LANES, LANES)
                 slot = len(moves) % PLACE_SLOTS
@@ -1373,7 +1727,7 @@
     kl = lands[:, 1].reshape(DH, width)
     parts, raised, tops = far_local(lens, k, v, ql)
     b, *saved = far_exchange(n, parts, ql, kl)
-    near, ctx, h1, u1, inv1 = attend(
+    near, ctx, h1, u1, inv1, ext = attend(
         lens, q, v, kl, b, left, right, taps, x, output_weight, output_bias, first_gain, first_bias
     )
     pre, layer_out, gs2, small2 = ffn_forward(
@@ -1382,21 +1736,24 @@
     d_outer, d_inner, gs1, d_inner_bias, small1 = ffn_backward(
         h1, gs2, pre, inner_weight, outer_weight, u1, inv1, first_gain
     )
-    gctx, gqn, gblend, gkl, grim = near_back(lens, gs1, output_weight, near, q, kl, b)
-    c, gleft, gright, gl = blend_exchange(n, gblend, grim, ql, kl, saved)
-    gkf, gvf, back = far_back(n, lens, k, v, raised, tops, b, c, ql, gkl, gl)
-    own = land_return(n, back)
-    gvc, gtaps, d_output = conv_back(lens, v, left, right, gctx, gleft, gright, taps, ctx, gs1)
-    input_grad, d_query, d_key, d_value, small0 = project_back(
-        lens, x, gs1, gqn, gkf, gvc, gvf, own, query_weight, key_weight, value_weight
-    )
-    grads = [d_outer, d_inner, d_output, d_query, d_key, d_value]
-    smalls = [small0, small1, small2, d_inner_bias, gtaps]
     weights = [outer_weight, inner_weight, output_weight, query_weight, key_weight, value_weight]
-    if n == 8 and lax.axis_size("dp") == 4:
-        sums = sum_on_block(grads, smalls, [w.shape for w in weights])
+    if n == SEQ_DEVICES and lax.axis_size("dp") == 4:
+        big = [gs1, output_weight, near, q, ctx, ext, k, v, raised, x, query_weight, key_weight, value_weight]
+        little = [tops, b, ql, kl, *saved, taps]
+        summed, packed, input_grad = tail(lens, d_outer, d_inner, big, little, small1, small2, d_inner_bias)
+        spans = ((0, 12), (12, 24), (24, 27), (27, 30), (30, 33), (33, 36))
+        sums = place_strips(summed, packed, spans, [w.shape for w in weights])
     else:
-        sums = sum_plain(grads + smalls)
+        gctx, gqn, gblend, gkl, grim = near_back(lens, gs1, output_weight, near, q, kl, b)
+        c, gleft, gright, gl = blend_exchange(n, gblend, grim, ql, kl, saved)
+        gkf, gvf, back = far_back(n, lens, k, v, raised, tops, b, c, ql, gkl, gl)
+        own = land_return(n, back)
+        gvc, gtaps, d_output = conv_back(lens, v, left, right, gctx, gleft, gright, taps, ctx, gs1)
+        input_grad, d_query, d_key, d_value, small0 = project_back(
+            lens, x, gs1, gqn, gkf, gvc, gvf, own, query_weight, key_weight, value_weight
+        )
+        grads = [d_outer, d_inner, d_output, d_query, d_key, d_value]
+        sums = sum_plain(grads + [small0, small1, small2, d_inner_bias, gtaps])
         small = sums[6:]
         sums = (
             [unstrip_tall(sums[0], width // LANES)] + [unstrip(s) for s in sums[1:6]]

time: 498 us -> 419 us (0.84); the launches traced: 491 us -> 419 us
  Pallas kernels: 485 us -> 412 us
    pallas_call x8 -> x2, Pallas kernels: 336 us -> 257 us  [the longest x1 245 us: tail(): pl.pallas_call(partial(tail_kernel, spans), in_specs=[smem()] + [anywhere...]
where the time goes in v2:
time: 419 us
  Pallas kernels  412 us (98%)
  local copies, waits for them, and re-layouts  6.01 us (1%)
    pallas_call x1, Pallas kernels, tail(): pl.pallas_call(partial(tail_kernel, spans), in_specs=[smem()] + [anywhere...  245 us
    pallas_call x1, Pallas kernels, ffn_backward(): pl.pallas_call(backward_kernel, grid=(inner // width,), in_specs=[const(s...  44 us
    pallas_call x1, Pallas kernels, ffn_forward(): pl.pallas_call(forward_kernel, grid=(inner // width,), in_specs=[smem(),...  26.8 us
    pallas_call x1, Pallas kernels, attend(): pl.pallas_call(attend_kernel, in_specs=[smem()] + [whole()] * 12, out_spe...  22.7 us
    pallas_call x1, Pallas kernels, place_strips(): pl.pallas_call(partial(place_strips_kernel, spans), in_specs=[anywhere, w...  21 us
    pallas_call x1, Pallas kernels, far_exchange(): pl.pallas_call(partial(far_exchange_kernel, n), in_specs=[whole()] * 3, o...  19.6 us
    pallas_call x1, Pallas kernels, land_exchange(): pl.pallas_call(partial(land_exchange_kernel, n), in_specs=[whole()] * 2,...  14.3 us
    pallas_call x1, Pallas kernels, project(): pl.pallas_call(project_kernel, in_specs=[smem(), whole()] + [anywhere] *...  12.4 us

profile of v2, /device:TPU:0, one launch (start us, length us, event | category | flops | bytes accessed | tf_op | source)
XLA Modules:
  0.0 418.7 jit_solution(7861970519340987940)
XLA Ops:
  0.7 0.8 copy.39
  1.4 0.1 broadcast_in_dim.3
  1.6 0.8 reshape.55.taps_ref
  2.3 12.4 %project.1 = (f32[512,768]{1,0:T(8,128)}, f32[512,768]{1,0:T(8,128)}, f32[512,768]{1,0:T(8,128)}, f32[2,8,768]{2,1,0:T(8,128)}, f32[32,768]{1,0:T(8,128)}) custom-call(s32[1,8]{1,0:T(1,128)} %lens_ref.9, f32[512,768]{1,0:T(8,128)} %bitcast.9, f32[768,768]{1,0:T(8,128)} %wq_hbm.3, f32[768,768]{1,0:T(8,128)} %wk_hbm.3, f32[768,768]{1,0:T(8,128)} %wv_hbm.3, ...), custom_call_target="tpu_custom_call" | custom-call | tf_op jit(solution)/shard_map/project/pallas_call | solution.py:233
  14.7 14.3 %land_exchange.1 = (f32[8,2,8,768]{3,2,1,0:T(8,128)}, f32[16,768]{1,0:T(8,128)}, f32[16,768]{1,0:T(8,128)}) custom-call(f32[2,8,768]{2,1,0:T(8,128)} %get-tuple-element.72.mine_ref, f32[32,768]{1,0:T(8,128)} %get-tuple-element.73.rim_ref), custom_call_target="tpu_custom_call" | custom-call | tf_op jit(solution)/shard_map/land_exchange/pallas_call | solution.py:328
  29.0 1.8 slice_bitcast_fusion
  30.8 6.5 %far_local.1 = (f32[6,72,128]{2,1,0:T(8,128)}, f32[512,768]{1,0:T(8,128)}, f32[1,768]{1,0:T(1,128)}) custom-call(s32[1,8]{1,0:T(1,128)} %lens_ref.9, f32[512,768]{1,0:T(8,128)} %get-tuple-element.75.k_ref.k_hbm, f32[512,768]{1,0:T(8,128)} %get-tuple-element.71.v_ref.v_hbm, f32[64,768]{1,0:T(8,128)} %get-tuple-element.158.ql_ref), custom_call_target="tpu_custom_call" | custom-call | tf_op jit(solution)/shard_map/far_local/pallas_call | solution.py:636
  37.3 19.6 %far_exchange.1 = (f32[6,72,128]{2,1,0:T(8,128)}, f32[128,128]{1,0:T(8,128)}, f32[7,128,128]{2,1,0:T(8,128)}, f32[6,128,128]{2,1,0:T(8,128)}, f32[6,128,128]{2,1...) custom-call(f32[6,72,128]{2,1,0:T(8,128)} %get-tuple-element.76.f_ref, f32[64,768]{1,0:T(8,128)} %get-tuple-element.158.ql_ref, ...), custom_call_target="tpu_custom_call" | custom-call | tf_op jit(solution)/shard_map/far_exchange/pallas_call | solution.py:446
  57.0 22.7 %attend.1 = (f32[512,768]{1,0:T(8,128)}, f32[512,768]{1,0:T(8,128)}, f32[512,768]{1,0:T(8,128)}, f32[512,768]{1,0:T(8,128)}, f32[512,1]{1,0:T(8,128)}, /*index=5*/f32[552,768]{1,0:T(8,128)}) custom-call(s32[1,8]{1,0:T(1,128)} %lens_ref.9, f32[512,768]{1,0:T(8,128)} %get-tuple-element.70.q_ref.q_hbm, f32[512,768]{1,0:T(8,128)} %get-tuple-element.71.v_ref.v_hbm, ...), custom_call_target="tpu_custom_call" | custom-call | tf_op jit(solution)/shard_map/attend/pallas_call | solution.py:711
  79.7 26.8 %ffn_forward.1 = (f32[512,3072]{1,0:T(8,128)}, f32[512,768]{1,0:T(8,128)}, f32[512,768]{1,0:T(8,128)}, f32[8,768]{1,0:T(8,128)}) custom-call(s32[1,8]{1,0:T(1,128)} %lens_ref.9, f32[512,768]{1,0:T(8,128)} %get-tuple-element.80.h1_ref, f32[768,3072]{1,0:T(8,128)} %wi_ref.3, f32[1,3072]{1,0:T(1,128)} %bitcast.14, f32[3072,768]{1,0:T(8,128)} %wo_ref.5, ...), custom_call_target="tpu_custom_call" | custom-call | tf_op jit(solution)/shard_map/ffn_forward/pallas_call | solution.py:773
  106.5 44.0 %ffn_backward.1 = (f32[24,768,128]{2,1,0:T(8,128)}, f32[24,768,128]{2,1,0:T(8,128)}, f32[512,768]{1,0:T(8,128)}, f32[1,3072]{1,0:T(1,128)}, f32[8,768]{1,0:T(8,128)}) custom-call(f32[512,768]{1,0:T(8,128)} %get-tuple-element.80.h1_ref, f32[512,768]{1,0:T(8,128)} %get-tuple-element.82.gs2_ref, f32[512,3072]{1,0:T(8,128)} %get-tuple-element.83.pre_ref, ...), custom_call_target="tpu_custom_call" | custom-call | tf_op jit(solution)/shard_map/ffn_backward/pallas_call | solution.py:852
  150.5 244.6 %tail.1 = (f32[2,36,768,128]{3,2,1,0:T(8,128)}, f32[112,128]{1,0:T(8,128)}, f32[512,768]{1,0:T(8,128)}) custom-call(s32[1,8]{1,0:T(1,128)} %lens_ref.9, f32[24,768,128]{2,1,0:T(8,128)} %get-tuple-element.86.dout_ref, f32[24,768,128]{2,1,0:T(8,128)} %get-tuple-element.87.din_ref, f32[512,768]{1,0:T(8,128)} %get-tuple-element.88.gs1_hbm, f32[768,768]{1,0:T(8,128)} %wo_hbm.1, ...), custom_call_target="tpu_custom_call" | custom-call | tf_op jit(solution)/shard_map/tail/pallas_call | solution.py:1629
  395.1 0.0 copy-start
  395.1 21.0 %place_strips.1 = (f32[3072,768]{1,0:T(8,128)}, f32[768,3072]{1,0:T(8,128)}, f32[768,768]{1,0:T(8,128)}, f32[768,768]{1,0:T(8,128)}, f32[768,768]{1,0:T(8,128)},...) custom-call(f32[2,36,768,128]{3,2,1,0:T(8,128)} %get-tuple-element.1, ...), custom_call_target="tpu_custom_call" | custom-call | tf_op jit(solution)/shard_map/place_strips/pallas_call | solution.py:1701
  416.1 1.4 copy.40
  417.5 0.0 copy-done
  417.5 1.1 copy.42
Async XLA Ops:
  395.1 22.4 %copy-start = (f32[512,768]{1,0:T(8,128)S(1)}, f32[512,768]{1,0:T(8,128)}, u32[]{:S(2)}) copy-start(f32[512,768]{1,0:T(8,128)} %get-tuple-element.103) | copy-start | bytes 4718596

commit v3 on v2

--- a/solution.py
+++ b/solution.py
@@ -1116,9 +1116,9 @@
     outs[-1][...] = s_ref[at : at + CONV, :HEADS]
 
 
-def reduce_stages(spans, grads, o_ref, bufs, sems):
-    acc, lc, l1, lz, l3 = bufs
-    local, out_local, cs, cr, s1, r1, zs, zr, s3, r3, s4, r4, gs, gr, s5, r5, es, er = sems
+def reduce_stages(gw, o_ref, bufs, sems):
+    acc, lc, l1, mid, lz, l3, ag = bufs
+    cs, cr, s1, r1, ms, zr, r3, r4, gs, gr, r5, keep, es, er = sems
     seq = lax.axis_index("seq")
     dp = lax.axis_index("dp")
     z = seq // 2
@@ -1140,170 +1140,130 @@
 
     aligned = lambda at: pl.multiple_of(at, 8)
     slot = lambda ref, k: lax.rem(k, ref.shape[0])
-    a1 = x * PART
-    b1 = HALF + y * PART
-    firsts = ((0, a1, (1 - x) * PART, by_x), (1, b1, HALF + (1 - y) * PART, by_y))
-    starts = (a1, b1)
-    az = a1 + z * Z_ROWS
-    bz = b1 + z * Z_ROWS
-    thirds = (
-        (0, az + y * OWN, az + (1 - y) * OWN, by_y),
-        (1, bz + x * OWN, bz + (1 - x) * OWN, by_x),
-    )
-
-    def rows(ref, k, at, size):
-        return ref.at[k, pl.ds(aligned(at), size)]
-
-    def acc_rows(k, at, size):
-        return rows(acc, slot(acc, k), at, size)
-
-    def core_copies(k, g, lo):
-        mine = pltpu.make_async_copy(g.at[2 * (k - lo) + c], acc.at[slot(acc, k)], local.at[k])
-        other = remote(g.at[2 * (k - lo) + 1 - c], lc.at[slot(lc, k)], cs.at[k], cr.at[k], by_core)
-        return mine, other
+    starts = (x * PART, HALF + y * PART)
+    others = ((1 - x) * PART, HALF + (1 - y) * PART)
+    own_rows = (pl.ds(aligned(y * OWN), OWN), pl.ds(aligned(x * OWN), OWN))
+    other_rows = (pl.ds(aligned((1 - y) * OWN), OWN), pl.ds(aligned((1 - x) * OWN), OWN))
+    first_to = (by_x, by_y)
+    third_to = (by_y, by_x)
+    ways = ((0, z, right), (1, zb, left))
+
+    def bytes_of(rows, send, recv, pieces=1):
+        part = lc.at[pl.ds(0, pieces), pl.ds(0, rows // pieces)]
+        return remote(part, part, send, recv, by_core)
+
+    def strip(k):
+        return lax.rem(k // 3, GW_SLOTS) * PAIRS + 2 * lax.rem(k, 3)
+
+    def core_copy(k):
+        return remote(gw.at[strip(k) + 1 - c], lc.at[slot(lc, k)], cs.at[k], cr.at[k], by_core)
 
     def core_out(k):
-        for g, (lo, hi) in zip(grads, spans):
-
-            @pl.when((k >= lo) & (k < hi))
-            def _(g=g, lo=lo):
-                for copy in core_copies(k, g, lo):
-                    copy.start()
-
-    def first(k, j):
-        _, _, other, target = firsts[j]
-        return remote(acc_rows(k, other, PART), l1.at[slot(l1, k), j], s1.at[k, j], r1.at[k, j], target)
+        core_copy(k).start()
 
     def first_out(k):
-        mine, other = core_copies(k, grads[0], k)
-        mine.wait()
-        other.wait_recv()
-        acc[slot(acc, k)] += lc[slot(lc, k)]
+        core_copy(k).wait()
+        at = slot(acc, k)
+        acc[at] = gw[strip(k) + c] + lc[slot(lc, k)]
         for j in range(2):
-            first(k, j).start()
-
-    def z_copy(k, j, way, step, block):
-        target = right if way == 0 else left
-        return remote(
-            acc_rows(k, starts[j] + block * Z_ROWS, Z_ROWS), lz.at[slot(lz, k), way, j, step],
-            zs.at[k, way, step, j], zr.at[k, way, step, j], target,
-        )
+            remote(
+                acc.at[at, pl.ds(aligned(others[j]), PART)], l1.at[slot(l1, k), j], s1.at[k], r1.at[k], first_to[j]
+            ).start()
+
+    def z_copy(k, way, step, block, target):
+        return remote(mid.at[slot(mid, k), block], lz.at[slot(lz, k), way, step], ms.at[k], zr.at[k, way, step], target)
 
     def z_out(k, step):
         if step == 0:
-            for j, mine, _, _ in firsts:
-                first(k, j).wait_recv()
-                acc[slot(acc, k), pl.ds(aligned(mine), PART)] += l1[slot(l1, k), j]
-        for way, at in ((0, z), (1, zb)):
+            bytes_of(HALF, s1.at[k], r1.at[k]).wait()
+            for j in range(2):
+                for block in range(4):
+                    here = pl.ds(aligned(starts[j] + block * Z_ROWS), Z_ROWS)
+                    there = pl.ds(block * Z_ROWS, Z_ROWS)
+                    mid[slot(mid, k), block, j] = acc[slot(acc, k), here] + l1[slot(l1, k), j, there]
+        for way, at, target in ways:
             block = 3 - step + z if way == 0 else step - zb
             if step > 0:
 
                 @pl.when((at > 0) & (at <= step))
-                def _(way=way, block=block):
-                    for j in range(2):
-                        z_copy(k, j, way, step - 1, 0).wait_recv()
-                        here = (slot(acc, k), pl.ds(aligned(starts[j] + block * Z_ROWS), Z_ROWS))
-                        acc[here] += lz[slot(lz, k), way, j, step - 1]
+                def _(way=way, block=block, target=target):
+                    z_copy(k, way, step - 1, 0, target).wait_recv()
+                    mid[slot(mid, k), block] += lz[slot(lz, k), way, step - 1]
 
             if step < 3:
 
                 @pl.when((at <= step) & (at < 3))
-                def _(way=way, block=block):
-                    for j in range(2):
-                        z_copy(k, j, way, step, block).start()
-
-    def third(k, j):
-        _, _, other, target = thirds[j]
-        return remote(acc_rows(k, other, OWN), l3.at[slot(l3, k), j], s3.at[k, j], r3.at[k, j], target)
+                def _(way=way, block=block, target=target):
+                    z_copy(k, way, step, block, target).start()
 
     def third_out(k):
         z_out(k, 3)
         for j in range(2):
-            third(k, j).start()
-
-    def back_third(k, j):
-        _, mine, _, target = thirds[j]
-        return remote(acc_rows(k, mine, OWN), rows(o_ref.at[c], k, mine, OWN), s4.at[k, j], r4.at[k, j], target)
-
-    def keep(k, j):
-        mine = thirds[j][1]
-        return pltpu.make_async_copy(acc_rows(k, mine, OWN), rows(o_ref.at[c], k, mine, OWN), out_local.at[k, j])
+            remote(
+                mid.at[slot(mid, k), z, j, other_rows[j]], l3.at[slot(l3, k), j], ms.at[k], r3.at[k], third_to[j]
+            ).start()
 
     def back_third_out(k):
-        for j, mine, _, _ in thirds:
-            third(k, j).wait_recv()
-            acc[slot(acc, k), pl.ds(aligned(mine), OWN)] += l3[slot(l3, k), j]
+        bytes_of(2 * OWN, ms.at[k], r3.at[k]).wait_recv()
         for j in range(2):
-            back_third(k, j).start()
-            keep(k, j).start()
-
-    def back_z(k, j, way, step, block):
-        target = right if way == 0 else left
-        part = rows(o_ref.at[c], k, starts[j] + block * Z_ROWS, Z_ROWS)
-        return remote(part, part, gs.at[k, way, step, j], gr.at[k, way, step, j], target)
+            ag[slot(ag, k), z, j, own_rows[j]] = mid[slot(mid, k), z, j, own_rows[j]] + l3[slot(l3, k), j]
+            part = ag.at[slot(ag, k), z, j, own_rows[j]]
+            remote(part, part, gs.at[k], r4.at[k], third_to[j]).start()
+
+    def back_z(k, way, step, block, target):
+        part = ag.at[slot(ag, k), block]
+        return remote(part, part, gs.at[k], gr.at[k, way, step], target)
 
     def back_z_out(k, step):
         if step == 0:
-            core_copies(k, grads[0], k)[1].wait_send()
-            for j in range(2):
-                keep(k, j).wait()
-                first(k, j).wait_send()
-                third(k, j).wait_send()
-                back_third(k, j).wait()
-            for s in range(3):
-                for way, at in ((0, z), (1, zb)):
-
-                    @pl.when((at <= s) & (at < 3))
-                    def _(way=way, s=s):
-                        for j in range(2):
-                            z_copy(k, j, way, s, 0).wait_send()
-
-        for way, at in ((0, z), (1, zb)):
+            bytes_of(6 * Z_ROWS + 2 * OWN, ms.at[k], r3.at[k]).wait_send()
+            bytes_of(2 * OWN, gs.at[k], r4.at[k]).wait_recv()
+        for way, at, target in ways:
             block = z - step if way == 0 else z + step
             if step > 0:
 
                 @pl.when(at >= step)
-                def _(way=way):
-                    for j in range(2):
-                        back_z(k, j, way, step - 1, 0).wait_recv()
+                def _(way=way, target=target):
+                    back_z(k, way, step - 1, 0, target).wait_recv()
 
             if step < 3:
 
                 @pl.when((at >= step) & (at < 3))
-                def _(way=way, block=block):
-                    for j in range(2):
-                        back_z(k, j, way, step, block).start()
-
-    def back_first(k, j):
-        _, mine, _, target = firsts[j]
-        part = rows(o_ref.at[c], k, mine, PART)
-        return remote(part, part, s5.at[k, j], r5.at[k, j], target)
+                def _(way=way, block=block, target=target):
+                    back_z(k, way, step, block, target).start()
+
+    blocks = (pl.ds(x * 4, 4), pl.ds(8 + y * 4, 4))
+
+    def keep_copy(k, j):
+        return pltpu.make_async_copy(ag.at[slot(ag, k), :, j], o_ref.at[c, k, blocks[j]], keep.at[k, j])
 
     def back_first_out(k):
         back_z_out(k, 3)
         for j in range(2):
-            back_first(k, j).start()
+            remote(ag.at[slot(ag, k), :, j], o_ref.at[c, k, blocks[j]], gs.at[k], r5.at[k], first_to[j]).start()
+            keep_copy(k, j).start()
 
     def back_core(k):
         part = o_ref.at[c, k]
         return remote(part, part, es.at[k], er.at[k], by_core)
 
     def back_core_out(k):
+        bytes_of(HALF, gs.at[k], r5.at[k]).wait_recv()
         for j in range(2):
-            back_first(k, j).wait_recv()
+            keep_copy(k, j).wait()
+
+        @pl.when((z == 0) | (z == 3))
+        def _():
+            bytes_of(2 * OWN + 2 * Z_ROWS + HALF, gs.at[k], r5.at[k]).wait_send()
+
+        @pl.when((z > 0) & (z < 3))
+        def _():
+            bytes_of(2 * OWN + 10 * Z_ROWS + HALF, gs.at[k], r5.at[k], 2).wait_send()
+
         back_core(k).start()
 
     def finish(k):
         back_core(k).wait()
-        for j in range(2):
-            back_first(k, j).wait_send()
-        for step in range(3):
-            for way, at in ((0, z), (1, zb)):
-
-                @pl.when((at >= step) & (at < 3))
-                def _(way=way, step=step):
-                    for j in range(2):
-                        back_z(k, j, way, step, 0).wait_send()
 
     stages = [
         core_out, first_out, partial(z_out, step=0), partial(z_out, step=1), partial(z_out, step=2), third_out,
@@ -1314,11 +1274,33 @@
 
 
 LAG = tuple(range(0, 2 * STAGES, 2))
-RING_ACC = 16
+CHUNKS = 36
+GW_SLOTS = 4
+RING_ACC = 6
 RING_LC = 4
+RING_MID = 12
 RING_Z = 6
+RING_AG = 16
 SEQ_DEVICES = 8
-SMALL_AT = 24
+SMALL_AT = 36
+ENTER = 2
+HELD = 30
+GAP = 2
+GS1, GS2, H1, ACT, GPRE, PRE, _, U1, GCTX, IG = range(10)
+GV, PROB, CTX, KEYS, NEAR, QUERY, VALS = GS2, H1, ACT, GPRE, PRE, PRE + 1, U1
+FFN_AT = (0, 4, 8, 13)
+GS1_AT = 17
+OUTPUT_AT, VALUE_AT, QUERY_AT, KEY_AT = 21, 28, 32, 33
+INPUT_AT = (34, 35, 36)
+
+
+def pick(t, table):
+    value = jnp.int32(0)
+    hit = t < 0
+    for when, what in table.items():
+        value = jnp.where(t == when, what, value)
+        hit = hit | (t == when)
+    return value, hit
 
 
 def greet_block():
@@ -1338,64 +1320,113 @@
 
 
 def tail_kernel(
-    spans,
-    lens_ref, dout_ref, din_ref, gs1_hbm, wo_hbm, near_hbm, q_hbm, ctx_hbm, ext_hbm, k_hbm, v_hbm, p_hbm, x_hbm,
-    wq_hbm, wk_hbm, wv_hbm,
-    m_ref, b_ref, ql_ref, kl_ref, core_ref, zs_ref, ps_ref, rs_ref, qs_ref, mx_ref, taps_ref,
-    small1_ref, small2_ref, dbi_ref,
+    lens_ref, gs2_hbm, h1_hbm, u1_hbm, pre_hbm, wout_hbm, win_hbm, wo_hbm, near_hbm, q_hbm, ctx_hbm, ext_hbm,
+    k_hbm, v_hbm, p_hbm, x_hbm, wq_hbm, wk_hbm, wv_hbm,
+    inv1_ref, g1_ref, m_ref, b_ref, ql_ref, kl_ref, core_ref, zs_ref, ps_ref, rs_ref, qs_ref, mx_ref, taps_ref, small2_ref,
     o_ref, so_ref, ig_hbm,
-    acc, lc, l1, lz, l3, sb, sl, gw,
-    stack, w, ext, k, v, gext, tap_scr, gtaps, small0,
+    acc, lc, l1, mid, lz, l3, ag, sb, sl, gw,
+    stack, w, ext, gext, tap_scr, gtaps, small0, small1, dbi,
     gb, rim, gkl, gql, gl, land, cmsg, gleft, gright, ng, ncore, ret, rland, own,
     loads, ig_sem, b1s, b1r, b2s, b2r, ms, mr, rets, retr, ss, sr,
     *sems,
 ):
     n = SEQ_DEVICES
-    chunks = spans[-1][1]
-    slots = k.shape[0]
+    _, slots, width = stack.shape
     segs = own.shape[1]
-    gs1, near, p, gv, ctx, q, gctx, ig = [stack.at[i] for i in range(8)]
-
-    def load(i, src, dst):
-        return pltpu.make_async_copy(src, dst, loads.at[i])
-
-    early = [
-        load(0, gs1_hbm, gs1), load(1, wo_hbm, w.at[0]), load(2, near_hbm, near), load(3, q_hbm, q), load(4, ctx_hbm, ctx),
-        load(5, ext_hbm, ext), load(6, v_hbm, v), load(7, p_hbm, p), load(8, k_hbm, k),
+    gs1, gv, p, ctx, k, near, q, v, gctx, ig = [
+        stack.at[i] for i in (GS1, GV, PROB, CTX, KEYS, NEAR, QUERY, VALS, GCTX, IG)
     ]
-    late = [load(9, x_hbm, q), load(10, wq_hbm, w.at[1]), load(11, wk_hbm, w.at[2]), load(12, wv_hbm, w.at[3])]
-    for copy in early:
+    moves = []
+
+    def load(src, dst):
+        moves.append(pltpu.make_async_copy(src, dst, loads.at[len(moves)]))
+        return moves[-1]
+
+    load_gs2 = load(gs2_hbm, stack.at[GS2])
+    load_w = []
+    load_pre = []
+    for j in range(4):
+        part = pl.ds(j * width, width)
+        load_w.append(load(wout_hbm.at[part, :], w.at[2 * j % 4]))
+        load_w.append(load(win_hbm.at[:, part], w.at[(2 * j + 1) % 4]))
+        load_pre.append(load(pre_hbm.at[:, part], stack.at[PRE + j % 2]))
+    for i, hbm in enumerate((wo_hbm, wv_hbm, wq_hbm, wk_hbm)):
+        load_w.append(load(hbm, w.at[i]))
+    load_h1, load_u1, load_ext = load(h1_hbm, stack.at[H1]), load(u1_hbm, stack.at[U1]), load(ext_hbm, ext)
+    load_near, load_q, load_ctx = load(near_hbm, near), load(q_hbm, q), load(ctx_hbm, ctx)
+    load_p, load_k, load_v, load_x = load(p_hbm, p), load(k_hbm, k), load(v_hbm, v), load(x_hbm, q)
+    a0, a1, a2, a3 = FFN_AT
+    starting = [
+        (a0 + 1, load_w[4]), (a0 + 1, load_pre[2]), (a0 + 4, load_w[5]), (a1 + 1, load_w[6]), (a1 + 1, load_pre[3]),
+        (a1 + 4, load_w[7]), (a2 + 1, load_w[8]), (a2 + 1, load_near), (a2 + 4, load_w[9]), (a3 + 1, load_w[10]),
+        (a3 + 1, load_q), (a3 + 2, load_ctx), (a3 + 3, load_p), (a3 + 4, load_w[11]), (a3 + 4, load_k), (a3 + 4, load_v),
+        (GS1_AT + 4, load_x),
+    ]
+    waiting = [
+        (a0, load_gs2), (a0 + 2, load_h1), (a3 + 3, load_u1), (GS1_AT, load_w[8]), (GS1_AT + 1, load_near),
+        (GS1_AT + 1, load_q), (OUTPUT_AT, load_ctx), (VALUE_AT, load_x),
+    ]
+    for j in range(4):
+        waiting += [(FFN_AT[j], load_w[2 * j]), (FFN_AT[j], load_pre[j]), (FFN_AT[j] + 3, load_w[2 * j + 1])]
+    for i in range(3):
+        waiting.append((INPUT_AT[i], load_w[9 + i]))
+    for copy in (load_gs2, load_w[0], load_pre[0], load_h1, load_w[1], load_pre[1], load_w[2], load_w[3], load_u1, load_ext):
         copy.start()
     me = greet_block()
     owner = me < PAIRS
-    stages, partners, remote = reduce_stages(spans, (dout_ref, din_ref, gw), o_ref, (acc, lc, l1, lz, l3), sems)
+    stages, partners, remote = reduce_stages(gw, o_ref, (acc, lc, l1, mid, lz, l3, ag), sems)
     ends = seg_ends(lens_ref, segs)
     count = ends[-1]
 
-    def weight_event(i):
-        left = jnp.where(i == 0, 4, 5)
-
+    def weight_event(e, left, right):
         def one(g, carry):
-            block = t_mm(stack[left, :, quad(g)], stack[i])
-            put_strips(gw, block, quad(g), i * PAIRS)
+            block = t_mm(stack[left, :, quad(g)], stack[right])
+            put_strips(gw, block, quad(g), lax.rem(e, GW_SLOTS) * PAIRS)
             return carry
 
         lax.fori_loop(0, QUADS, one, 0)
 
-    def through_event(i):
-        at = jnp.where(i == 0, 6, 7)
-
+    def through_event(source, target, weight):
         def one(g, carry):
-            stack[at, :, quad(g)] += mm_t(stack[i], w[i, quad(g), :])
+            stack[target, :, quad(g)] += mm_t(stack[source], w[weight, quad(g), :])
             return carry
 
         lax.fori_loop(0, QUADS, one, 0)
 
-    def ev_start():
-        gctx[...] = jnp.zeros_like(gctx)
-        early[0].wait()
-        early[1].wait()
-        ig[...] = gs1[...]
+    def inner_event(j):
+        @pl.when(j == 0)
+        def _():
+            stack[GS1] = stack[GS2]
+
+        at = PRE + lax.rem(j, 2)
+        weight = lax.rem(2 * j, 4)
+
+        def one(g, carry):
+            cols = quad(g)
+            pre = stack[at, :, cols]
+            phi_big = 0.5 * (1.0 + lax.erf(pre * ROOT_HALF))
+            slope = phi_big + pre * (INV_ROOT_TAU * jnp.exp(-0.5 * pre * pre))
+            gpre = mm_t(stack[GS2], w[weight, cols, :]) * slope
+            stack[GPRE, :, cols] = gpre
+            stack[ACT, :, cols] = pre * phi_big
+            dbi[:, pl.ds(pl.multiple_of(j * width + g * QUAD, QUAD), QUAD)] = jnp.sum(gpre, axis=0, keepdims=True)
+            return carry
+
+        lax.fori_loop(0, QUADS, one, 0)
+
+    def ev_norm():
+        e = gs1[...]
+        unit = stack[U1]
+        grad = norm_back(unit, inv1_ref[...], g1_ref[...][None, :], e)
+        gs1[...] = grad
+        ig[...] = grad
+        gctx[...] = jnp.zeros_like(grad)
+        small1[0:1, :] = jnp.sum(e * unit, axis=0, keepdims=True)
+        small1[1:2, :] = jnp.sum(e, axis=0, keepdims=True)
+        small1[2:3, :] = jnp.sum(grad, axis=0, keepdims=True)
+
+    def ev_rims():
+        rim[...] = rims_of(gctx[...], count)
 
     def ev_near(g):
         near_back_quad(g, gctx, near, q, kl_ref, b_ref, near, gb, gkl)
@@ -1413,8 +1444,6 @@
                 blend_copy(pair).start()
 
         rim_start(n, me, up, down, gleft, gright)
-        for copy in late[:2]:
-            copy.start()
 
     def mixed_copy(target):
         return to_seq(cmsg.at[me], cmsg.at[me], b2s.at[target], b2r.at[me], target)
@@ -1465,7 +1494,7 @@
     def ev_taps(part):
         @pl.when(part == 0)
         def _():
-            early[5].wait()
+            load_ext.wait()
             tap_scr[...] = jnp.zeros_like(tap_scr)
 
         taps_grad_into(tap_scr, gctx, ext, quarter * (part + 1), quarter * part, False)
@@ -1489,7 +1518,7 @@
             def _(pair=pair):
                 to_seq(cmsg.at[pair], cmsg.at[pair], b2s.at[pair], b2r.at[pair], pair).wait_recv()
 
-        for copy in early[6:]:
+        for copy in (load_k, load_v, load_p):
             copy.wait()
 
     def ev_far(g):
@@ -1500,8 +1529,6 @@
         for d in range(1, n):
             target = lax.rem(me + d, n)
             to_seq(ret.at[target], rland.at[me], rets.at[d], retr.at[me], target).start()
-        for copy in late[2:]:
-            copy.start()
 
     def ev_own():
         rland[me] = ret[me]
@@ -1516,16 +1543,19 @@
         member = member_rows(ends, slots)
         near[...] += t_mm(member, own[0] * inv)
         p[...] += t_mm(member, own[1] * inv)
-        gv[...] = jnp.where(valid_rows(count, slots), gv[...], 0.0)
         small0[0:1, :] = jnp.sum(near[...], axis=0, keepdims=True)
-        small0[1:2, :] = jnp.sum(gv[...], axis=0, keepdims=True)
+
+    def ev_values():
+        masked = jnp.where(valid_rows(count, slots), gv[...], 0.0)
+        gv[...] = masked
+        small0[1:2, :] = jnp.sum(masked, axis=0, keepdims=True)
 
     def small(i):
         return remote(sb.at[i], sl.at[i], ss.at[i], sr.at[i], partners[i])
 
     def ev_small(i):
         if i == 0:
-            pack_small(sb, small0, small1_ref, small2_ref, dbi_ref, gtaps)
+            pack_small(sb, small0, small1, small2_ref, dbi, gtaps)
         else:
             small(i - 1).wait_recv()
             sb[i] = sb[i - 1] + sl[i - 1]
@@ -1544,52 +1574,66 @@
         def _():
             event(after // every)
 
+    weights = {}
+    through = {}
+    for j, when in enumerate(FFN_AT):
+        weights[when + 1] = (2 * j, ACT, GS2)
+        weights[when + 2] = (2 * j + 1, H1, GPRE)
+        through[when + 3] = (GPRE, GS1, (2 * j + 1) % 4)
+    weights[OUTPUT_AT] = (8, CTX, GS1)
+    for i, (when, part) in enumerate(((VALUE_AT, GV), (QUERY_AT, NEAR), (KEY_AT, PROB))):
+        weights[when] = (9 + i, QUERY, part)
+        through[INPUT_AT[i]] = (part, IG, 1 + i)
+    through[GS1_AT] = (GS1, GCTX, 0)
+
+    def by_table(t, table, event):
+        columns = [pick(t, {when: row[i] for when, row in table.items()}) for i in range(3)]
+
+        @pl.when(columns[0][1])
+        def _():
+            event(*[value for value, _ in columns])
+
     def tick(t, carry):
         for stage, run in reversed(list(enumerate(stages))):
-            at = t - LAG[stage]
-
-            @pl.when((at >= 0) & (at < chunks))
+            since = t - ENTER - LAG[stage]
+            at = jnp.where(since < HELD, since, since - GAP)
+
+            @pl.when((since >= 0) & ((since < HELD) | (since >= HELD + GAP)) & (at < CHUNKS))
             def _(run=run, at=at):
                 run(at)
 
-        at_tick(t, 0, ev_start)
-        at_tick(t, 21, lambda: early[4].wait())
-        at_tick(t, 24, lambda: [copy.wait() for copy in late])
-        turn = jnp.where(t == 0, 0, (t - 23) // 3)
-
-        @pl.when((t == 0) | (t == 26) | (t == 29) | (t == 32))
+        for when, copy in starting:
+            at_tick(t, when, copy.start)
+        for when, copy in waiting:
+            at_tick(t, when, copy.wait)
+        block, hit = pick(t, {when: j for j, when in enumerate(FFN_AT)})
+
+        @pl.when(hit)
         def _():
-            through_event(turn)
-
-        @pl.when(t == 0)
-        def _():
-            rim[...] = rims_of(gctx[...], count)
-            early[2].wait()
-            early[3].wait()
-
-        at_ticks(t, 1, 1, QUADS, ev_near)
-        at_tick(t, 3, ev_blend)
-        at_ticks(t, 4, 1, 4, ev_taps)
-        at_tick(t, 7, ev_owner)
-        at_ticks(t, 8, 1, NEWTON, lambda i: ev_newton(NEWTON - 1 - i))
-        at_ticks(t, 9, 2, 4, ev_conv)
-        at_tick(t, 16, ev_core)
-        at_tick(t, 16, ev_mixed)
-        at_ticks(t, 16, 1, QUADS, ev_far)
-        at_tick(t, 19, ev_return)
-        at_tick(t, 23, ev_own)
-        filled = jnp.where(t == 21, 0, (t - 22) // 3)
-
-        @pl.when((t == 21) | (t == 25) | (t == 28) | (t == 31))
-        def _():
-            weight_event(filled)
-
-        at_tick(t, 33, lambda: pltpu.make_async_copy(ig, ig_hbm, ig_sem.at[0]).start())
+            inner_event(block)
+
+        by_table(t, through, through_event)
+        by_table(t, weights, weight_event)
+        at_tick(t, FFN_AT[3] + 3, ev_norm)
+        at_tick(t, GS1_AT, ev_rims)
+        at_ticks(t, GS1_AT + 1, 1, QUADS, ev_near)
+        at_tick(t, GS1_AT + 3, ev_blend)
+        at_tick(t, GS1_AT + 5, ev_owner)
+        at_ticks(t, GS1_AT + 6, 1, NEWTON, lambda i: ev_newton(NEWTON - 1 - i))
+        at_ticks(t, GS1_AT + 5, 1, 4, ev_conv)
+        at_tick(t, GS1_AT + 8, ev_mixed)
+        at_ticks(t, GS1_AT + 8, 1, QUADS, ev_far)
+        at_tick(t, GS1_AT + 10, ev_values)
+        at_tick(t, GS1_AT + 12, ev_core)
+        at_tick(t, GS1_AT + 12, ev_return)
+        at_ticks(t, GS1_AT + 11, 1, 4, ev_taps)
+        at_tick(t, GS1_AT + 14, ev_own)
+        at_tick(t, INPUT_AT[2], lambda: pltpu.make_async_copy(ig, ig_hbm, ig_sem.at[0]).start())
         for i in range(SMALL_STEPS + 1):
-            at_tick(t, SMALL_AT + 3 * i, partial(ev_small, i))
+            at_tick(t, SMALL_AT + 2 * i, partial(ev_small, i))
         return carry
 
-    lax.fori_loop(0, chunks + LAG[-1], tick, 0)
+    lax.fori_loop(0, CHUNKS + ENTER + GAP + LAG[-1], tick, 0)
     for i in range(SMALL_STEPS):
         small(i).wait_send()
     so_ref[...] = sb[SMALL_STEPS]
@@ -1613,40 +1657,38 @@
         to_seq(ret.at[target], rland.at[me], rets.at[d], retr.at[me], target).wait_send()
 
 
-def tail(lens, d_outer, d_inner, big, little, small1, small2, d_inner_bias):
+def tail(lens, big, little):
     slots, width = big[0].shape
     segs = lens.shape[1]
-    spans = ((0, 12), (12, 24), (24, 36))
-    at = spans[-1][1]
+    at = CHUNKS
     n = SEQ_DEVICES
     dma = pltpu.SemaphoreType.DMA
     vm = lambda *dims: pltpu.VMEM(dims, f32)
-    rows = vm(slots, width)
     anywhere = pl.BlockSpec(memory_space=pl.ANY)
-    two = dma((at, 2))
-    zsem = dma((at, 2, 3, 2))
     one = dma((at,))
+    zsem = dma((at, 2, 3))
     return pl.pallas_call(
-        partial(tail_kernel, spans),
-        in_specs=[smem()] + [anywhere] * (2 + len(big)) + [whole()] * (len(little) + 3),
+        tail_kernel,
+        in_specs=[smem()] + [anywhere] * len(big) + [whole()] * len(little),
         out_specs=[anywhere, whole(), anywhere],
-        out_shape=[shape(2, at, STRIP, LANES), shape(SMALL_ROWS, LANES), shape(slots, width)],
+        out_shape=[shape(2, at, STRIP // Z_ROWS, Z_ROWS, LANES), shape(SMALL_ROWS, LANES), shape(slots, width)],
         scratch_shapes=[
             vm(RING_ACC, STRIP, LANES), vm(RING_LC, STRIP, LANES), vm(RING_LC, 2, PART, LANES),
-            vm(RING_Z, 2, 2, 3, Z_ROWS, LANES), vm(RING_LC, 2, OWN, LANES),
-            vm(SMALL_STEPS + 1, SMALL_ROWS, LANES), vm(SMALL_STEPS, SMALL_ROWS, LANES), vm(24, STRIP, LANES),
-            vm(8, slots, width), vm(4, width, width), vm(slots + 40, width), rows, rows,
-            vm(slots + 40, width), vm(CONV, 8, width), vm(40, LANES), vm(8, width),
+            vm(RING_MID, 4, 2, Z_ROWS, LANES), vm(RING_Z, 2, 3, 2, Z_ROWS, LANES), vm(RING_LC, 2, OWN, LANES),
+            vm(RING_AG, 4, 2, Z_ROWS, LANES),
+            vm(SMALL_STEPS + 1, SMALL_ROWS, LANES), vm(SMALL_STEPS, SMALL_ROWS, LANES), vm(GW_SLOTS * PAIRS, STRIP, LANES),
+            vm(10, slots, width), vm(4, width, width), vm(slots + 40, width), vm(slots + 40, width),
+            vm(CONV, 8, width), vm(40, LANES), vm(8, width), vm(8, width), vm(1, 4 * width),
             vm(PAIRS, DH, LANES), vm(2 * RIM, width), vm(DH, width), vm(DH, width), vm(2, DH, width),
             vm(n, DH, LANES), vm(PAIRS, MSG, LANES), vm(RIM, width), vm(RIM, width), vm(LANES, LANES), vm(LANES, LANES),
             vm(n, 2, segs, width), vm(n, 2, segs, width), vm(2, segs, width),
-            dma((13,)), dma((1,)), dma((PAIRS,)), dma((n,)), dma((n,)), dma((n,)), dma((2,)), dma((2,)),
+            dma((27,)), dma((1,)), dma((PAIRS,)), dma((n,)), dma((n,)), dma((n,)), dma((2,)), dma((2,)),
             dma((n,)), dma((n,)), dma((SMALL_STEPS,)), dma((SMALL_STEPS,)),
-            one, two, one, one, two, two, zsem, zsem, two, two, two, two, zsem, zsem, two, two, one, one,
+            one, one, one, one, one, zsem, one, one, one, zsem, one, dma((at, 2)), one, one,
         ],
         compiler_params=params(collective_id=5, has_side_effects=True),
         name="tail",
-    )(lens, d_outer, d_inner, *big, *little, small1, small2, d_inner_bias)
+    )(lens, *big, *little)
 
 
 def unstrip(strips):
@@ -1663,21 +1705,23 @@
 PLACE_SLOTS = 24
 
 
-def place_strips_kernel(spans, s_ref, small_ref, *refs):
-    outs = refs[: len(spans)]
-    smalls = refs[len(spans) : -3]
+def place_strips_kernel(s_ref, small_ref, *refs):
+    outs = refs[:6]
+    smalls = refs[6:-3]
     buf, in_sem, out_sem = refs[-3:]
     moves = []
-    for out, (lo, hi) in zip(outs, spans):
-        across = out.shape[1] // LANES
-        for c in range(2):
-            for k in range(lo, hi):
-                at = 2 * (k - lo) + c
-                rows = pl.ds(at // across * STRIP, STRIP)
-                cols = pl.ds(at % across * LANES, LANES)
+    for e in range(CHUNKS // 3):
+        if e < 8:
+            out, row, col = outs[e % 2], (e // 2) * (1 - e % 2), (e // 2) * (e % 2)
+        else:
+            out, row, col = outs[e - 6], 0, 0
+        for k in range(3):
+            for c in range(2):
+                rows = pl.ds(row * STRIP, STRIP)
+                cols = pl.ds(col * STRIP + (2 * k + c) * LANES, LANES)
                 slot = len(moves) % PLACE_SLOTS
                 moves.append((
-                    pltpu.make_async_copy(s_ref.at[c, k], buf.at[slot], in_sem.at[slot]),
+                    pltpu.make_async_copy(s_ref.at[c, 3 * e + k], buf.at[slot], in_sem.at[slot]),
                     pltpu.make_async_copy(buf.at[slot], out.at[rows, cols], out_sem.at[slot]),
                 ))
     ahead = PLACE_SLOTS // 2
@@ -1694,12 +1738,12 @@
         out.wait()
 
 
-def place_strips(summed, packed, spans, shapes):
+def place_strips(summed, packed, shapes):
     anywhere = pl.BlockSpec(memory_space=pl.ANY)
     dma = pltpu.SemaphoreType.DMA
     width = shapes[0][1]
     return pl.pallas_call(
-        partial(place_strips_kernel, spans),
+        place_strips_kernel,
         in_specs=[anywhere, whole()],
         out_specs=[anywhere] * len(shapes) + [whole()] * 10,
         out_shape=[shape(*dims) for dims in shapes] + [shape(width)] * 8 + [shape(shapes[0][0]), shape(CONV, HEADS)],
@@ -1733,17 +1777,19 @@
     pre, layer_out, gs2, small2 = ffn_forward(
         lens, h1, inner_weight, inner_bias.reshape(1, -1), outer_weight, outer_bias, cot, second_gain, second_bias
     )
-    d_outer, d_inner, gs1, d_inner_bias, small1 = ffn_backward(
-        h1, gs2, pre, inner_weight, outer_weight, u1, inv1, first_gain
-    )
-    weights = [outer_weight, inner_weight, output_weight, query_weight, key_weight, value_weight]
+    weights = [outer_weight, inner_weight, output_weight, value_weight, query_weight, key_weight]
     if n == SEQ_DEVICES and lax.axis_size("dp") == 4:
-        big = [gs1, output_weight, near, q, ctx, ext, k, v, raised, x, query_weight, key_weight, value_weight]
-        little = [tops, b, ql, kl, *saved, taps]
-        summed, packed, input_grad = tail(lens, d_outer, d_inner, big, little, small1, small2, d_inner_bias)
-        spans = ((0, 12), (12, 24), (24, 27), (27, 30), (30, 33), (33, 36))
-        sums = place_strips(summed, packed, spans, [w.shape for w in weights])
+        big = [
+            gs2, h1, u1, pre, outer_weight, inner_weight, output_weight, near, q, ctx, ext, k, v, raised, x,
+            query_weight, key_weight, value_weight,
+        ]
+        little = [inv1, first_gain, tops, b, ql, kl, *saved, taps, small2]
+        summed, packed, input_grad = tail(lens, big, little)
+        sums = place_strips(summed.reshape(2, CHUNKS, STRIP, LANES), packed, [w.shape for w in weights])
     else:
+        d_outer, d_inner, gs1, d_inner_bias, small1 = ffn_backward(
+            h1, gs2, pre, inner_weight, outer_weight, u1, inv1, first_gain
+        )
         gctx, gqn, gblend, gkl, grim = near_back(lens, gs1, output_weight, near, q, kl, b)
         c, gleft, gright, gl = blend_exchange(n, gblend, grim, ql, kl, saved)
         gkf, gvf, back = far_back(n, lens, k, v, raised, tops, b, c, ql, gkl, gl)
@@ -1752,14 +1798,14 @@
         input_grad, d_query, d_key, d_value, small0 = project_back(
             lens, x, gs1, gqn, gkf, gvc, gvf, own, query_weight, key_weight, value_weight
         )
-        grads = [d_outer, d_inner, d_output, d_query, d_key, d_value]
+        grads = [d_outer, d_inner, d_output, d_value, d_query, d_key]
         sums = sum_plain(grads + [small0, small1, small2, d_inner_bias, gtaps])
         small = sums[6:]
         sums = (
             [unstrip_tall(sums[0], width // LANES)] + [unstrip(s) for s in sums[1:6]]
             + [small[0][0], small[0][1], *small[1][:3], *small[2][:3], small[3][0], small[4][:CONV, :HEADS]]
         )
-    d_outer, d_inner, d_output, d_query, d_key, d_value, *vectors = sums
+    d_outer, d_inner, d_output, d_value, d_query, d_key, *vectors = sums
     d_query_bias, d_value_bias, d_first_gain, d_first_bias, d_output_bias = vectors[:5]
     d_second_gain, d_second_bias, d_outer_bias, d_inner_bias, d_taps = vectors[5:]
     return (

time: 419 us -> 382 us (0.912)
  Pallas kernels: 412 us -> 375 us
    pallas_call x3 -> x2, Pallas kernels: 310 us -> 272 us  [the longest x1 251 us: tail(): pl.pallas_call(tail_kernel, in_specs=[smem()] + [anywhere] * len(big) + [...]
where the time goes in v3:
time: 382 us
  Pallas kernels  375 us (98%)
  local copies, waits for them, and re-layouts  6.04 us (2%)
    pallas_call x1, Pallas kernels, tail(): pl.pallas_call(tail_kernel, in_specs=[smem()] + [anywhere] * len(big) + [...  251 us
    pallas_call x1, Pallas kernels, ffn_forward(): pl.pallas_call(forward_kernel, grid=(inner // width,), in_specs=[smem(),...  26.8 us
    pallas_call x1, Pallas kernels, attend(): pl.pallas_call(attend_kernel, in_specs=[smem()] + [whole()] * 12, out_spe...  22.7 us
    pallas_call x1, Pallas kernels, place_strips(): pl.pallas_call(place_strips_kernel, in_specs=[anywhere, whole()], out_spe...  21 us
    pallas_call x1, Pallas kernels, far_exchange(): pl.pallas_call(partial(far_exchange_kernel, n), in_specs=[whole()] * 3, o...  19.7 us
    pallas_call x1, Pallas kernels, land_exchange(): pl.pallas_call(partial(land_exchange_kernel, n), in_specs=[whole()] * 2,...  14.3 us
    pallas_call x1, Pallas kernels, project(): pl.pallas_call(project_kernel, in_specs=[smem(), whole()] + [anywhere] *...  12.4 us

profile of v3, /device:TPU:0, one launch (start us, length us, event | category | flops | bytes accessed | tf_op | source)
XLA Modules:
  0.0 381.6 jit_solution(14401577856886104186)
XLA Ops:
  0.7 0.8 copy.39
  1.4 0.1 broadcast_in_dim.3
  1.6 0.8 reshape.58.taps_ref
  2.3 12.4 %project.1 = (f32[512,768]{1,0:T(8,128)}, f32[512,768]{1,0:T(8,128)}, f32[512,768]{1,0:T(8,128)}, f32[2,8,768]{2,1,0:T(8,128)}, f32[32,768]{1,0:T(8,128)}) custom-call(s32[1,8]{1,0:T(1,128)} %lens_ref.9, f32[512,768]{1,0:T(8,128)} %bitcast.11, f32[768,768]{1,0:T(8,128)} %wq_hbm.3, f32[768,768]{1,0:T(8,128)} %wk_hbm.3, f32[768,768]{1,0:T(8,128)} %wv_hbm.3, ...), custom_call_target="tpu_custom_call" | custom-call | tf_op jit(solution)/shard_map/project/pallas_call | solution.py:233
  14.7 14.3 %land_exchange.1 = (f32[8,2,8,768]{3,2,1,0:T(8,128)}, f32[16,768]{1,0:T(8,128)}, f32[16,768]{1,0:T(8,128)}) custom-call(f32[2,8,768]{2,1,0:T(8,128)} %get-tuple-element.67.mine_ref, f32[32,768]{1,0:T(8,128)} %get-tuple-element.68.rim_ref), custom_call_target="tpu_custom_call" | custom-call | tf_op jit(solution)/shard_map/land_exchange/pallas_call | solution.py:328
  29.0 1.8 slice_bitcast_fusion
  30.9 6.5 %far_local.1 = (f32[6,72,128]{2,1,0:T(8,128)}, f32[512,768]{1,0:T(8,128)}, f32[1,768]{1,0:T(1,128)}) custom-call(s32[1,8]{1,0:T(1,128)} %lens_ref.9, f32[512,768]{1,0:T(8,128)} %get-tuple-element.70.k_ref.k_hbm, f32[512,768]{1,0:T(8,128)} %get-tuple-element.66.v_ref.v_hbm, f32[64,768]{1,0:T(8,128)} %get-tuple-element.148.ql_ref), custom_call_target="tpu_custom_call" | custom-call | tf_op jit(solution)/shard_map/far_local/pallas_call | solution.py:636
  37.4 19.7 %far_exchange.1 = (f32[6,72,128]{2,1,0:T(8,128)}, f32[128,128]{1,0:T(8,128)}, f32[7,128,128]{2,1,0:T(8,128)}, f32[6,128,128]{2,1,0:T(8,128)}, f32[6,128,128]{2,1...) custom-call(f32[6,72,128]{2,1,0:T(8,128)} %get-tuple-element.71.f_ref, f32[64,768]{1,0:T(8,128)} %get-tuple-element.148.ql_ref, ...), custom_call_target="tpu_custom_call" | custom-call | tf_op jit(solution)/shard_map/far_exchange/pallas_call | solution.py:446
  57.0 22.7 %attend.1 = (f32[512,768]{1,0:T(8,128)}, f32[512,768]{1,0:T(8,128)}, f32[512,768]{1,0:T(8,128)}, f32[512,768]{1,0:T(8,128)}, f32[512,1]{1,0:T(8,128)}, /*index=5*/f32[552,768]{1,0:T(8,128)}) custom-call(s32[1,8]{1,0:T(1,128)} %lens_ref.9, f32[512,768]{1,0:T(8,128)} %get-tuple-element.65.q_ref.q_hbm, f32[512,768]{1,0:T(8,128)} %get-tuple-element.66.v_ref.v_hbm, ...), custom_call_target="tpu_custom_call" | custom-call | tf_op jit(solution)/shard_map/attend/pallas_call | solution.py:711
  79.7 26.8 %ffn_forward.1 = (f32[512,3072]{1,0:T(8,128)}, f32[512,768]{1,0:T(8,128)}, f32[512,768]{1,0:T(8,128)}, f32[8,768]{1,0:T(8,128)}) custom-call(s32[1,8]{1,0:T(1,128)} %lens_ref.9, f32[512,768]{1,0:T(8,128)} %get-tuple-element.75.h1_ref.h1_hbm, f32[768,3072]{1,0:T(8,128)} %win_hbm.1, f32[1,3072]{1,0:T(1,128)} %bitcast.16, f32[3072,768]{1,0:T(8,128)} %wout_hbm.1, ...), custom_call_target="tpu_custom_call" | custom-call | tf_op jit(solution)/shard_map/ffn_forward/pallas_call | solution.py:773
  106.5 251.4 %tail.1 = (f32[2,36,16,48,128]{4,3,2,1,0:T(8,128)}, f32[112,128]{1,0:T(8,128)}, f32[512,768]{1,0:T(8,128)}) custom-call(s32[1,8]{1,0:T(1,128)} %lens_ref.9, f32[512,768]{1,0:T(8,128)} %get-tuple-element.77.gs2_hbm, f32[512,768]{1,0:T(8,128)} %get-tuple-element.75.h1_ref.h1_hbm, f32[512,768]{1,0:T(8,128)} %get-tuple-element.78.u1_hbm, ...), custom_call_target="tpu_custom_call" | custom-call | tf_op jit(solution)/shard_map/tail/pallas_call | solution.py:1670
  358.0 0.0 copy-start
  358.0 21.0 %place_strips.1 = (f32[3072,768]{1,0:T(8,128)}, f32[768,3072]{1,0:T(8,128)}, f32[768,768]{1,0:T(8,128)}, f32[768,768]{1,0:T(8,128)}, f32[768,768]{1,0:T(8,128)},...) custom-call(f32[2,36,768,128]{3,2,1,0:T(8,128)} %bitcast.10, ...), custom_call_target="tpu_custom_call" | custom-call | tf_op jit(solution)/shard_map/place_strips/pallas_call | solution.py:1745
  379.0 1.4 copy.40
  380.4 0.0 copy-done
  380.4 1.1 copy.42
Async XLA Ops:
  358.0 22.4 %copy-start = (f32[512,768]{1,0:T(8,128)S(1)}, f32[512,768]{1,0:T(8,128)}, u32[]{:S(2)}) copy-start(f32[512,768]{1,0:T(8,128)} %get-tuple-element.93) | copy-start | bytes 4718596

commit v4 on v3

--- a/solution.py
+++ b/solution.py
@@ -186,75 +186,18 @@
     return jax.ShapeDtypeStruct(dims, f32)
 
 
-def project_kernel(
-    lens_ref, x_ref, wq_hbm, wk_hbm, wv_hbm, bq_ref, bv_ref,
-    q_ref, k_ref, v_ref, land_ref, rim_ref,
-    w_ref, bias_ref, out_ref, load,
-):
-    slots, width = x_ref.shape
-    segs = land_ref.shape[1]
-    loads = [
-        pltpu.make_async_copy(hbm.at[:, pl.ds(g * QUAD, QUAD)], w_ref.at[i * QUADS + g], load.at[i * QUADS + g])
-        for i, hbm in enumerate((wq_hbm, wk_hbm, wv_hbm))
-        for g in range(QUADS)
-    ]
-    for copy in loads:
-        copy.start()
-    ends = seg_ends(lens_ref, segs)
-    member = member_rows(ends, slots)
-    inv = inverse_lens(lens_ref, segs)
-    for g in range(QUADS):
-        bias_ref[g] = jnp.broadcast_to(bq_ref[pl.ds(g * QUAD, QUAD)][None, :], (8, QUAD))
-        bias_ref[QUADS + g] = jnp.zeros((8, QUAD), f32)
-        bias_ref[2 * QUADS + g] = jnp.broadcast_to(bv_ref[pl.ds(g * QUAD, QUAD)][None, :], (8, QUAD))
-
-    def one(i, carry):
-        pltpu.make_async_copy(wq_hbm.at[:, pl.ds(0, QUAD)], w_ref.at[i], load.at[i]).wait()
-        out_ref[i] = mm(x_ref[...], w_ref[i]) + bias_ref[i, 0:1, :]
-        return carry
-
-    lax.fori_loop(0, 3 * QUADS, one, 0)
-    valid = valid_rows(ends[-1], slots)
-    for g in range(QUADS):
-        cols = slice(g * QUAD, (g + 1) * QUAD)
-        q_ref[:, cols] = out_ref[g]
-        k_ref[:, cols] = out_ref[QUADS + g]
-        v_ref[:, cols] = jnp.where(valid, out_ref[2 * QUADS + g], 0.0)
-    land_ref[0] = mm(member, q_ref[...]) * inv
-    land_ref[1] = mm(member, k_ref[...]) * inv
-    rim_ref[...] = rims_of(v_ref[...], ends[-1])
-
-
-def project(lens, x, wq, wk, wv, bq, bv):
-    slots, width = x.shape
-    segs = lens.shape[1]
-    anywhere = pl.BlockSpec(memory_space=pl.ANY)
-    count = 3 * QUADS
-    return pl.pallas_call(
-        project_kernel,
-        in_specs=[smem(), whole()] + [anywhere] * 3 + [whole()] * 2,
-        out_specs=[whole()] * 5,
-        out_shape=[
-            shape(slots, width), shape(slots, width), shape(slots, width),
-            shape(2, segs, width), shape(2 * RIM, width),
-        ],
-        scratch_shapes=[
-            pltpu.VMEM((count, width, QUAD), f32), pltpu.VMEM((count, 8, QUAD), f32),
-            pltpu.VMEM((count, slots, QUAD), f32), pltpu.SemaphoreType.DMA((count,)),
-        ],
-        compiler_params=params(),
-        name="project",
-    )(lens, x, wq, wk, wv, bq, bv)
-
-
-def greet_all(n):
+def greet_signal(n):
     me = lax.axis_index("seq")
-    barrier = pltpu.get_barrier_semaphore()
     for d in range(1, n):
         pl.semaphore_signal(
-            barrier, inc=1, device_id={"seq": lax.rem(me + d, n)}, device_id_type=MESH
+            pltpu.get_barrier_semaphore(), inc=1, device_id={"seq": lax.rem(me + d, n)}, device_id_type=MESH
         )
-    pl.semaphore_wait(barrier, n - 1)
+    return me
+
+
+def greet_all(n):
+    me = greet_signal(n)
+    pl.semaphore_wait(pltpu.get_barrier_semaphore(), n - 1)
     return me
 
 
@@ -300,42 +243,6 @@
         up.wait_send()
 
 
-def land_exchange_kernel(
-    n, mine_ref, rim_ref, all_ref, left_ref, right_ref, send, recv, rsend, rrecv
-):
-    me = greet_all(n)
-    up, down = rim_copies(n, me, rim_ref, left_ref, right_ref, rsend, rrecv)
-    copies = []
-    for d in range(1, n):
-        copy = to_seq(
-            mine_ref, all_ref.at[me], send.at[d], recv.at[me], lax.rem(me + d, n)
-        )
-        copy.start()
-        copies.append(copy)
-    rim_start(n, me, up, down, left_ref, right_ref)
-    all_ref[me] = mine_ref[...]
-    for d in range(1, n):
-        source = lax.rem(me + d, n)
-        to_seq(mine_ref, all_ref.at[source], send.at[d], recv.at[source], source).wait_recv()
-    rim_wait(n, me, up, down)
-    for copy in copies:
-        copy.wait_send()
-
-
-def land_exchange(n, mine, rim):
-    _, segs, width = mine.shape
-    dma = pltpu.SemaphoreType.DMA
-    return pl.pallas_call(
-        partial(land_exchange_kernel, n),
-        in_specs=[whole()] * 2,
-        out_specs=[whole()] * 3,
-        out_shape=[shape(n, 2, segs, width), shape(RIM, width), shape(RIM, width)],
-        scratch_shapes=[dma((n,)), dma((n,)), dma((2,)), dma((2,))],
-        compiler_params=params(collective_id=1, has_side_effects=True),
-        name="land_exchange",
-    )(mine, rim)
-
-
 MSG = DH + 8
 
 
@@ -356,106 +263,6 @@
     scores = jnp.where(mask, mm_t(query, key, TOP) * SCALE, MASKED)
     raised = jnp.exp(scores - jnp.max(scores, axis=1, keepdims=True))
     return raised / jnp.sum(raised, axis=1, keepdims=True)
-
-
-def far_exchange_kernel(
-    n, f_ref, ql_ref, kl_ref, b_ref, core_ref, zs_ref, ps_ref, rs_ref, qs_ref, mx_ref,
-    land, s1, r1, s2, r2,
-):
-    me = greet_all(n)
-    for p in range(PAIRS):
-
-        @pl.when(me != p)
-        def _(p=p):
-            to_seq(f_ref.at[p], land.at[me], s1.at[p], r1.at[me], p).start()
-
-    @pl.when(me < PAIRS)
-    def _():
-        mask = head_mask(LANES)
-        lanes = pl.ds(pl.multiple_of(me * LANES, LANES), LANES)
-        query = spread(ql_ref[:, lanes], mask)
-        key = spread(kl_ref[:, lanes], mask)
-        core = core_of(query, key, mask)
-        core_ref[...] = core
-        colsum = jnp.sum(core, axis=0, keepdims=True)
-        sigma = jnp.sqrt(pair_sums(colsum * colsum))
-        z = core.T / sigma
-        unit = eye(LANES)
-        zs_ref[0] = z
-
-        def newton(step, carry):
-            z = zs_ref[step]
-            prod = mm(core_ref[...], z, TOP)
-            ps_ref[step] = prod
-            r = 15.0 * unit - mm(prod, 7.0 * unit - prod, TOP)
-            rs_ref[step] = r
-            q = 13.0 * unit - mm(prod, r, TOP)
-            qs_ref[step] = q
-            zs_ref[step + 1] = 0.25 * mm(z, q, TOP)
-            return carry
-
-        lax.fori_loop(0, NEWTON, newton, 0)
-        z = zs_ref[NEWTON]
-        land[me] = f_ref[me]
-        for s in range(n):
-
-            @pl.when(me != s)
-            def _(s=s):
-                to_seq(f_ref.at[0], land.at[s], s1.at[0], r1.at[s], s).wait_recv()
-
-        top = land[0][DH : DH + 1]
-        for s in range(1, n):
-            top = jnp.maximum(top, land[s][DH : DH + 1])
-        total = jnp.zeros_like(top)
-        mixed = jnp.zeros((DH, LANES), f32)
-        for s in range(n):
-            part = land[s]
-            factor = jnp.exp(part[DH : DH + 1] - top)
-            total = total + part[DH + 1 : DH + 2] * factor
-            mixed = mixed + part[:DH] * factor
-        mixed = mixed / total
-        mx_ref[...] = mixed
-        b_ref[me, 0:DH, :] = mm_t(mixed, z, TOP)
-        pad = jnp.zeros((MSG - DH - 2, LANES), f32)
-        b_ref[me, DH:MSG, :] = jnp.concatenate([top, total, pad], axis=0)
-        for t in range(n):
-
-            @pl.when(me != t)
-            def _(t=t):
-                to_seq(b_ref.at[me], b_ref.at[me], s2.at[t], r2.at[me], t).start()
-
-    for p in range(PAIRS):
-
-        @pl.when(me != p)
-        def _(p=p):
-            to_seq(b_ref.at[p], b_ref.at[p], s2.at[p], r2.at[p], p).wait_recv()
-            to_seq(f_ref.at[p], land.at[me], s1.at[p], r1.at[me], p).wait_send()
-
-    @pl.when(me < PAIRS)
-    def _():
-        for t in range(n):
-
-            @pl.when(me != t)
-            def _(t=t):
-                to_seq(b_ref.at[me], b_ref.at[me], s2.at[t], r2.at[me], t).wait_send()
-
-
-def far_exchange(n, parts, ql, kl):
-    dma = pltpu.SemaphoreType.DMA
-    square = (LANES, LANES)
-    return pl.pallas_call(
-        partial(far_exchange_kernel, n),
-        in_specs=[whole()] * 3,
-        out_specs=[whole()] * 7,
-        out_shape=[
-            shape(PAIRS, MSG, LANES), shape(*square), shape(NEWTON + 1, *square),
-            shape(NEWTON, *square), shape(NEWTON, *square), shape(NEWTON, *square),
-            shape(DH, LANES),
-        ],
-        scratch_shapes=[pltpu.VMEM((n, MSG, LANES), f32), dma((PAIRS,)), dma((n,)), dma((n,)), dma((n,))],
-        compiler_params=params(collective_id=2, has_side_effects=True),
-        name="far_exchange",
-    )(parts, ql, kl)
 
 
 def inverse_grad(gblend, mixed):
@@ -605,44 +412,6 @@
     )(parts)
 
 
-def far_kernel(lens_ref, k_ref, v_ref, ql_ref, f_ref, p_ref, m_ref):
-    slots = k_ref.shape[0]
-    count = seg_ends(lens_ref, lens_ref.shape[1])[-1]
-    valid = valid_rows(count, slots)
-    mask = head_mask(QUAD)
-
-    def one(g, carry):
-        cols = quad(g)
-        scores = mm_t(k_ref[:, cols], spread(ql_ref[:, cols], mask)) * SCALE
-        scores = jnp.where(valid, scores, MASKED)
-        top = jnp.max(scores, axis=0, keepdims=True)
-        raised = jnp.where(valid, jnp.exp(scores - top), 0.0)
-        p_ref[:, cols] = raised
-        m_ref[:, cols] = top
-        total = jnp.sum(raised, axis=0, keepdims=True)
-        weighted = fold(t_mm(v_ref[:, cols], raised), mask)
-        tail = jnp.concatenate([top, total, jnp.zeros((MSG - DH - 2, QUAD), f32)], axis=0)
-        for j in range(QUAD // LANES):
-            part = slice(j * LANES, (j + 1) * LANES)
-            f_ref[g * 2 + j, 0:DH, :] = weighted[:, part]
-            f_ref[g * 2 + j, DH:MSG, :] = tail[:, part]
-        return carry
-
-    lax.fori_loop(0, QUADS, one, 0)
-
-
-def far_local(lens, k, v, ql):
-    slots, width = k.shape
-    return pl.pallas_call(
-        far_kernel,
-        in_specs=[smem()] + [whole()] * 3,
-        out_specs=[whole()] * 3,
-        out_shape=[shape(PAIRS, MSG, LANES), shape(slots, width), shape(1, width)],
-        compiler_params=params(),
-        name="far_local",
-    )(lens, k, v, ql)
-
-
 def norm_stats(r):
     centered = r - jnp.mean(r, axis=1, keepdims=True)
     spread_ = jnp.mean(centered * centered, axis=1, keepdims=True)
@@ -667,55 +436,247 @@
     return jnp.concatenate([ref[2 * g, rows, :], ref[2 * g + 1, rows, :]], axis=1)
 
 
-def attend_kernel(
-    lens_ref, q_ref, v_ref, kl_ref, b_ref, left_ref, right_ref, taps_ref, x_ref, wo_ref, bo_ref, g1_ref, b1_ref,
-    near_ref, ctx_ref, h1_ref, u1_ref, inv1_ref, ext_ref,
+def front_kernel(
+    n, lens_ref, x_ref, taps_in, bq_ref, bv_ref, bo_ref, g1_ref, b1_ref, wq_hbm, wk_hbm, wv_hbm, wo_hbm,
+    q_out, k_out, v_out, p_out, near_out, ctx_out, ext_out, h1_out, u1_out,
+    m_ref, b_ref, ql_ref, kl_ref, core_ref, zs_ref, ps_ref, rs_ref, qs_ref, mx_ref, taps_ref, inv1_ref,
+    w, wo, bias, stack, ext, f_ref, mine, lands, rim, left, right, land,
+    load, out, ms, mr, ls, lr, s1, r1, s2, r2,
 ):
-    slots = q_ref.shape[0]
-    count = seg_ends(lens_ref, lens_ref.shape[1])[-1]
-    fill_extended(ext_ref, v_ref[...], left_ref[...], right_ref[...], count)
-    conv_into(ctx_ref, ext_ref, taps_ref, slots, False, False)
-    mask = head_mask(QUAD)
-    ones = jnp.where(mask, 1.0, 0.0)
-    head = lax.broadcasted_iota(jnp.int32, (slots, QUAD), 1) >> 6
-
-    def one(g, carry):
+    _, slots, width = stack.shape
+    segs = mine.shape[1]
+    v, q, k, p, near, ctx, h1, u1 = [stack.at[i] for i in range(8)]
+    loads = [
+        pltpu.make_async_copy(hbm.at[:, pl.ds(g * QUAD, QUAD)], w.at[i * QUADS + g], load.at[i * QUADS + g])
+        for i, hbm in enumerate((wv_hbm, wq_hbm, wk_hbm))
+        for g in range(QUADS)
+    ]
+    loads.append(pltpu.make_async_copy(wo_hbm, wo, load.at[3 * QUADS]))
+    for copy in loads:
+        copy.start()
+    leaving = []
+
+    def leave(src, dst):
+        leaving.append(pltpu.make_async_copy(src, dst, out.at[len(leaving)]))
+        leaving[-1].start()
+
+    me = greet_signal(n)
+    ends = seg_ends(lens_ref, segs)
+    count = ends[-1]
+    valid = valid_rows(count, slots)
+    member = member_rows(ends, slots)
+    inv = inverse_lens(lens_ref, segs)
+    for g in range(QUADS):
+        cols = pl.ds(g * QUAD, QUAD)
+        bias[g] = jnp.broadcast_to(bv_ref[cols][None, :], (8, QUAD))
+        bias[QUADS + g] = jnp.broadcast_to(bq_ref[cols][None, :], (8, QUAD))
+        bias[2 * QUADS + g] = jnp.zeros((8, QUAD), f32)
+
+    def one(i, carry):
+        pltpu.make_async_copy(wv_hbm.at[:, pl.ds(0, QUAD)], w.at[i], load.at[i]).wait()
+        stack[i // QUADS, :, quad(lax.rem(i, QUADS))] = mm(x_ref[...], w[i]) + bias[i, 0:1, :]
+
+        @pl.when(i == QUADS - 1)
+        def _():
+            v[...] = jnp.where(valid, v[...], 0.0)
+            rim[...] = rims_of(v[...], count)
+            pl.semaphore_wait(pltpu.get_barrier_semaphore(), n - 1)
+            rim_start(n, me, up, down, left, right)
+
+        return carry
+
+    up, down = rim_copies(n, me, rim, left, right, ms, mr)
+    lax.fori_loop(0, 3 * QUADS, one, 0)
+    mine[0] = mm(member, q[...]) * inv
+    mine[1] = mm(member, k[...]) * inv
+    for d in range(1, n):
+        to_seq(mine, lands.at[me], ls.at[d], lr.at[me], lax.rem(me + d, n)).start()
+    lands[me] = mine[...]
+    leave(q, q_out)
+    leave(k, k_out)
+    leave(v, v_out)
+    row = lax.broadcasted_iota(jnp.int32, (HEADS, width), 0)
+    col = lax.broadcasted_iota(jnp.int32, (HEADS, width), 1) >> 6
+    taps_ref[...] = mm(taps_in[...], jnp.where(row == col, 1.0, 0.0), TOP)
+    rim_wait(n, me, up, down)
+    fill_extended(ext, v[...], left[...], right[...], count)
+    leave(ext, ext_out)
+    conv_into(ctx, ext, taps_ref, slots, False, False)
+
+    for d in range(1, n):
+        source = lax.rem(me + d, n)
+        to_seq(mine, lands.at[source], ls.at[d], lr.at[source], source).wait_recv()
+    for s in range(n):
+        rows = slice(s * segs, (s + 1) * segs)
+        ql_ref[rows, :] = lands[s, 0]
+        kl_ref[rows, :] = lands[s, 1]
+
+    def far(g, carry):
         cols = quad(g)
-        scores = mm_t(q_ref[:, cols], spread(kl_ref[:, cols], mask)) * SCALE
+        mask = head_mask(QUAD)
+        scores = mm_t(k[:, cols], spread(ql_ref[:, cols], mask)) * SCALE
+        scores = jnp.where(valid, scores, MASKED)
+        top = jnp.max(scores, axis=0, keepdims=True)
+        raised = jnp.where(valid, jnp.exp(scores - top), 0.0)
+        p[:, cols] = raised
+        m_ref[:, cols] = top
+        total = jnp.sum(raised, axis=0, keepdims=True)
+        weighted = fold(t_mm(v[:, cols], raised), mask)
+        rest = jnp.concatenate([top, total, jnp.zeros((MSG - DH - 2, QUAD), f32)], axis=0)
+        for j in range(QUAD // LANES):
+            part = slice(j * LANES, (j + 1) * LANES)
+            f_ref[g * 2 + j, 0:DH, :] = weighted[:, part]
+            f_ref[g * 2 + j, DH:MSG, :] = rest[:, part]
+        return carry
+
+    lax.fori_loop(0, QUADS, far, 0)
+    for pair in range(PAIRS):
+
+        @pl.when(me != pair)
+        def _(pair=pair):
+            to_seq(f_ref.at[pair], land.at[me], s1.at[pair], r1.at[me], pair).start()
+
+    leave(p, p_out)
+
+    @pl.when(me < PAIRS)
+    def _():
+        mask = head_mask(LANES)
+        lanes = pl.ds(pl.multiple_of(me * LANES, LANES), LANES)
+        core = core_of(spread(ql_ref[:, lanes], mask), spread(kl_ref[:, lanes], mask), mask)
+        core_ref[...] = core
+        colsum = jnp.sum(core, axis=0, keepdims=True)
+        zs_ref[0] = core.T / jnp.sqrt(pair_sums(colsum * colsum))
+        unit = eye(LANES)
+
+        def newton(step, carry):
+            z = zs_ref[step]
+            prod = mm(core_ref[...], z, TOP)
+            ps_ref[step] = prod
+            r = 15.0 * unit - mm(prod, 7.0 * unit - prod, TOP)
+            rs_ref[step] = r
+            q_ = 13.0 * unit - mm(prod, r, TOP)
+            qs_ref[step] = q_
+            zs_ref[step + 1] = 0.25 * mm(z, q_, TOP)
+            return carry
+
+        lax.fori_loop(0, NEWTON, newton, 0)
+        land[me] = f_ref[me]
+        for s in range(n):
+
+            @pl.when(me != s)
+            def _(s=s):
+                to_seq(f_ref.at[0], land.at[s], s1.at[0], r1.at[s], s).wait_recv()
+
+        top = land[0][DH : DH + 1]
+        for s in range(1, n):
+            top = jnp.maximum(top, land[s][DH : DH + 1])
+        total = jnp.zeros_like(top)
+        mixed = jnp.zeros((DH, LANES), f32)
+        for s in range(n):
+            part = land[s]
+            factor = jnp.exp(part[DH : DH + 1] - top)
+            total = total + part[DH + 1 : DH + 2] * factor
+            mixed = mixed + part[:DH] * factor
+        mixed = mixed / total
+        mx_ref[...] = mixed
+        b_ref[me, 0:DH, :] = mm_t(mixed, zs_ref[NEWTON], TOP)
+        pad = jnp.zeros((MSG - DH - 2, LANES), f32)
+        b_ref[me, DH:MSG, :] = jnp.concatenate([top, total, pad], axis=0)
+        for t in range(n):
+
+            @pl.when(me != t)
+            def _(t=t):
+                to_seq(b_ref.at[me], b_ref.at[me], s2.at[t], r2.at[me], t).start()
+
+    def soft(g, carry):
+        cols = quad(g)
+        mask = head_mask(QUAD)
+        head = lax.broadcasted_iota(jnp.int32, (slots, QUAD), 1) >> 6
+        scores = mm_t(q[:, cols], spread(kl_ref[:, cols], mask)) * SCALE
         tops = [jnp.max(scores[:, h * DH : (h + 1) * DH], axis=1, keepdims=True) for h in range(4)]
         top = jnp.where(head < 2, jnp.where(head < 1, tops[0], tops[1]), jnp.where(head < 3, tops[2], tops[3]))
         raised = jnp.exp(scores - top)
-        near = raised / mm(raised, ones)
-        near_ref[:, cols] = near
-        blend = spread(pair_rows(b_ref, g, slice(0, DH)), mask)
-        ctx_ref[:, cols] += mm_t(near, blend)
+        near[:, cols] = raised / mm(raised, jnp.where(mask, 1.0, 0.0))
         return carry
 
-    lax.fori_loop(0, QUADS, one, 0)
-
-    def two(g, carry):
+    lax.fori_loop(0, QUADS, soft, 0)
+    leave(near, near_out)
+    for pair in range(PAIRS):
+
+        @pl.when(me != pair)
+        def _(pair=pair):
+            to_seq(b_ref.at[pair], b_ref.at[pair], s2.at[pair], r2.at[pair], pair).wait_recv()
+
+    def blend(g, carry):
         cols = quad(g)
-        u1_ref[:, cols] = mm(ctx_ref[...], wo_ref[:, cols])
+        ctx[:, cols] += mm_t(near[:, cols], spread(pair_rows(b_ref, g, slice(0, DH)), head_mask(QUAD)))
         return carry
 
-    lax.fori_loop(0, QUADS, two, 0)
-    summed = x_ref[...] + (u1_ref[...] + bo_ref[...][None, :])
-    unit, inv = norm_stats(summed)
-    u1_ref[...] = unit
-    inv1_ref[...] = inv
-    h1_ref[...] = unit * g1_ref[...][None, :] + b1_ref[...][None, :]
-
-
-def attend(lens, q, v, kl, b, left, right, taps, x, wo, bo, g1, b1):
-    slots, width = q.shape
+    lax.fori_loop(0, QUADS, blend, 0)
+    leave(ctx, ctx_out)
+    loads[-1].wait()
+
+    def project(g, carry):
+        cols = quad(g)
+        u1[:, cols] = mm(ctx[...], wo[:, cols])
+        return carry
+
+    lax.fori_loop(0, QUADS, project, 0)
+    unit, scale = norm_stats(x_ref[...] + (u1[...] + bo_ref[...][None, :]))
+    h1[...] = unit * g1_ref[...][None, :] + b1_ref[...][None, :]
+    leave(h1, h1_out)
+    u1[...] = unit
+    leave(u1, u1_out)
+    inv1_ref[...] = scale
+    for d in range(1, n):
+        to_seq(mine, lands.at[me], ls.at[d], lr.at[me], lax.rem(me + d, n)).wait_send()
+    for pair in range(PAIRS):
+
+        @pl.when(me != pair)
+        def _(pair=pair):
+            to_seq(f_ref.at[pair], land.at[me], s1.at[pair], r1.at[me], pair).wait_send()
+
+    @pl.when(me < PAIRS)
+    def _():
+        for t in range(n):
+
+            @pl.when(me != t)
+            def _(t=t):
+                to_seq(b_ref.at[me], b_ref.at[me], s2.at[t], r2.at[me], t).wait_send()
+
+    for copy in leaving:
+        copy.wait()
+
+
+def front(n, lens, x, taps, bq, bv, bo, g1, b1, wq, wk, wv, wo):
+    slots, width = x.shape
+    segs = lens.shape[1]
+    dma = pltpu.SemaphoreType.DMA
+    vm = lambda *dims: pltpu.VMEM(dims, f32)
+    anywhere = pl.BlockSpec(memory_space=pl.ANY)
+    square = (LANES, LANES)
+    rows = shape(slots, width)
+    count = 3 * QUADS
     return pl.pallas_call(
-        attend_kernel,
-        in_specs=[smem()] + [whole()] * 12,
-        out_specs=[whole()] * 6,
-        out_shape=[shape(slots, width)] * 4 + [shape(slots, 1), shape(slots + 40, width)],
-        compiler_params=params(),
-        name="attend",
-    )(lens, q, v, kl, b, left, right, taps, x, wo, bo, g1, b1)
+        partial(front_kernel, n),
+        in_specs=[smem()] + [whole()] * 7 + [anywhere] * 4,
+        out_specs=[anywhere] * 9 + [whole()] * 12,
+        out_shape=[rows] * 6 + [shape(slots + 40, width), rows, rows]
+        + [
+            shape(1, width), shape(PAIRS, MSG, LANES), shape(DH, width), shape(DH, width), shape(*square),
+            shape(NEWTON + 1, *square), shape(NEWTON, *square), shape(NEWTON, *square), shape(NEWTON, *square),
+            shape(DH, LANES), shape(CONV, width), shape(slots, 1),
+        ],
+        scratch_shapes=[
+            vm(count, width, QUAD), vm(width, width), vm(count, 8, QUAD), vm(8, slots, width), vm(slots + 40, width),
+            vm(PAIRS, MSG, LANES), vm(2, segs, width), vm(n, 2, segs, width), vm(2 * RIM, width), vm(RIM, width),
+            vm(RIM, width), vm(n, MSG, LANES),
+            dma((count + 1,)), dma((9,)), dma((2,)), dma((2,)), dma((n,)), dma((n,)), dma((PAIRS,)), dma((n,)),
+            dma((n,)), dma((n,)),
+        ],
+        compiler_params=params(collective_id=1, has_side_effects=True),
+        name="front",
+    )(lens, x, taps, bq, bv, bo, g1, b1, wq, wk, wv, wo)
 
 
 def forward_kernel(
@@ -983,31 +944,30 @@
 
 
 def conv_back_kernel(
-    lens_ref, v_ref, left_ref, right_ref, gctx_ref, gleft_ref, gright_ref, taps_ref, ctx_ref, gs1_ref,
+    lens_ref, values_ref, gctx_ref, gleft_ref, gright_ref, taps_ref, ctx_ref, gs1_ref,
     gv_ref, gtaps_ref, dwo_ref,
     ext_ref, scr_ref,
 ):
-    slots = v_ref.shape[0]
+    slots = gctx_ref.shape[0]
     count = seg_ends(lens_ref, lens_ref.shape[1])[-1]
     put_strips(dwo_ref, t_mm(ctx_ref[...], gs1_ref[...]))
     fill_extended(ext_ref, gctx_ref[...], gleft_ref[...], gright_ref[...], count)
     conv_into(gv_ref, ext_ref, taps_ref, slots, True, False)
-    fill_extended(ext_ref, v_ref[...], left_ref[...], right_ref[...], count)
-    taps_grad_into(scr_ref, gctx_ref, ext_ref, slots)
+    taps_grad_into(scr_ref, gctx_ref, values_ref, slots)
     gtaps_ref[...] = taps_sums(scr_ref)
 
 
-def conv_back(lens, v, left, right, gctx, gleft, gright, taps, ctx, gs1):
-    slots, width = v.shape
+def conv_back(lens, ext, gctx, gleft, gright, taps, ctx, gs1):
+    slots, width = gctx.shape
     return pl.pallas_call(
         conv_back_kernel,
-        in_specs=[smem()] + [whole()] * 9,
+        in_specs=[smem()] + [whole()] * 7,
         out_specs=[whole()] * 3,
         out_shape=[shape(slots, width), shape(40, LANES), shape(width // LANES, width, LANES)],
         scratch_shapes=[pltpu.VMEM((slots + 40, width), f32), pltpu.VMEM((CONV, 8, width), f32)],
         compiler_params=params(),
         name="conv_back",
-    )(lens, v, left, right, gctx, gleft, gright, taps, ctx, gs1)
+    )(lens, ext, gctx, gleft, gright, taps, ctx, gs1)
 
 
 def project_back_kernel(
@@ -1763,16 +1723,10 @@
     x = tokens.reshape(slots, width)
     cot = cotangent.reshape(slots, width)
     lens = segment_lens
-    taps = jnp.repeat(conv_taps, DH, axis=1)
-
-    q, k, v, land, rim = project(lens, x, query_weight, key_weight, value_weight, query_bias, value_bias)
-    lands, left, right = land_exchange(n, land, rim)
-    ql = lands[:, 0].reshape(DH, width)
-    kl = lands[:, 1].reshape(DH, width)
-    parts, raised, tops = far_local(lens, k, v, ql)
-    b, *saved = far_exchange(n, parts, ql, kl)
-    near, ctx, h1, u1, inv1, ext = attend(
-        lens, q, v, kl, b, left, right, taps, x, output_weight, output_bias, first_gain, first_bias
+
+    q, k, v, raised, near, ctx, ext, h1, u1, tops, b, ql, kl, *saved, taps, inv1 = front(
+        n, lens, x, conv_taps, query_bias, value_bias, output_bias, first_gain, first_bias,
+        query_weight, key_weight, value_weight, output_weight,
     )
     pre, layer_out, gs2, small2 = ffn_forward(
         lens, h1, inner_weight, inner_bias.reshape(1, -1), outer_weight, outer_bias, cot, second_gain, second_bias
@@ -1794,7 +1748,7 @@
         c, gleft, gright, gl = blend_exchange(n, gblend, grim, ql, kl, saved)
         gkf, gvf, back = far_back(n, lens, k, v, raised, tops, b, c, ql, gkl, gl)
         own = land_return(n, back)
-        gvc, gtaps, d_output = conv_back(lens, v, left, right, gctx, gleft, gright, taps, ctx, gs1)
+        gvc, gtaps, d_output = conv_back(lens, ext, gctx, gleft, gright, taps, ctx, gs1)
         input_grad, d_query, d_key, d_value, small0 = project_back(
             lens, x, gs1, gqn, gkf, gvc, gvf, own, query_weight, key_weight, value_weight
         )

time: 382 us -> 353 us (0.924)
  Pallas kernels: 375 us -> 348 us
    pallas_call x5 -> x1, Pallas kernels: 75.5 us -> 47.7 us  [front(): pl.pallas_call(partial(front_kernel, n), in_specs=[smem()] + [whole()] *...]
where the time goes in v4:
time: 353 us; the launch traced here: 352 us
  Pallas kernels  348 us (99%)
  local copies, waits for them, and re-layouts  3.94 us (1%)
    pallas_call x1, Pallas kernels, tail(): pl.pallas_call(tail_kernel, in_specs=[smem()] + [anywhere] * len(big) + [...  252 us
    pallas_call x1, Pallas kernels, front(): pl.pallas_call(partial(front_kernel, n), in_specs=[smem()] + [whole()] *...  47.7 us
    pallas_call x1, Pallas kernels, ffn_forward(): pl.pallas_call(forward_kernel, grid=(inner // width,), in_specs=[smem(),...  26.8 us
    pallas_call x1, Pallas kernels, place_strips(): pl.pallas_call(place_strips_kernel, in_specs=[anywhere, whole()], out_spe...  21 us

profile of v4, /device:TPU:0, one launch (start us, length us, event | category | flops | bytes accessed | tf_op | source)
XLA Modules:
  0.0 352.5 jit_solution(10012094693150077074)
XLA Ops:
  0.7 1.4 copy.37.taps_in
  2.0 47.7 %front.1 = (f32[512,768]{1,0:T(8,128)}, f32[512,768]{1,0:T(8,128)}, f32[512,768]{1,0:T(8,128)}, f32[512,768]{1,0:T(8,128)}, f32[512,768]{1,0:T(8,128)}, /*index=...) custom-call(s32[1,8]{1,0:T(1,128)} %lens_ref.5, ...), custom_call_target="tpu_custom_call" | custom-call | tf_op jit(solution)/shard_map/front/pallas_call | solution.py:660
  49.8 26.8 %ffn_forward.1 = (f32[512,3072]{1,0:T(8,128)}, f32[512,768]{1,0:T(8,128)}, f32[512,768]{1,0:T(8,128)}, f32[8,768]{1,0:T(8,128)}) custom-call(s32[1,8]{1,0:T(1,128)} %lens_ref.5, f32[512,768]{1,0:T(8,128)} %get-tuple-element.62.h1_ref.h1_hbm, f32[768,3072]{1,0:T(8,128)} %win_hbm.1, f32[1,3072]{1,0:T(1,128)} %bitcast.11, f32[3072,768]{1,0:T(8,128)} %wout_hbm.1, ...), custom_call_target="tpu_custom_call" | custom-call | tf_op jit(solution)/shard_map/ffn_forward/pallas_call | solution.py:734
  76.6 252.3 %tail.1 = (f32[2,36,16,48,128]{4,3,2,1,0:T(8,128)}, f32[112,128]{1,0:T(8,128)}, f32[512,768]{1,0:T(8,128)}) custom-call(s32[1,8]{1,0:T(1,128)} %lens_ref.5, f32[512,768]{1,0:T(8,128)} %get-tuple-element.64.gs2_hbm, f32[512,768]{1,0:T(8,128)} %get-tuple-element.62.h1_ref.h1_hbm, f32[512,768]{1,0:T(8,128)} %get-tuple-element.65.u1_hbm, ...), custom_call_target="tpu_custom_call" | custom-call | tf_op jit(solution)/shard_map/tail/pallas_call | solution.py:1630
  328.9 0.0 copy-start
  328.9 21.0 %place_strips.1 = (f32[3072,768]{1,0:T(8,128)}, f32[768,3072]{1,0:T(8,128)}, f32[768,768]{1,0:T(8,128)}, f32[768,768]{1,0:T(8,128)}, f32[768,768]{1,0:T(8,128)},...) custom-call(f32[2,36,768,128]{3,2,1,0:T(8,128)} %bitcast.6, ...), custom_call_target="tpu_custom_call" | custom-call | tf_op jit(solution)/shard_map/place_strips/pallas_call | solution.py:1705
  349.9 1.4 copy.38
  351.3 0.0 copy-done
  351.3 1.1 copy.40
Async XLA Ops:
  328.9 22.4 %copy-start = (f32[512,768]{1,0:T(8,128)S(1)}, f32[512,768]{1,0:T(8,128)}, u32[]{:S(2)}) copy-start(f32[512,768]{1,0:T(8,128)} %get-tuple-element.87) | copy-start | bytes 4718596

commit v5 on v4

--- a/solution.py
+++ b/solution.py
@@ -278,6 +278,22 @@
     return 0.25 * mm_t(g, q, TOP) + mm(core.T, gp, TOP), gcore + mm_t(gp, z, TOP)
 
 
+def newton_lead(z, prod):
+    zp = mm(z, prod, TOP)
+    zpp = mm(zp, prod, TOP)
+    return jnp.concatenate([0.25 * z.T, -0.25 * zp.T, 0.25 * zpp.T], axis=0)
+
+
+def newton_short(g, gcore, lead, core, z, prod, r, q):
+    gqrs = mm(lead, g, TOP)
+    gq, gr, gs = [gqrs[at : at + LANES] for at in range(0, 3 * LANES, LANES)]
+    left = jnp.concatenate([gq, gr], axis=1)
+    right = jnp.concatenate([r, 7.0 * eye(LANES) - prod], axis=1)
+    gp = -mm_t(left, right, TOP) - gs
+    through = mm(jnp.concatenate([g, core.T], axis=1), jnp.concatenate([0.25 * q.T, gp], axis=0), TOP)
+    return through, gcore + mm_t(gp, z, TOP)
+
+
 def core_back(g, gcore, core, first, ql_ref, kl_ref, gl_ref, me):
     mask = head_mask(LANES)
     colsum = jnp.sum(core, axis=0, keepdims=True)
@@ -440,18 +456,13 @@
     n, lens_ref, x_ref, taps_in, bq_ref, bv_ref, bo_ref, g1_ref, b1_ref, wq_hbm, wk_hbm, wv_hbm, wo_hbm,
     q_out, k_out, v_out, p_out, near_out, ctx_out, ext_out, h1_out, u1_out,
     m_ref, b_ref, ql_ref, kl_ref, core_ref, zs_ref, ps_ref, rs_ref, qs_ref, mx_ref, taps_ref, inv1_ref,
-    w, wo, bias, stack, ext, f_ref, mine, lands, rim, left, right, land,
+    w, bias, stack, ext, f_ref, mine, lands, rim, left, right, land,
     load, out, ms, mr, ls, lr, s1, r1, s2, r2,
 ):
     _, slots, width = stack.shape
     segs = mine.shape[1]
     v, q, k, p, near, ctx, h1, u1 = [stack.at[i] for i in range(8)]
-    loads = [
-        pltpu.make_async_copy(hbm.at[:, pl.ds(g * QUAD, QUAD)], w.at[i * QUADS + g], load.at[i * QUADS + g])
-        for i, hbm in enumerate((wv_hbm, wq_hbm, wk_hbm))
-        for g in range(QUADS)
-    ]
-    loads.append(pltpu.make_async_copy(wo_hbm, wo, load.at[3 * QUADS]))
+    loads = [pltpu.make_async_copy(hbm, w.at[i], load.at[i]) for i, hbm in enumerate((wv_hbm, wq_hbm, wk_hbm, wo_hbm))]
     for copy in loads:
         copy.start()
     leaving = []
@@ -466,17 +477,15 @@
     valid = valid_rows(count, slots)
     member = member_rows(ends, slots)
     inv = inverse_lens(lens_ref, segs)
-    for g in range(QUADS):
-        cols = pl.ds(g * QUAD, QUAD)
-        bias[g] = jnp.broadcast_to(bv_ref[cols][None, :], (8, QUAD))
-        bias[QUADS + g] = jnp.broadcast_to(bq_ref[cols][None, :], (8, QUAD))
-        bias[2 * QUADS + g] = jnp.zeros((8, QUAD), f32)
+    bias[0:1, :] = bv_ref[...][None, :]
+    bias[1:2, :] = bq_ref[...][None, :]
+    bias[2:3, :] = jnp.zeros((1, width), f32)
 
     def one(i, carry):
-        pltpu.make_async_copy(wv_hbm.at[:, pl.ds(0, QUAD)], w.at[i], load.at[i]).wait()
-        stack[i // QUADS, :, quad(lax.rem(i, QUADS))] = mm(x_ref[...], w[i]) + bias[i, 0:1, :]
-
-        @pl.when(i == QUADS - 1)
+        pltpu.make_async_copy(wv_hbm, w.at[i], load.at[i]).wait()
+        stack[i] = mm(x_ref[...], w[i]) + bias[pl.ds(i, 1), :]
+
+        @pl.when(i == 0)
         def _():
             v[...] = jnp.where(valid, v[...], 0.0)
             rim[...] = rims_of(v[...], count)
@@ -486,7 +495,7 @@
         return carry
 
     up, down = rim_copies(n, me, rim, left, right, ms, mr)
-    lax.fori_loop(0, 3 * QUADS, one, 0)
+    lax.fori_loop(0, 3, one, 0)
     mine[0] = mm(member, q[...]) * inv
     mine[1] = mm(member, k[...]) * inv
     for d in range(1, n):
@@ -497,7 +506,7 @@
     leave(v, v_out)
     row = lax.broadcasted_iota(jnp.int32, (HEADS, width), 0)
     col = lax.broadcasted_iota(jnp.int32, (HEADS, width), 1) >> 6
-    taps_ref[...] = mm(taps_in[...], jnp.where(row == col, 1.0, 0.0), TOP)
+    taps_ref[...] = t_mm(taps_in[...], jnp.where(row == col, 1.0, 0.0), TOP)
     rim_wait(n, me, up, down)
     fill_extended(ext, v[...], left[...], right[...], count)
     leave(ext, ext_out)
@@ -616,13 +625,7 @@
     leave(ctx, ctx_out)
     loads[-1].wait()
 
-    def project(g, carry):
-        cols = quad(g)
-        u1[:, cols] = mm(ctx[...], wo[:, cols])
-        return carry
-
-    lax.fori_loop(0, QUADS, project, 0)
-    unit, scale = norm_stats(x_ref[...] + (u1[...] + bo_ref[...][None, :]))
+    unit, scale = norm_stats(x_ref[...] + (mm(ctx[...], w[3]) + bo_ref[...][None, :]))
     h1[...] = unit * g1_ref[...][None, :] + b1_ref[...][None, :]
     leave(h1, h1_out)
     u1[...] = unit
@@ -656,7 +659,6 @@
     anywhere = pl.BlockSpec(memory_space=pl.ANY)
     square = (LANES, LANES)
     rows = shape(slots, width)
-    count = 3 * QUADS
     return pl.pallas_call(
         partial(front_kernel, n),
         in_specs=[smem()] + [whole()] * 7 + [anywhere] * 4,
@@ -668,10 +670,10 @@
             shape(DH, LANES), shape(CONV, width), shape(slots, 1),
         ],
         scratch_shapes=[
-            vm(count, width, QUAD), vm(width, width), vm(count, 8, QUAD), vm(8, slots, width), vm(slots + 40, width),
+            vm(4, width, width), vm(8, width), vm(8, slots, width), vm(slots + 40, width),
             vm(PAIRS, MSG, LANES), vm(2, segs, width), vm(n, 2, segs, width), vm(2 * RIM, width), vm(RIM, width),
             vm(RIM, width), vm(n, MSG, LANES),
-            dma((count + 1,)), dma((9,)), dma((2,)), dma((2,)), dma((n,)), dma((n,)), dma((PAIRS,)), dma((n,)),
+            dma((4,)), dma((9,)), dma((2,)), dma((2,)), dma((n,)), dma((n,)), dma((PAIRS,)), dma((n,)),
             dma((n,)), dma((n,)),
         ],
         compiler_params=params(collective_id=1, has_side_effects=True),
@@ -1073,7 +1075,7 @@
         for j in range(ref.shape[0] // LANES):
             ref[pl.ds(j * LANES, LANES)] = s_ref[at, :]
             at += 1
-    outs[-1][...] = s_ref[at : at + CONV, :HEADS]
+    outs[-1][...] = s_ref[at : at + 40, :].T[:HEADS, :CONV]
 
 
 def reduce_stages(gw, o_ref, bufs, sems):
@@ -1233,7 +1235,7 @@
     return stages, (by_core, by_x, by_y, near_z, opposite), remote
 
 
-LAG = tuple(range(0, 2 * STAGES, 2))
+LAG = (0, 1, 3, 5, 7, 9, 11, 13, 15, 17, 19, 21, 22)
 CHUNKS = 36
 GW_SLOTS = 4
 RING_ACC = 6
@@ -1242,7 +1244,7 @@
 RING_Z = 6
 RING_AG = 16
 SEQ_DEVICES = 8
-SMALL_AT = 36
+SMALL_AT = 44
 ENTER = 2
 HELD = 30
 GAP = 2
@@ -1251,7 +1253,8 @@
 FFN_AT = (0, 4, 8, 13)
 GS1_AT = 17
 OUTPUT_AT, VALUE_AT, QUERY_AT, KEY_AT = 21, 28, 32, 33
-INPUT_AT = (34, 35, 36)
+INPUT_AT = (41, 42, 43)
+TAPS_AT = 36
 
 
 def pick(t, table):
@@ -1286,7 +1289,7 @@
     o_ref, so_ref, ig_hbm,
     acc, lc, l1, mid, lz, l3, ag, sb, sl, gw,
     stack, w, ext, gext, tap_scr, gtaps, small0, small1, dbi,
-    gb, rim, gkl, gql, gl, land, cmsg, gleft, gright, ng, ncore, ret, rland, own,
+    gb, rim, gkl, gql, gl, land, cmsg, gleft, gright, ng, ncore, nlead, ret, rland, own,
     loads, ig_sem, b1s, b1r, b2s, b2r, ms, mr, rets, retr, ss, sr,
     *sems,
 ):
@@ -1339,19 +1342,10 @@
     count = ends[-1]
 
     def weight_event(e, left, right):
-        def one(g, carry):
-            block = t_mm(stack[left, :, quad(g)], stack[right])
-            put_strips(gw, block, quad(g), lax.rem(e, GW_SLOTS) * PAIRS)
-            return carry
-
-        lax.fori_loop(0, QUADS, one, 0)
+        put_strips(gw, t_mm(stack[left], stack[right]), slice(None), lax.rem(e, GW_SLOTS) * PAIRS)
 
     def through_event(source, target, weight):
-        def one(g, carry):
-            stack[target, :, quad(g)] += mm_t(stack[source], w[weight, quad(g), :])
-            return carry
-
-        lax.fori_loop(0, QUADS, one, 0)
+        stack[target] += mm_t(stack[source], w[weight])
 
     def inner_event(j):
         @pl.when(j == 0)
@@ -1434,15 +1428,18 @@
 
             ng[...] = inverse_grad(gblend, mixed)
             ncore[...] = jnp.zeros_like(ncore)
+            nlead[...] = newton_lead(zs_ref[NEWTON - 1], ps_ref[NEWTON - 1])
 
         gl[...] = jnp.zeros_like(gl)
 
     def ev_newton(step):
         @pl.when(owner)
         def _():
-            ng[...], ncore[...] = newton_back(
-                ng[...], ncore[...], core_ref[...], zs_ref[step], ps_ref[step], rs_ref[step], qs_ref[step]
+            lead = newton_lead(zs_ref[jnp.maximum(step - 1, 0)], ps_ref[jnp.maximum(step - 1, 0)])
+            ng[...], ncore[...] = newton_short(
+                ng[...], ncore[...], nlead[...], core_ref[...], zs_ref[step], ps_ref[step], rs_ref[step], qs_ref[step]
             )
+            nlead[...] = lead
 
     def ev_core():
         @pl.when(owner)
@@ -1553,6 +1550,23 @@
         def _():
             event(*[value for value, _ in columns])
 
+    def by_group(t, table, size=6):
+        for low in range(0, max(when for when, _ in table) + 1, size):
+            mine = [row for row in table if low <= row[0] < low + size]
+            if mine:
+
+                @pl.when((t >= low) & (t < low + size))
+                def _(mine=mine):
+                    for when, event in mine:
+                        at_tick(t, when, event)
+
+    copies = [(when, copy.start) for when, copy in starting] + [(when, copy.wait) for when, copy in waiting]
+    others = [(FFN_AT[3] + 3, ev_norm), (GS1_AT, ev_rims)]
+    last = [
+        (GS1_AT + 12, ev_core), (GS1_AT + 12, ev_return), (GS1_AT + 14, ev_own),
+        (INPUT_AT[2], lambda: pltpu.make_async_copy(ig, ig_hbm, ig_sem.at[0]).start()),
+    ] + [(SMALL_AT + 2 * i, partial(ev_small, i)) for i in range(SMALL_STEPS + 1)]
+
     def tick(t, carry):
         for stage, run in reversed(list(enumerate(stages))):
             since = t - ENTER - LAG[stage]
@@ -1562,10 +1576,7 @@
             def _(run=run, at=at):
                 run(at)
 
-        for when, copy in starting:
-            at_tick(t, when, copy.start)
-        for when, copy in waiting:
-            at_tick(t, when, copy.wait)
+        by_group(t, copies)
         block, hit = pick(t, {when: j for j, when in enumerate(FFN_AT)})
 
         @pl.when(hit)
@@ -1574,23 +1585,24 @@
 
         by_table(t, through, through_event)
         by_table(t, weights, weight_event)
-        at_tick(t, FFN_AT[3] + 3, ev_norm)
-        at_tick(t, GS1_AT, ev_rims)
-        at_ticks(t, GS1_AT + 1, 1, QUADS, ev_near)
-        at_tick(t, GS1_AT + 3, ev_blend)
-        at_tick(t, GS1_AT + 5, ev_owner)
-        at_ticks(t, GS1_AT + 6, 1, NEWTON, lambda i: ev_newton(NEWTON - 1 - i))
-        at_ticks(t, GS1_AT + 5, 1, 4, ev_conv)
-        at_tick(t, GS1_AT + 8, ev_mixed)
-        at_ticks(t, GS1_AT + 8, 1, QUADS, ev_far)
-        at_tick(t, GS1_AT + 10, ev_values)
-        at_tick(t, GS1_AT + 12, ev_core)
-        at_tick(t, GS1_AT + 12, ev_return)
-        at_ticks(t, GS1_AT + 11, 1, 4, ev_taps)
-        at_tick(t, GS1_AT + 14, ev_own)
-        at_tick(t, INPUT_AT[2], lambda: pltpu.make_async_copy(ig, ig_hbm, ig_sem.at[0]).start())
-        for i in range(SMALL_STEPS + 1):
-            at_tick(t, SMALL_AT + 2 * i, partial(ev_small, i))
+        by_group(t, others)
+
+        @pl.when((t > GS1_AT) & (t < GS1_AT + 12))
+        def _():
+            at_ticks(t, GS1_AT + 1, 1, QUADS, ev_near)
+            at_tick(t, GS1_AT + 3, ev_blend)
+            at_tick(t, GS1_AT + 5, ev_owner)
+            at_ticks(t, GS1_AT + 6, 1, NEWTON, lambda i: ev_newton(NEWTON - 1 - i))
+            at_ticks(t, GS1_AT + 5, 1, 4, ev_conv)
+            at_tick(t, GS1_AT + 8, ev_mixed)
+            at_ticks(t, GS1_AT + 8, 1, QUADS, ev_far)
+            at_tick(t, GS1_AT + 10, ev_values)
+
+        @pl.when(t >= GS1_AT + 12)
+        def _():
+            at_ticks(t, TAPS_AT, 1, 4, ev_taps)
+            by_group(t, last)
+
         return carry
 
     lax.fori_loop(0, CHUNKS + ENTER + GAP + LAG[-1], tick, 0)
@@ -1641,7 +1653,7 @@
             vm(CONV, 8, width), vm(40, LANES), vm(8, width), vm(8, width), vm(1, 4 * width),
             vm(PAIRS, DH, LANES), vm(2 * RIM, width), vm(DH, width), vm(DH, width), vm(2, DH, width),
             vm(n, DH, LANES), vm(PAIRS, MSG, LANES), vm(RIM, width), vm(RIM, width), vm(LANES, LANES), vm(LANES, LANES),
-            vm(n, 2, segs, width), vm(n, 2, segs, width), vm(2, segs, width),
+            vm(3 * LANES, LANES), vm(n, 2, segs, width), vm(n, 2, segs, width), vm(2, segs, width),
             dma((27,)), dma((1,)), dma((PAIRS,)), dma((n,)), dma((n,)), dma((n,)), dma((2,)), dma((2,)),
             dma((n,)), dma((n,)), dma((SMALL_STEPS,)), dma((SMALL_STEPS,)),
             one, one, one, one, one, zsem, one, one, one, zsem, one, dma((at, 2)), one, one,
@@ -1706,7 +1718,7 @@
         place_strips_kernel,
         in_specs=[anywhere, whole()],
         out_specs=[anywhere] * len(shapes) + [whole()] * 10,
-        out_shape=[shape(*dims) for dims in shapes] + [shape(width)] * 8 + [shape(shapes[0][0]), shape(CONV, HEADS)],
+        out_shape=[shape(*dims) for dims in shapes] + [shape(width)] * 8 + [shape(shapes[0][0]), shape(HEADS, CONV)],
         scratch_shapes=[pltpu.VMEM((PLACE_SLOTS, STRIP, LANES), f32), dma((PLACE_SLOTS,)), dma((PLACE_SLOTS,))],
         compiler_params=params(),
         name="place_strips",
@@ -1725,7 +1737,7 @@
     lens = segment_lens
 
     q, k, v, raised, near, ctx, ext, h1, u1, tops, b, ql, kl, *saved, taps, inv1 = front(
-        n, lens, x, conv_taps, query_bias, value_bias, output_bias, first_gain, first_bias,
+        n, lens, x, conv_taps.T, query_bias, value_bias, output_bias, first_gain, first_bias,
         query_weight, key_weight, value_weight, output_weight,
     )
     pre, layer_out, gs2, small2 = ffn_forward(
@@ -1757,14 +1769,14 @@
         small = sums[6:]
         sums = (
             [unstrip_tall(sums[0], width // LANES)] + [unstrip(s) for s in sums[1:6]]
-            + [small[0][0], small[0][1], *small[1][:3], *small[2][:3], small[3][0], small[4][:CONV, :HEADS]]
+            + [small[0][0], small[0][1], *small[1][:3], *small[2][:3], small[3][0], small[4][:CONV, :HEADS].T]
         )
     d_outer, d_inner, d_output, d_value, d_query, d_key, *vectors = sums
     d_query_bias, d_value_bias, d_first_gain, d_first_bias, d_output_bias = vectors[:5]
     d_second_gain, d_second_bias, d_outer_bias, d_inner_bias, d_taps = vectors[5:]
     return (
         layer_out.reshape(tokens.shape), input_grad.reshape(tokens.shape),
-        d_query, d_query_bias, d_key, d_value, d_value_bias, d_taps,
+        d_query, d_query_bias, d_key, d_value, d_value_bias, d_taps.T,
         d_output, d_output_bias, d_first_gain, d_first_bias,
         d_inner, d_inner_bias, d_outer, d_outer_bias, d_second_gain, d_second_bias,
     )

time: 353 us -> 337 us (0.955)
  Pallas kernels: 348 us -> 335 us
    pallas_call x1, Pallas kernels: 252 us -> 241 us  [tail(): pl.pallas_call(tail_kernel, in_specs=[smem()] + [anywhere] * len(big) + [...]
where the time goes in v5:
time: 337 us
  Pallas kernels  335 us (99%)
    pallas_call x1, Pallas kernels, tail(): pl.pallas_call(tail_kernel, in_specs=[smem()] + [anywhere] * len(big) + [...  241 us
    pallas_call x1, Pallas kernels, front(): pl.pallas_call(partial(front_kernel, n), in_specs=[smem()] + [whole()] *...  46.7 us
    pallas_call x1, Pallas kernels, ffn_forward(): pl.pallas_call(forward_kernel, grid=(inner // width,), in_specs=[smem(),...  26.8 us
    pallas_call x1, Pallas kernels, place_strips(): pl.pallas_call(place_strips_kernel, in_specs=[anywhere, whole()], out_spe...  21 us

profile of v5, /device:TPU:0, one launch (start us, length us, event | category | flops | bytes accessed | tf_op | source)
XLA Modules:
  0.0 337.1 jit_solution(5238184455265493551)
XLA Ops:
  0.7 46.7 %front.1 = (f32[512,768]{1,0:T(8,128)}, f32[512,768]{1,0:T(8,128)}, f32[512,768]{1,0:T(8,128)}, f32[512,768]{1,0:T(8,128)}, f32[512,768]{1,0:T(8,128)}, /*index=...) custom-call(s32[1,8]{1,0:T(1,128)} %lens_ref.5, ...), custom_call_target="tpu_custom_call" | custom-call | tf_op jit(solution)/shard_map/front/pallas_call | solution.py:662
  47.3 26.8 %ffn_forward.1 = (f32[512,3072]{1,0:T(8,128)}, f32[512,768]{1,0:T(8,128)}, f32[512,768]{1,0:T(8,128)}, f32[8,768]{1,0:T(8,128)}) custom-call(s32[1,8]{1,0:T(1,128)} %lens_ref.5, f32[512,768]{1,0:T(8,128)} %get-tuple-element.62.h1_ref.h1_hbm, f32[768,3072]{1,0:T(8,128)} %win_hbm.1, f32[1,3072]{1,0:T(1,128)} %bitcast.13, f32[3072,768]{1,0:T(8,128)} %wout_hbm.1, ...), custom_call_target="tpu_custom_call" | custom-call | tf_op jit(solution)/shard_map/ffn_forward/pallas_call | solution.py:736
  74.2 240.7 %tail.1 = (f32[2,36,16,48,128]{4,3,2,1,0:T(8,128)}, f32[112,128]{1,0:T(8,128)}, f32[512,768]{1,0:T(8,128)}) custom-call(s32[1,8]{1,0:T(1,128)} %lens_ref.5, f32[512,768]{1,0:T(8,128)} %get-tuple-element.64.gs2_hbm, f32[512,768]{1,0:T(8,128)} %get-tuple-element.62.h1_ref.h1_hbm, f32[512,768]{1,0:T(8,128)} %get-tuple-element.65.u1_hbm, ...), custom_call_target="tpu_custom_call" | custom-call | tf_op jit(solution)/shard_map/tail/pallas_call | solution.py:1642
  314.9 0.0 copy-start
  314.9 21.0 %place_strips.1 = (f32[3072,768]{1,0:T(8,128)}, f32[768,3072]{1,0:T(8,128)}, f32[768,768]{1,0:T(8,128)}, f32[768,768]{1,0:T(8,128)}, f32[768,768]{1,0:T(8,128)},...) custom-call(f32[2,36,768,128]{3,2,1,0:T(8,128)} %bitcast.8, ...), custom_call_target="tpu_custom_call" | custom-call | tf_op jit(solution)/shard_map/place_strips/pallas_call | solution.py:1717
  335.9 0.0 copy-done
  336.0 1.1 copy.38
Async XLA Ops:
  314.9 21.1 %copy-start = (f32[512,768]{1,0:T(8,128)S(1)}, f32[512,768]{1,0:T(8,128)}, u32[]{:S(2)}) copy-start(f32[512,768]{1,0:T(8,128)} %get-tuple-element.87) | copy-start | bytes 4718596

commit v6 on v5

--- a/solution.py
+++ b/solution.py
@@ -246,6 +246,17 @@
 MSG = DH + 8
 
 
+def owner_of(pair, n):
+    return pair if pair < PAIRS // 2 else pair + n // 2 - PAIRS // 2
+
+
+def pair_at(me, n):
+    half = PAIRS // 2
+    low = me < half
+    owns = low | ((me >= n // 2) & (me < n // 2 + half))
+    return owns, jnp.where(low, me, jnp.where(owns, me - n // 2 + half, 0))
+
+
 def eye(size):
     row = lax.broadcasted_iota(jnp.int32, (size, size), 0)
     col = lax.broadcasted_iota(jnp.int32, (size, size), 1)
@@ -294,7 +305,7 @@
     return through, gcore + mm_t(gp, z, TOP)
 
 
-def core_back(g, gcore, core, first, ql_ref, kl_ref, gl_ref, me):
+def core_back(g, gcore, core, first, ql_ref, kl_ref, gl_ref, pair):
     mask = head_mask(LANES)
     colsum = jnp.sum(core, axis=0, keepdims=True)
     square = pair_sums(colsum * colsum)
@@ -302,7 +313,7 @@
     dot = pair_sums(jnp.sum(g * first, axis=0, keepdims=True))
     gcore = gcore + g.T / sigma - jnp.where(mask, dot / square * colsum, 0.0)
     gscore = core * (gcore - jnp.sum(core * gcore, axis=1, keepdims=True)) * SCALE
-    lanes = pl.ds(pl.multiple_of(me * LANES, LANES), LANES)
+    lanes = pl.ds(pl.multiple_of(pair * LANES, LANES), LANES)
     query = spread(ql_ref[:, lanes], mask)
     key = spread(kl_ref[:, lanes], mask)
     gl_ref[...] = jnp.zeros_like(gl_ref)
@@ -316,23 +327,24 @@
     land, s1, r1, s2, r2, rsend, rrecv,
 ):
     me = greet_all(n)
+    owns, pair_here = pair_at(me, n)
     for p in range(PAIRS):
 
-        @pl.when(me != p)
+        @pl.when(me != owner_of(p, n))
         def _(p=p):
-            to_seq(g_ref.at[p], land.at[me], s1.at[p], r1.at[me], p).start()
+            to_seq(g_ref.at[p], land.at[me], s1.at[p], r1.at[me], owner_of(p, n)).start()
 
     up, down = rim_copies(n, me, rim_ref, left_ref, right_ref, rsend, rrecv)
     rim_start(n, me, up, down, left_ref, right_ref)
 
-    @pl.when(me >= PAIRS)
+    @pl.when(jnp.logical_not(owns))
     def _():
         gl_ref[...] = jnp.zeros_like(gl_ref)
 
-    @pl.when(me < PAIRS)
+    @pl.when(owns)
     def _():
         mask = head_mask(LANES)
-        land[me] = g_ref[me]
+        land[me] = g_ref[pair_here]
         for s in range(n):
 
             @pl.when(me != s)
@@ -344,38 +356,38 @@
             gblend = gblend + land[s]
         mixed = mx_ref[...]
         gmixed = mm(gblend, zs_ref[NEWTON], TOP)
-        c_ref[me, 0:DH, :] = gmixed
+        c_ref[pair_here, 0:DH, :] = gmixed
         dots = jnp.sum(gmixed * mixed, axis=0, keepdims=True)
         pad = jnp.zeros((MSG - DH - 1, LANES), f32)
-        c_ref[me, DH:MSG, :] = jnp.concatenate([dots, pad], axis=0)
+        c_ref[pair_here, DH:MSG, :] = jnp.concatenate([dots, pad], axis=0)
         for t in range(n):
 
             @pl.when(me != t)
             def _(t=t):
-                to_seq(c_ref.at[me], c_ref.at[me], s2.at[t], r2.at[me], t).start()
+                to_seq(c_ref.at[pair_here], c_ref.at[pair_here], s2.at[t], r2.at[pair_here], t).start()
 
         gcore = jnp.zeros((LANES, LANES), f32)
         g = inverse_grad(gblend, mixed)
         for step in reversed(range(NEWTON)):
             g, gcore = newton_back(g, gcore, core_ref[...], zs_ref[step], ps_ref[step], rs_ref[step], qs_ref[step])
-        core_back(g, gcore, core_ref[...], zs_ref[0], ql_ref, kl_ref, gl_ref, me)
+        core_back(g, gcore, core_ref[...], zs_ref[0], ql_ref, kl_ref, gl_ref, pair_here)
 
     for p in range(PAIRS):
 
-        @pl.when(me != p)
+        @pl.when(me != owner_of(p, n))
         def _(p=p):
-            to_seq(c_ref.at[p], c_ref.at[p], s2.at[p], r2.at[p], p).wait_recv()
-            to_seq(g_ref.at[p], land.at[me], s1.at[p], r1.at[me], p).wait_send()
+            to_seq(c_ref.at[p], c_ref.at[p], s2.at[p], r2.at[p], owner_of(p, n)).wait_recv()
+            to_seq(g_ref.at[p], land.at[me], s1.at[p], r1.at[me], owner_of(p, n)).wait_send()
 
     rim_wait(n, me, up, down)
 
-    @pl.when(me < PAIRS)
+    @pl.when(owns)
     def _():
         for t in range(n):
 
             @pl.when(me != t)
             def _(t=t):
-                to_seq(c_ref.at[me], c_ref.at[me], s2.at[t], r2.at[me], t).wait_send()
+                to_seq(c_ref.at[pair_here], c_ref.at[pair_here], s2.at[t], r2.at[pair_here], t).wait_send()
 
 
 def blend_exchange(n, gblend, rim, ql, kl, saved):
@@ -472,6 +484,7 @@
         leaving[-1].start()
 
     me = greet_signal(n)
+    owns, pair_here = pair_at(me, n)
     ends = seg_ends(lens_ref, segs)
     count = ends[-1]
     valid = valid_rows(count, slots)
@@ -494,12 +507,23 @@
 
         return carry
 
+    def land_copy(kind, source, d, target):
+        return to_seq(mine.at[kind], lands.at[source, kind], ls.at[kind, d], lr.at[kind, source], target)
+
+    def land_rows(kind, rows_ref):
+        for d in range(1, n):
+            source = lax.rem(me + d, n)
+            land_copy(kind, source, d, source).wait_recv()
+        for s in range(n):
+            rows_ref[slice(s * segs, (s + 1) * segs), :] = lands[s, kind]
+
     up, down = rim_copies(n, me, rim, left, right, ms, mr)
     lax.fori_loop(0, 3, one, 0)
     mine[0] = mm(member, q[...]) * inv
     mine[1] = mm(member, k[...]) * inv
-    for d in range(1, n):
-        to_seq(mine, lands.at[me], ls.at[d], lr.at[me], lax.rem(me + d, n)).start()
+    for kind in range(2):
+        for d in range(1, n):
+            land_copy(kind, me, d, lax.rem(me + d, n)).start()
     lands[me] = mine[...]
     leave(q, q_out)
     leave(k, k_out)
@@ -512,13 +536,7 @@
     leave(ext, ext_out)
     conv_into(ctx, ext, taps_ref, slots, False, False)
 
-    for d in range(1, n):
-        source = lax.rem(me + d, n)
-        to_seq(mine, lands.at[source], ls.at[d], lr.at[source], source).wait_recv()
-    for s in range(n):
-        rows = slice(s * segs, (s + 1) * segs)
-        ql_ref[rows, :] = lands[s, 0]
-        kl_ref[rows, :] = lands[s, 1]
+    land_rows(0, ql_ref)
 
     def far(g, carry):
         cols = quad(g)
@@ -541,16 +559,17 @@
     lax.fori_loop(0, QUADS, far, 0)
     for pair in range(PAIRS):
 
-        @pl.when(me != pair)
+        @pl.when(me != owner_of(pair, n))
         def _(pair=pair):
-            to_seq(f_ref.at[pair], land.at[me], s1.at[pair], r1.at[me], pair).start()
+            to_seq(f_ref.at[pair], land.at[me], s1.at[pair], r1.at[me], owner_of(pair, n)).start()
 
     leave(p, p_out)
-
-    @pl.when(me < PAIRS)
+    land_rows(1, kl_ref)
+
+    @pl.when(owns)
     def _():
         mask = head_mask(LANES)
-        lanes = pl.ds(pl.multiple_of(me * LANES, LANES), LANES)
+        lanes = pl.ds(pl.multiple_of(pair_here * LANES, LANES), LANES)
         core = core_of(spread(ql_ref[:, lanes], mask), spread(kl_ref[:, lanes], mask), mask)
         core_ref[...] = core
         colsum = jnp.sum(core, axis=0, keepdims=True)
@@ -569,7 +588,7 @@
             return carry
 
         lax.fori_loop(0, NEWTON, newton, 0)
-        land[me] = f_ref[me]
+        land[me] = f_ref[pair_here]
         for s in range(n):
 
             @pl.when(me != s)
@@ -588,14 +607,14 @@
             mixed = mixed + part[:DH] * factor
         mixed = mixed / total
         mx_ref[...] = mixed
-        b_ref[me, 0:DH, :] = mm_t(mixed, zs_ref[NEWTON], TOP)
+        b_ref[pair_here, 0:DH, :] = mm_t(mixed, zs_ref[NEWTON], TOP)
         pad = jnp.zeros((MSG - DH - 2, LANES), f32)
-        b_ref[me, DH:MSG, :] = jnp.concatenate([top, total, pad], axis=0)
+        b_ref[pair_here, DH:MSG, :] = jnp.concatenate([top, total, pad], axis=0)
         for t in range(n):
 
             @pl.when(me != t)
             def _(t=t):
-                to_seq(b_ref.at[me], b_ref.at[me], s2.at[t], r2.at[me], t).start()
+                to_seq(b_ref.at[pair_here], b_ref.at[pair_here], s2.at[t], r2.at[pair_here], t).start()
 
     def soft(g, carry):
         cols = quad(g)
@@ -612,9 +631,9 @@
     leave(near, near_out)
     for pair in range(PAIRS):
 
-        @pl.when(me != pair)
+        @pl.when(me != owner_of(pair, n))
         def _(pair=pair):
-            to_seq(b_ref.at[pair], b_ref.at[pair], s2.at[pair], r2.at[pair], pair).wait_recv()
+            to_seq(b_ref.at[pair], b_ref.at[pair], s2.at[pair], r2.at[pair], owner_of(pair, n)).wait_recv()
 
     def blend(g, carry):
         cols = quad(g)
@@ -631,21 +650,22 @@
     u1[...] = unit
     leave(u1, u1_out)
     inv1_ref[...] = scale
-    for d in range(1, n):
-        to_seq(mine, lands.at[me], ls.at[d], lr.at[me], lax.rem(me + d, n)).wait_send()
+    for kind in range(2):
+        for d in range(1, n):
+            land_copy(kind, me, d, lax.rem(me + d, n)).wait_send()
     for pair in range(PAIRS):
 
-        @pl.when(me != pair)
+        @pl.when(me != owner_of(pair, n))
         def _(pair=pair):
-            to_seq(f_ref.at[pair], land.at[me], s1.at[pair], r1.at[me], pair).wait_send()
-
-    @pl.when(me < PAIRS)
+            to_seq(f_ref.at[pair], land.at[me], s1.at[pair], r1.at[me], owner_of(pair, n)).wait_send()
+
+    @pl.when(owns)
     def _():
         for t in range(n):
 
             @pl.when(me != t)
             def _(t=t):
-                to_seq(b_ref.at[me], b_ref.at[me], s2.at[t], r2.at[me], t).wait_send()
+                to_seq(b_ref.at[pair_here], b_ref.at[pair_here], s2.at[t], r2.at[pair_here], t).wait_send()
 
     for copy in leaving:
         copy.wait()
@@ -673,7 +693,7 @@
             vm(4, width, width), vm(8, width), vm(8, slots, width), vm(slots + 40, width),
             vm(PAIRS, MSG, LANES), vm(2, segs, width), vm(n, 2, segs, width), vm(2 * RIM, width), vm(RIM, width),
             vm(RIM, width), vm(n, MSG, LANES),
-            dma((4,)), dma((9,)), dma((2,)), dma((2,)), dma((n,)), dma((n,)), dma((PAIRS,)), dma((n,)),
+            dma((4,)), dma((9,)), dma((2,)), dma((2,)), dma((2, n)), dma((2, n)), dma((PAIRS,)), dma((n,)),
             dma((n,)), dma((n,)),
         ],
         compiler_params=params(collective_id=1, has_side_effects=True),
@@ -1336,7 +1356,7 @@
     for copy in (load_gs2, load_w[0], load_pre[0], load_h1, load_w[1], load_pre[1], load_w[2], load_w[3], load_u1, load_ext):
         copy.start()
     me = greet_block()
-    owner = me < PAIRS
+    owner, pair_here = pair_at(me, n)
     stages, partners, remote = reduce_stages(gw, o_ref, (acc, lc, l1, mid, lz, l3, ag), sems)
     ends = seg_ends(lens_ref, segs)
     count = ends[-1]
@@ -1386,26 +1406,26 @@
         near_back_quad(g, gctx, near, q, kl_ref, b_ref, near, gb, gkl)
 
     def blend_copy(pair):
-        return to_seq(gb.at[pair], land.at[me], b1s.at[pair], b1r.at[me], pair)
+        return to_seq(gb.at[pair], land.at[me], b1s.at[pair], b1r.at[me], owner_of(pair, n))
 
     up, down = rim_copies(n, me, rim, gleft, gright, ms, mr)
 
     def ev_blend():
         for pair in range(PAIRS):
 
-            @pl.when(me != pair)
+            @pl.when(me != owner_of(pair, n))
             def _(pair=pair):
                 blend_copy(pair).start()
 
         rim_start(n, me, up, down, gleft, gright)
 
     def mixed_copy(target):
-        return to_seq(cmsg.at[me], cmsg.at[me], b2s.at[target], b2r.at[me], target)
+        return to_seq(cmsg.at[pair_here], cmsg.at[pair_here], b2s.at[target], b2r.at[pair_here], target)
 
     def ev_owner():
         @pl.when(owner)
         def _():
-            land[me] = gb[me]
+            land[me] = gb[pair_here]
             for s in range(n):
 
                 @pl.when(me != s)
@@ -1417,9 +1437,9 @@
                 gblend = gblend + land[s]
             mixed = mx_ref[...]
             gmixed = mm(gblend, zs_ref[NEWTON], TOP)
-            cmsg[me, 0:DH, :] = gmixed
+            cmsg[pair_here, 0:DH, :] = gmixed
             dots = jnp.sum(gmixed * mixed, axis=0, keepdims=True)
-            cmsg[me, DH:MSG, :] = jnp.concatenate([dots, jnp.zeros((MSG - DH - 1, LANES), f32)], axis=0)
+            cmsg[pair_here, DH:MSG, :] = jnp.concatenate([dots, jnp.zeros((MSG - DH - 1, LANES), f32)], axis=0)
             for t in range(n):
 
                 @pl.when(me != t)
@@ -1444,7 +1464,7 @@
     def ev_core():
         @pl.when(owner)
         def _():
-            core_back(ng[...], ncore[...], core_ref[...], zs_ref[0], ql_ref, kl_ref, gl, me)
+            core_back(ng[...], ncore[...], core_ref[...], zs_ref[0], ql_ref, kl_ref, gl, pair_here)
 
     quarter = slots // 4
 
@@ -1471,9 +1491,9 @@
     def ev_mixed():
         for pair in range(PAIRS):
 
-            @pl.when(me != pair)
+            @pl.when(me != owner_of(pair, n))
             def _(pair=pair):
-                to_seq(cmsg.at[pair], cmsg.at[pair], b2s.at[pair], b2r.at[pair], pair).wait_recv()
+                to_seq(cmsg.at[pair], cmsg.at[pair], b2s.at[pair], b2r.at[pair], owner_of(pair, n)).wait_recv()
 
         for copy in (load_k, load_v, load_p):
             copy.wait()
@@ -1612,7 +1632,7 @@
     pltpu.make_async_copy(ig, ig_hbm, ig_sem.at[0]).wait()
     for pair in range(PAIRS):
 
-        @pl.when(me != pair)
+        @pl.when(me != owner_of(pair, n))
         def _(pair=pair):
             blend_copy(pair).wait_send()
 

time: 337 us -> 335 us (level)
  no operation moved by 1% of the time
where the time goes in v6:
time: 335 us
  Pallas kernels  333 us (99%)
    pallas_call x1, Pallas kernels, tail(): pl.pallas_call(tail_kernel, in_specs=[smem()] + [anywhere] * len(big) + [...  239 us
    pallas_call x1, Pallas kernels, front(): pl.pallas_call(partial(front_kernel, n), in_specs=[smem()] + [whole()] *...  45.8 us
    pallas_call x1, Pallas kernels, ffn_forward(): pl.pallas_call(forward_kernel, grid=(inner // width,), in_specs=[smem(),...  26.8 us
    pallas_call x1, Pallas kernels, place_strips(): pl.pallas_call(place_strips_kernel, in_specs=[anywhere, whole()], out_spe...  21 us

profile of v6, /device:TPU:0, one launch (start us, length us, event | category | flops | bytes accessed | tf_op | source)
XLA Modules:
  0.0 334.6 jit_solution(3617854334620893603)
XLA Ops:
  0.7 45.8 %front.1 = (f32[512,768]{1,0:T(8,128)}, f32[512,768]{1,0:T(8,128)}, f32[512,768]{1,0:T(8,128)}, f32[512,768]{1,0:T(8,128)}, f32[512,768]{1,0:T(8,128)}, /*index=...) custom-call(s32[1,8]{1,0:T(1,128)} %lens_ref.5, ...), custom_call_target="tpu_custom_call" | custom-call | tf_op jit(solution)/shard_map/front/pallas_call | solution.py:682
  46.4 26.8 %ffn_forward.1 = (f32[512,3072]{1,0:T(8,128)}, f32[512,768]{1,0:T(8,128)}, f32[512,768]{1,0:T(8,128)}, f32[8,768]{1,0:T(8,128)}) custom-call(s32[1,8]{1,0:T(1,128)} %lens_ref.5, f32[512,768]{1,0:T(8,128)} %get-tuple-element.62.h1_ref.h1_hbm, f32[768,3072]{1,0:T(8,128)} %win_hbm.1, f32[1,3072]{1,0:T(1,128)} %bitcast.13, f32[3072,768]{1,0:T(8,128)} %wout_hbm.1, ...), custom_call_target="tpu_custom_call" | custom-call | tf_op jit(solution)/shard_map/ffn_forward/pallas_call | solution.py:756
  73.3 239.1 %tail.1 = (f32[2,36,16,48,128]{4,3,2,1,0:T(8,128)}, f32[112,128]{1,0:T(8,128)}, f32[512,768]{1,0:T(8,128)}) custom-call(s32[1,8]{1,0:T(1,128)} %lens_ref.5, f32[512,768]{1,0:T(8,128)} %get-tuple-element.64.gs2_hbm, f32[512,768]{1,0:T(8,128)} %get-tuple-element.62.h1_ref.h1_hbm, f32[512,768]{1,0:T(8,128)} %get-tuple-element.65.u1_hbm, ...), custom_call_target="tpu_custom_call" | custom-call | tf_op jit(solution)/shard_map/tail/pallas_call | solution.py:1662
  312.4 0.0 copy-start
  312.4 21.0 %place_strips.1 = (f32[3072,768]{1,0:T(8,128)}, f32[768,3072]{1,0:T(8,128)}, f32[768,768]{1,0:T(8,128)}, f32[768,768]{1,0:T(8,128)}, f32[768,768]{1,0:T(8,128)},...) custom-call(f32[2,36,768,128]{3,2,1,0:T(8,128)} %bitcast.8, ...), custom_call_target="tpu_custom_call" | custom-call | tf_op jit(solution)/shard_map/place_strips/pallas_call | solution.py:1737
  333.5 0.0 copy-done
  333.5 1.1 copy.38
Async XLA Ops:
  312.4 21.1 %copy-start = (f32[512,768]{1,0:T(8,128)S(1)}, f32[512,768]{1,0:T(8,128)}, u32[]{:S(2)}) copy-start(f32[512,768]{1,0:T(8,128)} %get-tuple-element.87) | copy-start | bytes 4718596

commit v7 on v6

--- a/solution.py
+++ b/solution.py
@@ -712,21 +712,10 @@
     def _():
         acc_ref[...] = jnp.zeros_like(acc_ref)
 
-    def one(g, carry):
-        cols = quad(g)
-        pre = mm(h1_ref[...], wi_ref[:, cols]) + bi_ref[:, cols]
-        pre_ref[:, cols] = pre
-        act_ref[:, cols] = 0.5 * pre * (1.0 + lax.erf(pre * ROOT_HALF))
-        return carry
-
-    lax.fori_loop(0, QUADS, one, 0)
-
-    def two(g, carry):
-        cols = quad(g)
-        acc_ref[:, cols] += mm(act_ref[...], wo_ref[:, cols])
-        return carry
-
-    lax.fori_loop(0, QUADS, two, 0)
+    pre = mm(h1_ref[...], wi_ref[...]) + bi_ref[...]
+    pre_ref[...] = pre
+    act_ref[...] = 0.5 * pre * (1.0 + lax.erf(pre * ROOT_HALF))
+    acc_ref[...] += mm(act_ref[...], wo_ref[...])
 
     @pl.when(step == pl.num_programs(0) - 1)
     def _():

time: 335 us -> 333 us (level)
  no operation moved by 1% of the time
where the time goes in v7:
time: 333 us
  Pallas kernels  331 us (99%)
    pallas_call x1, Pallas kernels, tail(): pl.pallas_call(tail_kernel, in_specs=[smem()] + [anywhere] * len(big) + [...  239 us
    pallas_call x1, Pallas kernels, front(): pl.pallas_call(partial(front_kernel, n), in_specs=[smem()] + [whole()] *...  45.8 us
    pallas_call x1, Pallas kernels, ffn_forward(): pl.pallas_call(forward_kernel, grid=(inner // width,), in_specs=[smem(),...  24.7 us
    pallas_call x1, Pallas kernels, place_strips(): pl.pallas_call(place_strips_kernel, in_specs=[anywhere, whole()], out_spe...  21 us

profile of v7, /device:TPU:0, one launch (start us, length us, event | category | flops | bytes accessed | tf_op | source)
XLA Modules:
  0.0 332.5 jit_solution(14155615782626154136)
XLA Ops:
  0.7 45.8 %front.1 = (f32[512,768]{1,0:T(8,128)}, f32[512,768]{1,0:T(8,128)}, f32[512,768]{1,0:T(8,128)}, f32[512,768]{1,0:T(8,128)}, f32[512,768]{1,0:T(8,128)}, /*index=...) custom-call(s32[1,8]{1,0:T(1,128)} %lens_ref.5, ...), custom_call_target="tpu_custom_call" | custom-call | tf_op jit(solution)/shard_map/front/pallas_call | solution.py:682
  46.4 24.7 %ffn_forward.1 = (f32[512,3072]{1,0:T(8,128)}, f32[512,768]{1,0:T(8,128)}, f32[512,768]{1,0:T(8,128)}, f32[8,768]{1,0:T(8,128)}) custom-call(s32[1,8]{1,0:T(1,128)} %lens_ref.5, f32[512,768]{1,0:T(8,128)} %get-tuple-element.62.h1_ref.h1_hbm, f32[768,3072]{1,0:T(8,128)} %win_hbm.1, f32[1,3072]{1,0:T(1,128)} %bitcast.13, f32[3072,768]{1,0:T(8,128)} %wout_hbm.1, ...), custom_call_target="tpu_custom_call" | custom-call | tf_op jit(solution)/shard_map/ffn_forward/pallas_call | solution.py:745
  71.2 239.2 %tail.1 = (f32[2,36,16,48,128]{4,3,2,1,0:T(8,128)}, f32[112,128]{1,0:T(8,128)}, f32[512,768]{1,0:T(8,128)}) custom-call(s32[1,8]{1,0:T(1,128)} %lens_ref.5, f32[512,768]{1,0:T(8,128)} %get-tuple-element.64.gs2_hbm, f32[512,768]{1,0:T(8,128)} %get-tuple-element.62.h1_ref.h1_hbm, f32[512,768]{1,0:T(8,128)} %get-tuple-element.65.u1_hbm, ...), custom_call_target="tpu_custom_call" | custom-call | tf_op jit(solution)/shard_map/tail/pallas_call | solution.py:1651
  310.3 0.0 copy-start
  310.3 21.0 %place_strips.1 = (f32[3072,768]{1,0:T(8,128)}, f32[768,3072]{1,0:T(8,128)}, f32[768,768]{1,0:T(8,128)}, f32[768,768]{1,0:T(8,128)}, f32[768,768]{1,0:T(8,128)},...) custom-call(f32[2,36,768,128]{3,2,1,0:T(8,128)} %bitcast.8, ...), custom_call_target="tpu_custom_call" | custom-call | tf_op jit(solution)/shard_map/place_strips/pallas_call | solution.py:1726
  331.4 0.0 copy-done
  331.4 1.1 copy.38
Async XLA Ops:
  310.3 21.1 %copy-start = (f32[512,768]{1,0:T(8,128)S(1)}, f32[512,768]{1,0:T(8,128)}, u32[]{:S(2)}) copy-start(f32[512,768]{1,0:T(8,128)} %get-tuple-element.87) | copy-start | bytes 4718596
